TPU v7x, 32 devices: a whole 2x2x4 slice. The times are simulated.
32 devices in a mesh: span: 8 (over z, x), wall: 4 (over y, core).
Axes of the slice: x: 2, y: 2, z: 4, core: 2. Of those that a mesh axis runs over, the one named last changes fastest.
Arguments:
- forcing: float32 [768, 16384], P('wall', 'span'), may hold values from -6 to 6
- start: float32 [768, 16384], P('wall', 'span'), may hold values from -2 to 2
- wall_even: float32 [384, 384], replicated, may hold values from -0.3125 to 0.3125
- wall_odd: float32 [384, 384], replicated, may hold values from -0.3125 to 0.3125
- diag_shift: float32 [768, 512], P('wall', 'span'), may hold values from 0.5 to 2
- band_coef: float32 [8, 768, 512], P(None, 'wall', 'span'), may hold values from -2 to 2
- offsets: int32 [8], replicated, may hold values from -128 to 128, as said below
- pattern: int32 [8, 512], P(None, 'span'), may hold values 0 or 1
- block_inv: float32 [768, 192], P('wall'), may hold values from -0.109375 to 0.109375
Outputs:
- solution: float32 [768, 16384], P('wall', 'span')
- residual: float32 [768, 16384], P('wall', 'span')
Inputs may be any that keep to these rules, and one draw needn't show every extreme that they name: `offsets`: every offset lies within 128 spanwise points; in every draw one band has offset 2 * 64 and one has offset -128.
All inputs are finite; a program needn't handle non-finite values. No bound on the sum of `pattern` on one device may be relied on, other than what follows from the above.
Results may differ from a plain program's by a relative error of at most 0.0001.
Values sent between devices are 32-bit elements; how exact they have to be, the bound alone decides.
No kernel may reach another device: no remote copies, remote signals or barrier semaphores. Data moves between devices by JAX's collectives and lax.ppermute only.
A program may use at most 128 MiB of HBM per device.

v0:
```python
import functools

import jax
import jax.numpy as jnp
from jax import lax
from jax.experimental import pallas as pl
from jax.experimental.pallas import tpu as pltpu
from jax.sharding import PartitionSpec as P


SWEEPS = 2
CHUNKS = 2
LANES = 128
HALF = LANES // 2
REACH = 2


def exchange(value, bit):
    count = lax.axis_size("wall")
    return lax.ppermute(value, "wall", [(i, i ^ bit) for i in range(count)])


def partner(value):
    count = lax.axis_size("span")
    return lax.ppermute(value, "span", [(i, i ^ 1) for i in range(count)])


def far(value, first):
    count = lax.axis_size("span")
    pairs = []
    for i in range(count):
        up = (i % 2 == 1) == first
        pairs.append((i, (i + (REACH if up else -REACH)) % count))
    return lax.ppermute(value, "span", pairs)


def params():
    return pltpu.CompilerParams(vmem_limit_bytes=20 << 20)


SMEM = pl.BlockSpec(memory_space=pltpu.SMEM)
VMEM = pl.BlockSpec(memory_space=pltpu.VMEM)


def split_kernel(width, x_ref, *out_refs):
    chunks = len(out_refs)
    cw = width // chunks
    half = cw // 2
    per = LANES // width

    def step(g, _):
        lanes = pl.ds(pl.multiple_of(g * LANES, LANES), LANES)
        top = x_ref[:LANES, lanes].T.reshape(per, width, LANES)
        low = x_ref[LANES:, lanes]
        pair = jnp.concatenate([low, pltpu.roll(low, LANES - half, 1)], 0)
        pair = pair.T.reshape(per, width, LANES)
        here = pl.ds(g * per, per)
        for k, out_ref in enumerate(out_refs):
            out_ref[here, :cw, :] = top[:, k * cw : (k + 1) * cw, :]
            out_ref[here, cw:, :] = pair[:, k * cw : k * cw + half, :]
        return 0

    lax.fori_loop(0, x_ref.shape[1] // LANES, step, 0)


def split(x, chunks, points):
    rows, breadth = x.shape
    width = breadth // points
    cw = width // chunks
    out = jax.ShapeDtypeStruct((points, cw + cw // 2, LANES), x.dtype)
    return pl.pallas_call(
        functools.partial(split_kernel, width),
        out_shape=(out,) * chunks,
        in_specs=[VMEM],
        out_specs=(VMEM,) * chunks,
        compiler_params=params(),
        cost_estimate=pl.CostEstimate(flops=0, bytes_accessed=8 * rows * breadth, transcendentals=0),
        name="split",
    )(x)


def join(width, sol_parts, res_parts, sol_ref, res_ref, begin, end):
    chunks = len(sol_parts)
    cw = width // chunks
    half = cw // 2
    per = LANES // width
    lower = lax.broadcasted_iota(jnp.int32, (half, LANES), 1) < HALF

    def step(g, _):
        lanes = pl.ds(pl.multiple_of(g * LANES, LANES), LANES)
        for out_ref, parts in ((sol_ref, sol_parts), (res_ref, res_parts)):
            rows = [part[g * per + z, :cw, :] for z in range(per) for part in parts]
            out_ref[:LANES, lanes] = jnp.concatenate(rows, 0).T
        rows = []
        for z in range(per):
            for sol, res in zip(sol_parts, res_parts):
                a = sol[g * per + z, cw:, :]
                b = res[g * per + z, cw:, :]
                rows.append(jnp.where(lower, a, pltpu.roll(b, HALF, 1)))
                rows.append(jnp.where(lower, pltpu.roll(a, HALF, 1), b))
        both = jnp.concatenate(rows, 0).T
        sol_ref[LANES:, lanes] = both[:HALF]
        res_ref[LANES:, lanes] = both[HALF:]
        return 0

    lax.fori_loop(begin, end, step, 0, unroll=2)


UNROLL = 4


def fill(ext_ref, pieces, points):
    def step(i, _):
        for slot in range(ext_ref.shape[0] // points):
            here = pl.ds(slot * points + i * UNROLL, UNROLL)
            ext_ref[here] = jnp.zeros((UNROLL, *ext_ref.shape[1:]), jnp.float32)
        return 0

    lax.fori_loop(0, points // UNROLL, step, 0)

    def copy(i, _):
        for ref, slot in pieces:
            ext_ref[pl.ds(slot * points + i * UNROLL, UNROLL)] = ref[pl.ds(i * UNROLL, UNROLL)]
        return 0

    lax.fori_loop(0, points // UNROLL, copy, 0)


def scaled(w_ref, row, value, cw):
    top = w_ref[0, pl.ds(row, 1), :] * value[:cw]
    low = w_ref[1, pl.ds(row, 1), :] * value[cw:]
    return top, low


def near_kernel(bands, off_ref, sign_ref, x_ref, far_ref, w_ref, theirs_ref, partial_ref, sum_ref, ext_ref):
    points, rows, _ = x_ref.shape
    cw = rows * 2 // 3
    sign = sign_ref[0]
    own = jnp.where(sign > 0, REACH, REACH + 1)
    fill(ext_ref, [(x_ref, own), (far_ref, own + 2 * sign)], points)

    for out_ref, weights, shift in ((partial_ref, theirs_ref, sign), (sum_ref, w_ref, 0)):
        starts = [(own + shift) * points + off_ref[b] for b in range(bands)]

        def step(i, _):
            for u in range(UNROLL):
                p = i * UNROLL + u
                if out_ref is sum_ref:
                    top, low = scaled(weights, bands * points + p, x_ref[p], cw)
                else:
                    top, low = None, None
                for b in range(bands):
                    t, l = scaled(weights, b * points + p, ext_ref[starts[b] + p], cw)
                    top, low = (t, l) if top is None else (top + t, low + l)
                out_ref[p, :cw, :] = top
                out_ref[p, cw:, :] = low
            return 0

        lax.fori_loop(0, points // UNROLL, step, 0)


def near(offsets, sign, x, first, w, theirs):
    bands = offsets.shape[0]
    points, rows, _ = x.shape
    out = jax.ShapeDtypeStruct(x.shape, x.dtype)
    return pl.pallas_call(
        functools.partial(near_kernel, bands),
        out_shape=(out, out),
        in_specs=[SMEM, SMEM, VMEM, VMEM, VMEM, VMEM],
        out_specs=(VMEM, VMEM),
        scratch_shapes=[pltpu.VMEM(((2 * REACH + 2) * points, rows, LANES), jnp.float32)],
        compiler_params=params(),
        cost_estimate=pl.CostEstimate(flops=1000000000, bytes_accessed=6 * x.size * 4, transcendentals=0),
        name="near",
    )(offsets, sign, x, first, w, theirs)


def halves(value):
    high = value.astype(jnp.bfloat16)
    low = (value - high.astype(jnp.float32)).astype(jnp.bfloat16)
    return high, low


def product(high, low, w_high, w_low):
    dot = functools.partial(jnp.dot, preferred_element_type=jnp.float32)
    return dot(high, w_high) + (dot(low, w_high) + dot(high, w_low))


def stage(high_ref, low_ref, at, ref, cw):
    points = ref.shape[0]
    half = cw // 2
    count = points * half
    low = ref[:, cw:, :].reshape(count, LANES)
    turned = pltpu.roll(low, HALF, 1)
    for part, top, rest in ((0, ref[:, :half, :], low), (1, ref[:, half:cw, :], turned)):
        rows = slice(part * count, (part + 1) * count)
        for n, value in enumerate((top.reshape(count, LANES), rest)):
            columns = slice(at + n * LANES, at + (n + 1) * LANES)
            high, small = halves(value)
            high_ref[rows, columns] = high
            low_ref[rows, columns] = small


def unstage(value, points, cw):
    half = cw // 2
    count = points * half
    first, second = value[:count], value[count:]
    top = [v[:, :LANES].reshape(points, half, LANES) for v in (first, second)]
    low = first[:, LANES:] + pltpu.roll(second[:, LANES:], HALF, 1)
    return top, low.reshape(points, half, LANES)


def wall_kernel(n_blocks, f_ref, s_ref, mh_ref, ml_ref, *rest):
    blocks = rest[:n_blocks]
    out_ref, high_ref, low_ref = rest[n_blocks:]
    points, rows, _ = f_ref.shape
    cw = rows * 2 // 3
    half = cw // 2
    for k, ref in enumerate(blocks):
        stage(high_ref, low_ref, 2 * LANES * k, ref, cw)
    result = product(high_ref[...], low_ref[...], mh_ref[...], ml_ref[...])
    top, low = unstage(result, points, cw)
    out_ref[:, :half, :] = f_ref[:, :half, :] - s_ref[:, :half, :] - top[0]
    out_ref[:, half:cw, :] = f_ref[:, half:cw, :] - s_ref[:, half:cw, :] - top[1]
    out_ref[:, cw:, :] = f_ref[:, cw:, :] - s_ref[:, cw:, :] - low


def wall(f, s, mh, ml, blocks):
    points, rows, _ = f.shape
    n_blocks = len(blocks)
    m_rows = points * rows * 2 // 3
    return pl.pallas_call(
        functools.partial(wall_kernel, n_blocks),
        out_shape=jax.ShapeDtypeStruct(f.shape, f.dtype),
        in_specs=[VMEM] * (4 + n_blocks),
        out_specs=VMEM,
        scratch_shapes=[pltpu.VMEM((m_rows, 2 * LANES * n_blocks), jnp.bfloat16)] * 2,
        compiler_params=params(),
        cost_estimate=pl.CostEstimate(flops=3000000000, bytes_accessed=8 * f.size * 4, transcendentals=0),
        name="wall",
    )(f, s, mh, ml, *blocks)


def far_terms(bands, lo, n, sign, off_ref, w_ref, far_ref, r_ref):
    points, rows, _ = far_ref.shape
    cw = rows * 2 // 3

    def band(b, _):
        shift = off_ref[b] + 2 * sign * points
        first = jnp.maximum(lo, -shift)
        count = jnp.minimum(lo + n, points - shift) - first

        def point(p):
            top, low = scaled(w_ref, b * points + p, far_ref[p + shift], cw)
            r_ref[p - lo, :cw, :] = r_ref[p - lo, :cw, :] - top
            r_ref[p - lo, cw:, :] = r_ref[p - lo, cw:, :] - low

        def several(i, _):
            for u in range(UNROLL):
                point(first + i * UNROLL + u)
            return 0

        def one(i, _):
            point(first + i)
            return 0

        groups = jnp.maximum(count, 0) // UNROLL
        lax.fori_loop(0, groups, several, 0)
        lax.fori_loop(groups * UNROLL, count, one, 0)
        return 0

    lax.fori_loop(0, bands, band, 0)


def update(x_ref, lo, r_ref, high_ref, low_ref, bh_ref, bl_ref, x_new_ref):
    n, rows, _ = r_ref.shape
    cw = rows * 2 // 3
    half = cw // 2
    stage(high_ref, low_ref, 0, r_ref, cw)
    result = product(high_ref[...], low_ref[...], bh_ref[...], bl_ref[...])
    top, low = unstage(result, n, cw)
    here = pl.ds(lo, n)
    x_new_ref[:, :half, :] = x_ref[here, :half, :] + top[0]
    x_new_ref[:, half:cw, :] = x_ref[here, half:cw, :] + top[1]
    x_new_ref[:, cw:, :] = x_ref[here, cw:, :] + low


def last_kernel(bands, off_ref, sign_ref, g_ref, t_ref, x_ref, w_ref, bh_ref, bl_ref, far_ref, x_new_ref, r_ref, high_ref, low_ref):
    points = x_ref.shape[0]

    def begin(i, _):
        here = pl.ds(i * UNROLL, UNROLL)
        r_ref[here] = g_ref[here] - t_ref[here]
        return 0

    lax.fori_loop(0, points // UNROLL, begin, 0)
    far_terms(bands, 0, points, sign_ref[0], off_ref, w_ref, far_ref, r_ref)
    update(x_ref, 0, r_ref, high_ref, low_ref, bh_ref, bl_ref, x_new_ref)


def last(offsets, sign, g, t, x, w, bh, bl, second):
    bands = offsets.shape[0]
    points, rows, _ = x.shape
    out = jax.ShapeDtypeStruct(x.shape, x.dtype)
    m_rows = points * rows * 2 // 3
    return pl.pallas_call(
        functools.partial(last_kernel, bands),
        out_shape=(out, out),
        in_specs=[SMEM, SMEM] + [VMEM] * 7,
        out_specs=(VMEM, VMEM),
        scratch_shapes=[pltpu.VMEM((m_rows, 2 * LANES), jnp.bfloat16)] * 2,
        compiler_params=params(),
        cost_estimate=pl.CostEstimate(flops=1000000000, bytes_accessed=8 * x.size * 4, transcendentals=0),
        name="last",
    )(offsets, sign, g, t, x, w, bh, bl, second)


def piece_start(sizes, i, points):
    before = sum(sizes[:i])
    even = lax.rem(lax.axis_index("span"), 2) == 0
    return jnp.where(even, points - before - sizes[i], before)


def finish_kernel(bands, width, sizes, i, off_ref, g_ref, t_ref, x_ref, w_ref, bh_ref, bl_ref, *rest):
    fars = rest[: i + 1]
    n_outs = 2 if i else 0
    *earlier, sol_hbm, res_hbm, far_ref, high_ref, low_ref, x_new_ref, r_ref, sol_ref, res_ref, sems = rest[i + 1 :]
    if i:
        earlier = earlier[:-n_outs]
    points = x_ref.shape[0]
    n = sizes[i]
    sign = 1 - 2 * lax.rem(lax.axis_index("span"), 2)
    lo = piece_start(sizes, i, points)
    for m, ref in enumerate(fars):
        at = piece_start(sizes, m, points)

        def copy(j, _):
            far_ref[pl.ds(at + j * UNROLL, UNROLL)] = ref[pl.ds(j * UNROLL, UNROLL)]
            return 0

        lax.fori_loop(0, sizes[m] // UNROLL, copy, 0)

    def begin(j, _):
        here = pl.ds(lo + j * UNROLL, UNROLL)
        r_ref[pl.ds(j * UNROLL, UNROLL)] = g_ref[here] - t_ref[here]
        return 0

    lax.fori_loop(0, n // UNROLL, begin, 0)
    far_terms(bands, lo, n, sign, off_ref, w_ref, far_ref, r_ref)
    update(x_ref, lo, r_ref, high_ref, low_ref, bh_ref, bl_ref, x_new_ref)
    views = [ref.at[pl.ds(lo, n)] for ref in earlier]
    slabs = sems.shape[1]
    wide = n * width // slabs
    copies = []
    for m in range(slabs):
        join(width, [*views[::2], x_new_ref], [*views[1::2], r_ref], sol_ref, res_ref, m * wide // LANES, (m + 1) * wide // LANES)
        here = pl.ds(m * wide, wide)
        there = pl.ds(pl.multiple_of(lo * width + m * wide, LANES), wide)
        for which, (ref, hbm) in enumerate(((sol_ref, sol_hbm), (res_ref, res_hbm))):
            copy = pltpu.make_async_copy(ref.at[:, here], hbm.at[:, there], sems.at[which, m])
            copy.start()
            copies.append(copy)
    for copy in copies:
        copy.wait()


SLABS = 2


def finish(offsets, g, t, x, w, bh, bl, fars, earlier, outs, sizes, i, width):
    bands = offsets.shape[0]
    points, rows, _ = x.shape
    n = sizes[i]
    piece = pltpu.VMEM((n, rows, LANES), jnp.float32)
    out = jax.ShapeDtypeStruct((LANES + HALF, points * width), x.dtype)
    m_rows = n * rows * 2 // 3
    slab = pltpu.VMEM((LANES + HALF, n * width), jnp.float32)
    hbm = pl.BlockSpec(memory_space=pltpu.HBM)
    inputs = (offsets, g, t, x, w, bh, bl, *fars, *earlier)
    return pl.pallas_call(
        functools.partial(finish_kernel, bands, width, sizes, i),
        out_shape=(out, out),
        in_specs=[SMEM] + [VMEM] * (len(inputs) - 1) + [hbm] * len(outs),
        out_specs=(hbm, hbm),
        input_output_aliases={len(inputs) + k: k for k in range(len(outs))},
        scratch_shapes=[
            pltpu.VMEM(x.shape, jnp.float32),
            pltpu.VMEM((m_rows, 2 * LANES), jnp.bfloat16),
            pltpu.VMEM((m_rows, 2 * LANES), jnp.bfloat16),
            piece,
            piece,
            slab,
            slab,
            pltpu.SemaphoreType.DMA((2, SLABS)),
        ],
        compiler_params=params(),
        cost_estimate=pl.CostEstimate(flops=1000000000, bytes_accessed=8 * x.size * 4, transcendentals=0),
        name="finish",
    )(*inputs, *outs)


def flip_matrix(rows, turned):
    size = 2 * LANES
    i = lax.broadcasted_iota(jnp.int32, (size, size), 0)
    j = lax.broadcasted_iota(jnp.int32, (size, size), 1)
    target = jnp.where(turned, rows - 1 - i, i)
    return jnp.where(jnp.logical_and(j == target, i < rows), 1.0, 0.0).astype(jnp.bfloat16)


def prep_kernel(count, index_ref, even_ref, odd_ref, inv_ref, mh_ref, ml_ref, bh_ref, bl_ref, pad_ref):
    rows = inv_ref.shape[0]
    size = 2 * LANES
    index = index_ref[0]
    half = count // 2
    lower = index >= half
    at = pl.ds(pl.multiple_of(jnp.where(lower, count - 1 - index, index) * rows, 8), rows)
    pad_ref[...] = jnp.zeros_like(pad_ref)

    def transposed(value):
        pad_ref[:rows, :rows] = value
        return pad_ref[...].T

    high, low = halves(transposed(inv_ref[...]))
    bh_ref[...] = high
    bl_ref[...] = low
    keep_or_turn = flip_matrix(rows, lower)
    turn = flip_matrix(rows, True)
    dot = functools.partial(jnp.dot, preferred_element_type=jnp.float32)
    even = even_ref[at, :]
    odd = odd_ref[at, :]
    for j in range(count):
        block = j if j < half else count - 1 - j
        columns = slice(block * rows, (block + 1) * rows)
        weight = jnp.where(lower == (j >= half), 0.5, -0.5)
        parts = halves(transposed(0.5 * even[:, columns] + weight * odd[:, columns]))
        place = pl.ds(pl.multiple_of(jnp.bitwise_xor(index, j) * size, size), size)
        for out_ref, part in zip((mh_ref, ml_ref), parts):
            if j >= half:
                part = dot(turn, part).astype(jnp.bfloat16)
            out_ref[place, :] = dot(part, keep_or_turn).astype(jnp.bfloat16)


def prep(wall_even, wall_odd, block_inv):
    count = lax.axis_size("wall")
    index = lax.axis_index("wall").astype(jnp.int32)[None]
    size = 2 * LANES
    m = jax.ShapeDtypeStruct((count * size, size), jnp.bfloat16)
    b = jax.ShapeDtypeStruct((size, size), jnp.bfloat16)
    return pl.pallas_call(
        functools.partial(prep_kernel, count),
        out_shape=(m, m, b, b),
        in_specs=[SMEM, VMEM, VMEM, VMEM],
        out_specs=(VMEM,) * 4,
        scratch_shapes=[pltpu.VMEM((size, size), jnp.float32)],
        compiler_params=params(),
        cost_estimate=pl.CostEstimate(flops=600000000, bytes_accessed=3000000, transcendentals=0),
        name="prep",
    )(index, wall_even, wall_odd, block_inv)


def after(value, *others):
    return lax.optimization_barrier((value, *others))[0]


def sweeps(forcing, start, wall_even, wall_odd, diag_shift, band_coef, offsets, pattern, block_inv):
    rows, breadth = start.shape
    points = diag_shift.shape[1]
    bands = band_coef.shape[0]
    width = breadth // points
    chunks = CHUNKS
    n_wall = lax.axis_size("wall")
    sign = jnp.where(lax.axis_index("span") % 2 == 0, 1, -1).astype(jnp.int32)[None]

    raw_first = far(start, True)
    state = list(split(start, chunks, points))
    weights = jnp.swapaxes(band_coef, 1, 2) * pattern.astype(jnp.float32)[:, :, None]
    weights = jnp.concatenate([weights, diag_shift.T[None]], 0).reshape((bands + 1) * points, rows)
    low = weights[:, LANES:]
    own_w = jnp.stack([weights[:, :LANES], jnp.concatenate([low, low], 1)])
    their_w = partner(own_w[:, : bands * points])
    mh, ml, bh, bl = prep(wall_even, wall_odd, block_inv)
    f = split(forcing, chunks, points)
    sizes = (points - points // 4, points // 4)
    arrived = raw_first
    order = [0]
    bit = n_wall // 2
    while bit:
        order = order + [o ^ bit for o in order]
        bit //= 2
    for sweep in range(SWEEPS):
        final_sweep = sweep == SWEEPS - 1
        if sweep:
            firsts = [far(after(state[k], arrived), True) for k in range(chunks)]
            arrived = firsts[-1]
        else:
            firsts = split(raw_first, chunks, points)
        seconds = []
        for k in range(chunks):
            value = after(state[k], arrived)
            if final_sweep and k == chunks - 1:
                parts = [lax.dynamic_slice_in_dim(value, piece_start(sizes, i, points), n, 0) for i, n in enumerate(sizes)]
                seconds.append([far(v, False) for v in parts])
            else:
                seconds.append(far(value, False))
        arrived = seconds[-1]
        walls = []
        for k in range(chunks):
            got = [state[k]]
            bit = n_wall // 2
            while bit:
                got = got + [exchange(v, bit) for v in got]
                bit //= 2
            walls.append([got[order.index(o)] for o in range(n_wall)])
        theirs = []
        sums = []
        for k in range(chunks):
            partial, own_sum = near(offsets, sign, state[k], firsts[k], own_w, their_w)
            sums.append(own_sum)
            theirs.append(partner(partial))
        new = []
        for k in range(chunks):
            g = wall(f[k], sums[k], mh, ml, walls[k])
            if final_sweep and k == chunks - 1:
                earlier = [a for pair in new for a in pair]
                outs = ()
                for i in range(len(sizes)):
                    call = functools.partial(finish, sizes=sizes, i=i, width=width)
                    fars = seconds[k][: i + 1]
                    outs = call(offsets, g, theirs[k], state[k], own_w, bh, bl, fars, earlier, outs)
                return outs
            new.append(last(offsets, sign, g, theirs[k], state[k], own_w, bh, bl, seconds[k]))
        state = [pair[0] for pair in new]


def solution(mesh):
    in_specs = (
        P("wall", "span"),
        P("wall", "span"),
        P(),
        P(),
        P("wall", "span"),
        P(None, "wall", "span"),
        P(),
        P(None, "span"),
        P("wall", None),
    )
    out_specs = (P("wall", "span"), P("wall", "span"))
    return jax.shard_map(sweeps, mesh=mesh, in_specs=in_specs, out_specs=out_specs, check_vma=False)
```

profile of v0, /device:TPU:16, one launch (start us, length us, event | category | flops | bytes accessed | tf_op | source)
XLA Modules:
  0.0 184.4 jit_solution(347929137081793241)
XLA Ops:
  1.1 1.4 copy-done
  2.6 3.3 %split.4 = (f32[64,24,128]{2,1,0:T(8,128)S(1)}, f32[64,24,128]{2,1,0:T(8,128)}) custom-call(f32[192,2048]{1,0:T(8,128)S(1)} %copy-done), custom_call_target="tpu_custom_call" | custom-call | bytes 3145728 | tf_op jit(solution)/shard_map/split/pallas_call | solution.py:71
  5.8 1.5 collective-permute-start.3
  7.8 0.9 fusion
  8.7 2.6 %collective-permute-start.1 = (f32[2,512,128]{2,1,0:T(8,128)}, f32[2,512,128]{2,1,0:T(8,128)S(1)}, u32[]{:S(2)}, u32[]{:S(2)}) collective-permute-start(f32[2,512,128]{2,1,0:T(8,128)} %fusion), channel_id=1, source_target_pairs={{0,4},{4,0},{8,12},{12,8},{16,20},{20,16},{24,28},{28,24},{1,5},{5... | collective-permute-start | bytes 1572872 | tf_op jit(solution)/shard_map/ppermute | solution.py:25
  11.3 0.5 collective-permute-start.15
  11.8 1.1 pad_maximum_fusion.w_ref
  12.9 13.7 %collective-permute-done.3.rest_2_ = f32[64,24,128]{2,1,0:T(8,128)} collective-permute-done((f32[64,24,128]{2,1,0:T(8,128)}, f32[64,24,128]{2,1,0:T(8,128)}, u32[]{:S(2)}, u32[]{:S(2)}) %collective-permute-start.3) | collective-permute-done | bytes 786464 | tf_op jit(solution)/shard_map/ppermute | solution.py:20
  26.6 10.5 %collective-permute-done.x_ref = f32[192,2048]{1,0:T(8,128)S(1)} collective-permute-done((f32[192,2048]{1,0:T(8,128)}, f32[192,2048]{1,0:T(8,128)S(1)}, u32[]{:S(2)}, u32[]{:S(2)}) %collective-permute-start) | collective-permute-done | bytes 1572896 | tf_op jit(solution)/shard_map/ppermute | solution.py:34
  37.0 2.4 %split.5 = (f32[64,24,128]{2,1,0:T(8,128)S(1)}, f32[64,24,128]{2,1,0:T(8,128)S(1)}) custom-call(f32[192,2048]{1,0:T(8,128)S(1)} %collective-permute-done.x_ref), custom_call_target="tpu_custom_call" | custom-call | bytes 3145728 | tf_op jit(solution)/shard_map/split/pallas_call | solution.py:71
  39.4 3.4 %near.4 = (f32[64,24,128]{2,1,0:T(8,128)S(1)}, f32[64,24,128]{2,1,0:T(8,128)S(1)}) custom-call(s32[8]{0:T(128)S(1)} %copy-done.4, s32[1]{0:T(128)} %bitcast.sign_ref, f32[64,24,128]{2,1,0:T(8,128)} %get-tuple-element.41.x_ref.rest_0_, f32[64,24,128]{2,1,0:T(8,128)S(1)} %get-tuple-element.34.far_ref, f32[2,576,128]{2,1,0:T(8,128)S(1)} %pad_maximum_fusion.w_ref, ...), custom_call_target="tpu_custom_call" | custom-call | flops 1000000000 | bytes 4718592 | tf_op jit(solution)/shard_map/near/pallas_call | solution.py:166
  42.8 0.9 copy-done.20
  43.7 1.5 collective-permute-start.5
  45.2 1.9 %collective-permute-start.6 = (f32[64,24,128]{2,1,0:T(8,128)}, f32[64,24,128]{2,1,0:T(8,128)}, u32[]{:S(2)}, u32[]{:S(2)}) collective-permute-start(f32[64,24,128]{2,1,0:T(8,128)} %get-tuple-element.41.x_ref.rest_0_), channel_id=1, source_target_pairs={{0,8},{4,28},{8,16},{12,4},{16,24},{20,12},{24,0},{28,20},{1,9},{5... | collective-permute-start | bytes 2359304 | tf_op jit(solution)/shard_map/ppermute | solution.py:34
  47.1 0.5 collective-permute-start.16
  47.6 3.5 %near.6 = (f32[64,24,128]{2,1,0:T(8,128)}, f32[64,24,128]{2,1,0:T(8,128)S(1)}) custom-call(s32[8]{0:T(128)S(1)} %copy-done.4, s32[1]{0:T(128)} %bitcast.sign_ref, f32[64,24,128]{2,1,0:T(8,128)S(1)} %get-tuple-element.52.x_ref.rest_0_, f32[64,24,128]{2,1,0:T(8,128)S(1)} %get-tuple-element.49.far_ref, f32[2,576,128]{2,1,0:T(8,128)S(1)} %pad_maximum_fusion.w_ref, ...), custom_call_target="tpu_custom_call" | custom-call | flops 1000000000 | bytes 4718592 | tf_op jit(solution)/shard_map/near/pallas_call | solution.py:166
  51.1 0.9 copy-done.18
  52.1 0.9 copy-done.11
  52.9 11.2 %collective-permute-done.5.t_ref = f32[64,24,128]{2,1,0:T(8,128)S(1)} collective-permute-done((f32[64,24,128]{2,1,0:T(8,128)S(1)}, f32[64,24,128]{2,1,0:T(8,128)S(1)}, u32[]{:S(2)}, u32[]{:S(2)}) %collective-permute-start.5) | collective-permute-done | bytes 786464 | tf_op jit(solution)/shard_map/ppermute | solution.py:25
  64.1 0.9 copy-done.2
  65.0 3.4 %collective-permute-start.18 = (f32[64,24,128]{2,1,0:T(8,128)S(1)}, f32[64,24,128]{2,1,0:T(8,128)}, u32[]{:S(2)}, u32[]{:S(2)}) collective-permute-start(f32[64,24,128]{2,1,0:T(8,128)S(1)} %get-tuple-element.52.x_ref.rest_0_), channel_id=1, source_target_pairs={{0,8},{4,28},{8,16},{12,4},{16,24},{20,12},{24,0},{28,20},{1,9},{5... | collective-permute-start | bytes 2359304 | tf_op jit(solution)/shard_map/ppermute | solution.py:34
  68.4 2.4 %split.3 = (f32[64,24,128]{2,1,0:T(8,128)S(1)}, f32[64,24,128]{2,1,0:T(8,128)S(1)}) custom-call(f32[192,2048]{1,0:T(8,128)S(1)} %copy-done.1), custom_call_target="tpu_custom_call" | custom-call | bytes 3145728 | tf_op jit(solution)/shard_map/split/pallas_call | solution.py:71
  70.8 1.5 copy-done.14
  72.3 1.0 prep.1
  73.4 3.8 %wall.4.g_ref = f32[64,24,128]{2,1,0:T(8,128)S(1)} custom-call(f32[64,24,128]{2,1,0:T(8,128)S(1)} %get-tuple-element.32.f_ref, f32[64,24,128]{2,1,0:T(8,128)S(1)} %copy-done.21, bf16[1024,256]{1,0:T(8,128)(2,1)S(1)} %get-tuple-element.36.mh_ref, bf16[1024,256]{1,0:T(8,128)(2,1)S(1)} %get-tuple-element.37.ml_ref, ...), custom_call_target="tpu_custom_call" | custom-call | flops 3000000000 | bytes 6291456 | tf_op jit(solution)/shard_map/wall/pallas_call | solution.py:232
  77.3 2.9 %last.3 = (f32[64,24,128]{2,1,0:T(8,128)S(1)}, f32[64,24,128]{2,1,0:T(8,128)}) custom-call(s32[8]{0:T(128)S(1)} %copy-done.4, s32[1]{0:T(128)} %bitcast.sign_ref, f32[64,24,128]{2,1,0:T(8,128)S(1)} %wall.4.g_ref, f32[64,24,128]{2,1,0:T(8,128)S(1)} %copy-done.3, f32[64,24,128]{2,1,0:T(8,128)} %get-tuple-element.41.x_ref.rest_0_, ...), custom_call_target="tpu_custom_call" | custom-call | flops 1000000000 | bytes 6291456 | tf_op jit(solution)/shard_map/last/pallas_call | solution.py:306
  80.2 3.5 %wall.6.g_ref = f32[64,24,128]{2,1,0:T(8,128)S(1)} custom-call(f32[64,24,128]{2,1,0:T(8,128)S(1)} %get-tuple-element.47.f_ref, f32[64,24,128]{2,1,0:T(8,128)S(1)} %copy-done.19, bf16[1024,256]{1,0:T(8,128)(2,1)S(1)} %get-tuple-element.36.mh_ref, bf16[1024,256]{1,0:T(8,128)(2,1)S(1)} %get-tuple-element.37.ml_ref, ...), custom_call_target="tpu_custom_call" | custom-call | flops 3000000000 | bytes 6291456 | tf_op jit(solution)/shard_map/wall/pallas_call | solution.py:232
  83.8 23.1 %collective-permute-done.18.far_ref = f32[64,24,128]{2,1,0:T(8,128)} collective-permute-done((f32[64,24,128]{2,1,0:T(8,128)S(1)}, f32[64,24,128]{2,1,0:T(8,128)}, u32[]{:S(2)}, u32[]{:S(2)}) %collective-permute-start.18) | collective-permute-done | bytes 786464 | tf_op jit(solution)/shard_map/ppermute | solution.py:34
  106.9 3.5 %last.4 = (f32[64,24,128]{2,1,0:T(8,128)}, f32[64,24,128]{2,1,0:T(8,128)}) custom-call(s32[8]{0:T(128)S(1)} %copy-done.4, s32[1]{0:T(128)} %bitcast.sign_ref, f32[64,24,128]{2,1,0:T(8,128)S(1)} %wall.6.g_ref, f32[64,24,128]{2,1,0:T(8,128)} %collective-permute-done.17.t_ref, f32[64,24,128]{2,1,0:T(8,128)S(1)} %get-tuple-element.52.x_ref.rest_0_, ...), custom_call_target="tpu_custom_call" | custom-call | flops 1000000000 | bytes 6291456 | tf_op jit(solution)/shard_map/last/pallas_call | solution.py:306
  110.4 1.5 collective-permute-start.21
  111.9 0.5 collective-permute-start.9
  112.4 0.9 copy-done.9
  113.8 8.9 %collective-permute-done.21.rest_2_ = f32[64,24,128]{2,1,0:T(8,128)} collective-permute-done((f32[64,24,128]{2,1,0:T(8,128)}, f32[64,24,128]{2,1,0:T(8,128)}, u32[]{:S(2)}, u32[]{:S(2)}) %collective-permute-start.21) | collective-permute-done | bytes 786464 | tf_op jit(solution)/shard_map/ppermute | solution.py:20
  122.7 8.3 %collective-permute-done.9.rest_2_ = f32[64,24,128]{2,1,0:T(8,128)S(1)} collective-permute-done((f32[64,24,128]{2,1,0:T(8,128)S(1)}, f32[64,24,128]{2,1,0:T(8,128)S(1)}, u32[]{:S(2)}, u32[]{:S(2)}) %collective-permute-start.9) | collective-permute-done | bytes 786464 | tf_op jit(solution)/shard_map/ppermute | solution.py:20
  131.0 1.1 copy-done.10
  132.1 2.6 %near.5 = (f32[64,24,128]{2,1,0:T(8,128)S(1)}, f32[64,24,128]{2,1,0:T(8,128)S(1)}) custom-call(s32[8]{0:T(128)S(1)} %copy-done.4, s32[1]{0:T(128)} %bitcast.sign_ref, f32[64,24,128]{2,1,0:T(8,128)S(1)} %get-tuple-element.46.x_ref.rest_0_, f32[64,24,128]{2,1,0:T(8,128)S(1)} %copy-done.10, f32[2,576,128]{2,1,0:T(8,128)S(1)} %pad_maximum_fusion.w_ref, ...), custom_call_target="tpu_custom_call" | custom-call | flops 1000000000 | bytes 4718592 | tf_op jit(solution)/shard_map/near/pallas_call | solution.py:166
  134.8 2.6 %collective-permute-start.24 = (f32[64,24,128]{2,1,0:T(8,128)}, f32[64,24,128]{2,1,0:T(8,128)S(1)}, u32[]{:S(2)}, u32[]{:S(2)}) collective-permute-start(f32[64,24,128]{2,1,0:T(8,128)} %get-tuple-element.57.x_ref.rest_0_), channel_id=1, source_target_pairs={{0,8},{4,28},{8,16},{12,4},{16,24},{20,12},{24,0},{28,20},{1,9},{5... | collective-permute-start | bytes 2359304 | tf_op jit(solution)/shard_map/ppermute | solution.py:34
  137.4 3.5 %near.7 = (f32[64,24,128]{2,1,0:T(8,128)S(1)}, f32[64,24,128]{2,1,0:T(8,128)S(1)}) custom-call(s32[8]{0:T(128)S(1)} %copy-done.4, s32[1]{0:T(128)} %bitcast.sign_ref, f32[64,24,128]{2,1,0:T(8,128)} %get-tuple-element.57.x_ref.rest_0_, f32[64,24,128]{2,1,0:T(8,128)} %collective-permute-done.19.far_ref, f32[2,576,128]{2,1,0:T(8,128)S(1)} %pad_maximum_fusion.w_ref, ...), custom_call_target="tpu_custom_call" | custom-call | flops 1000000000 | bytes 4718592 | tf_op jit(solution)/shard_map/near/pallas_call | solution.py:166
  141.0 2.0 %collective-permute-start.11 = (f32[64,24,128]{2,1,0:T(8,128)S(1)}, f32[64,24,128]{2,1,0:T(8,128)S(1)}, u32[]{:S(2)}, u32[]{:S(2)}) collective-permute-start(f32[64,24,128]{2,1,0:T(8,128)S(1)} %get-tuple-element.45), channel_id=1, source_target_pairs={{0,4},{4,0},{8,12},{12,8},{16,20},{20,16},{24,28},{28,24},{1,5},{5... | collective-permute-start | bytes 2359304 | tf_op jit(solution)/shard_map/ppermute | solution.py:25
  143.2 3.9 %wall.7.g_ref = f32[64,24,128]{2,1,0:T(8,128)S(1)} custom-call(f32[64,24,128]{2,1,0:T(8,128)S(1)} %copy-done.8, f32[64,24,128]{2,1,0:T(8,128)S(1)} %get-tuple-element.55.s_ref, bf16[1024,256]{1,0:T(8,128)(2,1)S(1)} %copy-done.23, bf16[1024,256]{1,0:T(8,128)(2,1)S(1)} %copy-done.25, f32[64,24,128]{2,1,0:T(8,128)} %get-tuple-element.57.x_ref.rest_0_, ...), custom_call_target="tpu_custom_call" | custom-call | flops 3000000000 | bytes 6291456 | tf_op jit(solution)/shard_map/wall/pallas_call | solution.py:232
  147.4 3.3 %wall.5.g_ref = f32[64,24,128]{2,1,0:T(8,128)S(1)} custom-call(f32[64,24,128]{2,1,0:T(8,128)S(1)} %copy-done.6, f32[64,24,128]{2,1,0:T(8,128)S(1)} %get-tuple-element.44.s_ref, bf16[1024,256]{1,0:T(8,128)(2,1)S(1)} %copy-done.23, bf16[1024,256]{1,0:T(8,128)(2,1)S(1)} %copy-done.25, f32[64,24,128]{2,1,0:T(8,128)S(1)} %get-tuple-element.46.x_ref.rest_0_, ...), custom_call_target="tpu_custom_call" | custom-call | flops 3000000000 | bytes 6291456 | tf_op jit(solution)/shard_map/wall/pallas_call | solution.py:232
  150.7 5.0 %collective-permute-done.24.far_ref = f32[64,24,128]{2,1,0:T(8,128)S(1)} collective-permute-done((f32[64,24,128]{2,1,0:T(8,128)}, f32[64,24,128]{2,1,0:T(8,128)S(1)}, u32[]{:S(2)}, u32[]{:S(2)}) %collective-permute-start.24) | collective-permute-done | bytes 786464 | tf_op jit(solution)/shard_map/ppermute | solution.py:34
  155.7 5.8 %collective-permute-done.23.t_ref = f32[64,24,128]{2,1,0:T(8,128)S(1)} collective-permute-done((f32[64,24,128]{2,1,0:T(8,128)S(1)}, f32[64,24,128]{2,1,0:T(8,128)S(1)}, u32[]{:S(2)}, u32[]{:S(2)}) %collective-permute-start.23) | collective-permute-done | bytes 786464 | tf_op jit(solution)/shard_map/ppermute | solution.py:25
  161.4 2.3 %last.5 = (f32[64,24,128]{2,1,0:T(8,128)S(1)}, f32[64,24,128]{2,1,0:T(8,128)S(1)}) custom-call(s32[8]{0:T(128)S(1)} %copy-done.4, s32[1]{0:T(128)} %bitcast.sign_ref, f32[64,24,128]{2,1,0:T(8,128)S(1)} %wall.7.g_ref, f32[64,24,128]{2,1,0:T(8,128)S(1)} %collective-permute-done.23.t_ref, f32[64,24,128]{2,1,0:T(8,128)} %get-tuple-element.57.x_ref.rest_0_, ...), custom_call_target="tpu_custom_call" | custom-call | flops 1000000000 | bytes 6291456 | tf_op jit(solution)/shard_map/last/pallas_call | solution.py:306
  163.8 4.4 %collective-permute-done.12.rest_0_ = f32[48,24,128]{2,1,0:T(8,128)S(1)} collective-permute-done((f32[48,24,128]{2,1,0:T(8,128)S(1)}, f32[48,24,128]{2,1,0:T(8,128)S(1)}, u32[]{:S(2)}, u32[]{:S(2)}) %collective-permute-start.12) | collective-permute-done | bytes 589856 | tf_op jit(solution)/shard_map/ppermute | solution.py:34
  168.2 9.3 %collective-permute-done.11.t_ref = f32[64,24,128]{2,1,0:T(8,128)S(1)} collective-permute-done((f32[64,24,128]{2,1,0:T(8,128)S(1)}, f32[64,24,128]{2,1,0:T(8,128)S(1)}, u32[]{:S(2)}, u32[]{:S(2)}) %collective-permute-start.11) | collective-permute-done | bytes 786464 | tf_op jit(solution)/shard_map/ppermute | solution.py:25
  177.5 4.1 %finish.2 = (f32[192,2048]{1,0:T(8,128)}, f32[192,2048]{1,0:T(8,128)}) custom-call(s32[8]{0:T(128)S(1)} %copy-done.4, f32[64,24,128]{2,1,0:T(8,128)S(1)} %wall.5.g_ref, f32[64,24,128]{2,1,0:T(8,128)S(1)} %collective-permute-done.11.t_ref, f32[64,24,128]{2,1,0:T(8,128)S(1)} %get-tuple-element.46.x_ref.rest_0_, f32[2,576,128]{2,1,0:T(8,128)S(1)} %pad_maximum_fusion.w_ref, ...), custom_call_target="tpu_custom_call" | custom-call | flops 1000000000 | bytes 6291456 | tf_op jit(solution)/shard_map/finish/pallas_call | solution.py:380
  181.7 2.6 %finish.3 = (f32[192,2048]{1,0:T(8,128)}, f32[192,2048]{1,0:T(8,128)}) custom-call(s32[8]{0:T(128)S(1)} %copy-done.4, f32[64,24,128]{2,1,0:T(8,128)S(1)} %wall.5.g_ref, f32[64,24,128]{2,1,0:T(8,128)S(1)} %collective-permute-done.11.t_ref, f32[64,24,128]{2,1,0:T(8,128)S(1)} %get-tuple-element.46.x_ref.rest_0_, ...), custom_call_target="tpu_custom_call", output_to_operand_aliasing={{0}: (11, {}), {1}: (12, {})} | custom-call | flops 1000000000 | bytes 6291456 | tf_op jit(solution)/shard_map/finish/pallas_call | solution.py:380
  (90 shorter events, 2.1 us)
Async XLA Ops:
  0.6 36.4 %collective-permute-start = (f32[192,2048]{1,0:T(8,128)}, f32[192,2048]{1,0:T(8,128)S(1)}, u32[]{:S(2)}, u32[]{:S(2)}) collective-permute-start(f32[192,2048]{1,0:T(8,128)} %x_ref.3), channel_id=1, source_target_pairs={{0,24},{4,12},{8,0},{12,20},{16,8},{20,28},{24,16},{28,4},{1,25},{... | collective-permute-start | bytes 4718600 | tf_op jit(solution)/shard_map/ppermute | solution.py:34
  2.6 4.8 %copy-start.30 = (s32[8,64]{1,0:T(8,128)S(1)}, s32[8,64]{1,0:T(8,128)}, u32[]{:S(2)}) copy-start(s32[8,64]{1,0:T(8,128)} %param.16) | copy-start | bytes 6148
  2.6 4.8 %copy-start.28 = (f32[8,192,64]{1,2,0:T(8,128)S(1)}, f32[8,192,64]{1,2,0:T(8,128)}, u32[]{:S(2)}) copy-start(f32[8,192,64]{1,2,0:T(8,128)} %param.14) | copy-start | bytes 1179652
  2.6 4.9 %copy-start.29 = (f32[192,64]{0,1:T(8,128)S(1)}, f32[192,64]{0,1:T(8,128)}, u32[]{:S(2)}) copy-start(f32[192,64]{0,1:T(8,128)} %param.13) | copy-start | bytes 147460
  5.8 20.7 %collective-permute-start.3 = (f32[64,24,128]{2,1,0:T(8,128)}, f32[64,24,128]{2,1,0:T(8,128)}, u32[]{:S(2)}, u32[]{:S(2)}) collective-permute-start(f32[64,24,128]{2,1,0:T(8,128)} %get-tuple-element.41.x_ref.rest_0_), channel_id=1, source_target_pairs={{0,2},{1,3},{2,0},{3,1},{4,6},{5,7},{6,4},{7,5},{8,10},{9,11},{10,... | collective-permute-start | bytes 2359304 | tf_op jit(solution)/shard_map/ppermute | solution.py:20
  7.7 3.5 %copy-start.26 = (f32[1,576,128]{2,1,0:T(8,128)}, f32[1,576,128]{2,1,0:T(8,128)S(1)}, u32[]{:S(2)}) copy-start(f32[1,576,128]{2,1,0:T(8,128)S(1)} %get-tuple-element.62) | copy-start | bytes 884740
  7.8 3.5 %copy-start.27 = (f32[1,576,128]{2,1,0:T(8,128)}, f32[1,576,128]{2,1,0:T(8,128)S(1)}, u32[]{:S(2)}) copy-start(f32[1,576,128]{2,1,0:T(8,128)S(1)} %get-tuple-element.63) | copy-start | bytes 884740
  8.7 30.8 %copy-start.4 = (s32[8]{0:T(128)S(1)}, s32[8]{0:T(128)}, u32[]{:S(2)}) copy-start(s32[8]{0:T(128)} %off_ref.17) | copy-start | bytes 100
  8.7 30.7 %collective-permute-start.1 = (f32[2,512,128]{2,1,0:T(8,128)}, f32[2,512,128]{2,1,0:T(8,128)S(1)}, u32[]{:S(2)}, u32[]{:S(2)}) collective-permute-start(f32[2,512,128]{2,1,0:T(8,128)} %fusion), channel_id=1, source_target_pairs={{0,4},{4,0},{8,12},{12,8},{16,20},{20,16},{24,28},{28,24},{1,5},{5... | collective-permute-start | bytes 1572872 | tf_op jit(solution)/shard_map/ppermute | solution.py:25
  11.3 35.8 %collective-permute-start.15 = (f32[64,24,128]{2,1,0:T(8,128)S(1)}, f32[64,24,128]{2,1,0:T(8,128)}, u32[]{:S(2)}, u32[]{:S(2)}) collective-permute-start(f32[64,24,128]{2,1,0:T(8,128)S(1)} %get-tuple-element.52.x_ref.rest_0_), channel_id=1, source_target_pairs={{0,2},{1,3},{2,0},{3,1},{4,6},{5,7},{6,4},{7,5},{8,10},{9,11},{10,... | collective-permute-start | bytes 2359304 | tf_op jit(solution)/shard_map/ppermute | solution.py:20
  11.8 35.3 %collective-permute-start.2 = (f32[64,24,128]{2,1,0:T(8,128)}, f32[64,24,128]{2,1,0:T(8,128)}, u32[]{:S(2)}, u32[]{:S(2)}) collective-permute-start(f32[64,24,128]{2,1,0:T(8,128)} %get-tuple-element.41.x_ref.rest_0_), channel_id=1, source_target_pairs={{0,1},{1,0},{2,3},{3,2},{4,5},{5,4},{6,7},{7,6},{8,9},{9,8},{10,11... | collective-permute-start | bytes 2359304 | tf_op jit(solution)/shard_map/ppermute | solution.py:20
  26.6 25.5 %collective-permute-start.4 = (f32[64,24,128]{2,1,0:T(8,128)}, f32[64,24,128]{2,1,0:T(8,128)S(1)}, u32[]{:S(2)}, u32[]{:S(2)}) collective-permute-start(f32[64,24,128]{2,1,0:T(8,128)} %collective-permute-done.3.rest_2_), channel_id=1, source_target_pairs={{0,1},{1,0},{2,3},{3,2},{4,5},{5,4},{6,7},{7,6},{8,9},{9,8},{10,11... | collective-permute-start | bytes 2359304 | tf_op jit(solution)/shard_map/ppermute | solution.py:20
  39.4 8.2 %copy-start.15 = (f32[2,512,128]{2,1,0:T(8,128)}, f32[2,512,128]{2,1,0:T(8,128)S(1)}, u32[]{:S(2)}) copy-start(f32[2,512,128]{2,1,0:T(8,128)S(1)} %collective-permute-done.1.theirs_ref) | copy-start | bytes 1572868
  43.7 20.4 %collective-permute-start.5 = (f32[64,24,128]{2,1,0:T(8,128)S(1)}, f32[64,24,128]{2,1,0:T(8,128)S(1)}, u32[]{:S(2)}, u32[]{:S(2)}) collective-permute-start(f32[64,24,128]{2,1,0:T(8,128)S(1)} %get-tuple-element.38), channel_id=1, source_target_pairs={{0,4},{4,0},{8,12},{12,8},{16,20},{20,16},{24,28},{28,24},{1,5},{5... | collective-permute-start | bytes 2359304 | tf_op jit(solution)/shard_map/ppermute | solution.py:25
  45.2 32.1 %collective-permute-start.6 = (f32[64,24,128]{2,1,0:T(8,128)}, f32[64,24,128]{2,1,0:T(8,128)}, u32[]{:S(2)}, u32[]{:S(2)}) collective-permute-start(f32[64,24,128]{2,1,0:T(8,128)} %get-tuple-element.41.x_ref.rest_0_), channel_id=1, source_target_pairs={{0,8},{4,28},{8,16},{12,4},{16,24},{20,12},{24,0},{28,20},{1,9},{5... | collective-permute-start | bytes 2359304 | tf_op jit(solution)/shard_map/ppermute | solution.py:34
  47.1 33.1 %collective-permute-start.14 = (f32[64,24,128]{2,1,0:T(8,128)S(1)}, f32[64,24,128]{2,1,0:T(8,128)}, u32[]{:S(2)}, u32[]{:S(2)}) collective-permute-start(f32[64,24,128]{2,1,0:T(8,128)S(1)} %get-tuple-element.52.x_ref.rest_0_), channel_id=1, source_target_pairs={{0,1},{1,0},{2,3},{3,2},{4,5},{5,4},{6,7},{7,6},{8,9},{9,8},{10,11... | collective-permute-start | bytes 2359304 | tf_op jit(solution)/shard_map/ppermute | solution.py:20
  47.1 33.1 %collective-permute-start.16 = (f32[64,24,128]{2,1,0:T(8,128)}, f32[64,24,128]{2,1,0:T(8,128)}, u32[]{:S(2)}, u32[]{:S(2)}) collective-permute-start(f32[64,24,128]{2,1,0:T(8,128)} %collective-permute-done.15.rest_2_), channel_id=1, source_target_pairs={{0,1},{1,0},{2,3},{3,2},{4,5},{5,4},{6,7},{7,6},{8,9},{9,8},{10,11... | collective-permute-start | bytes 2359304 | tf_op jit(solution)/shard_map/ppermute | solution.py:20
  47.6 20.8 %copy-start.1 = (f32[192,2048]{1,0:T(8,128)S(1)}, f32[192,2048]{1,0:T(8,128)}, u32[]{:S(2)}) copy-start(f32[192,2048]{1,0:T(8,128)} %x_ref.2) | copy-start | bytes 4718596
  52.0 18.7 %copy-start.13 = (f32[384,384]{1,0:T(8,128)S(1)}, f32[384,384]{1,0:T(8,128)}, u32[]{:S(2)}) copy-start(f32[384,384]{1,0:T(8,128)} %even_ref.1) | copy-start | bytes 1769476
  52.9 30.9 %collective-permute-start.17 = (f32[64,24,128]{2,1,0:T(8,128)}, f32[64,24,128]{2,1,0:T(8,128)}, u32[]{:S(2)}, u32[]{:S(2)}) collective-permute-start(f32[64,24,128]{2,1,0:T(8,128)} %get-tuple-element.51), channel_id=1, source_target_pairs={{0,4},{4,0},{8,12},{12,8},{16,20},{20,16},{24,28},{28,24},{1,5},{5... | collective-permute-start | bytes 2359304 | tf_op jit(solution)/shard_map/ppermute | solution.py:25
  65.0 41.9 %collective-permute-start.18 = (f32[64,24,128]{2,1,0:T(8,128)S(1)}, f32[64,24,128]{2,1,0:T(8,128)}, u32[]{:S(2)}, u32[]{:S(2)}) collective-permute-start(f32[64,24,128]{2,1,0:T(8,128)S(1)} %get-tuple-element.52.x_ref.rest_0_), channel_id=1, source_target_pairs={{0,8},{4,28},{8,16},{12,4},{16,24},{20,12},{24,0},{28,20},{1,9},{5... | collective-permute-start | bytes 2359304 | tf_op jit(solution)/shard_map/ppermute | solution.py:34
  68.4 2.4 %copy-start.17 = (f32[192,192]{1,0:T(8,128)S(1)}, f32[192,192]{1,0:T(8,128)}, u32[]{:S(2)}) copy-start(f32[192,192]{1,0:T(8,128)} %inv_ref.1) | copy-start | bytes 442372
  68.4 4.9 %copy-start.12 = (f32[64,24,128]{2,1,0:T(8,128)S(1)}, f32[64,24,128]{2,1,0:T(8,128)}, u32[]{:S(2)}) copy-start(f32[64,24,128]{2,1,0:T(8,128)} %copy-done.11) | copy-start | bytes 2359300
  70.7 6.5 %copy-start.5 = (f32[64,24,128]{2,1,0:T(8,128)}, f32[64,24,128]{2,1,0:T(8,128)S(1)}, u32[]{:S(2)}) copy-start(f32[64,24,128]{2,1,0:T(8,128)S(1)} %get-tuple-element.32.f_ref) | copy-start | bytes 2359300
  70.8 9.4 %copy-start.7 = (f32[64,24,128]{2,1,0:T(8,128)}, f32[64,24,128]{2,1,0:T(8,128)S(1)}, u32[]{:S(2)}) copy-start(f32[64,24,128]{2,1,0:T(8,128)S(1)} %get-tuple-element.47.f_ref) | copy-start | bytes 2359300
  70.8 1.5 copy-start.14
  73.3 6.9 %copy-start.22 = (bf16[1024,256]{1,0:T(8,128)(2,1)}, bf16[1024,256]{1,0:T(8,128)(2,1)S(1)}, u32[]{:S(2)}) copy-start(bf16[1024,256]{1,0:T(8,128)(2,1)S(1)} %get-tuple-element.36.mh_ref) | copy-start | bytes 1572868
  73.3 6.9 %copy-start.24 = (bf16[1024,256]{1,0:T(8,128)(2,1)}, bf16[1024,256]{1,0:T(8,128)(2,1)S(1)}, u32[]{:S(2)}) copy-start(bf16[1024,256]{1,0:T(8,128)(2,1)S(1)} %get-tuple-element.37.ml_ref) | copy-start | bytes 1572868
  73.4 3.8 %copy-start.3 = (f32[64,24,128]{2,1,0:T(8,128)S(1)}, f32[64,24,128]{2,1,0:T(8,128)}, u32[]{:S(2)}) copy-start(f32[64,24,128]{2,1,0:T(8,128)} %copy-done.2) | copy-start | bytes 2359300
  77.3 3.0 %copy-start.19 = (f32[64,24,128]{2,1,0:T(8,128)S(1)}, f32[64,24,128]{2,1,0:T(8,128)}, u32[]{:S(2)}) copy-start(f32[64,24,128]{2,1,0:T(8,128)} %copy-done.18) | copy-start | bytes 2359300
  80.2 32.2 %collective-permute-start.7 = (f32[64,24,128]{2,1,0:T(8,128)S(1)}, f32[64,24,128]{2,1,0:T(8,128)S(1)}, u32[]{:S(2)}, u32[]{:S(2)}) collective-permute-start(f32[64,24,128]{2,1,0:T(8,128)S(1)} %get-tuple-element.46.x_ref.rest_0_), channel_id=1, source_target_pairs={{0,24},{4,12},{8,0},{12,20},{16,8},{20,28},{24,16},{28,4},{1,25},{... | collective-permute-start | bytes 2359304 | tf_op jit(solution)/shard_map/ppermute | solution.py:34
  83.8 47.2 %copy-start.16 = (f32[2,512,128]{2,1,0:T(8,128)S(1)}, f32[2,512,128]{2,1,0:T(8,128)}, u32[]{:S(2)}) copy-start(f32[2,512,128]{2,1,0:T(8,128)} %copy-done.15) | copy-start | bytes 1572868
  110.4 12.3 %collective-permute-start.21 = (f32[64,24,128]{2,1,0:T(8,128)}, f32[64,24,128]{2,1,0:T(8,128)}, u32[]{:S(2)}, u32[]{:S(2)}) collective-permute-start(f32[64,24,128]{2,1,0:T(8,128)} %get-tuple-element.57.x_ref.rest_0_), channel_id=1, source_target_pairs={{0,2},{1,3},{2,0},{3,1},{4,6},{5,7},{6,4},{7,5},{8,10},{9,11},{10,... | collective-permute-start | bytes 2359304 | tf_op jit(solution)/shard_map/ppermute | solution.py:20
  111.9 19.1 %collective-permute-start.9 = (f32[64,24,128]{2,1,0:T(8,128)S(1)}, f32[64,24,128]{2,1,0:T(8,128)S(1)}, u32[]{:S(2)}, u32[]{:S(2)}) collective-permute-start(f32[64,24,128]{2,1,0:T(8,128)S(1)} %get-tuple-element.46.x_ref.rest_0_), channel_id=1, source_target_pairs={{0,2},{1,3},{2,0},{3,1},{4,6},{5,7},{6,4},{7,5},{8,10},{9,11},{10,... | collective-permute-start | bytes 2359304 | tf_op jit(solution)/shard_map/ppermute | solution.py:20
  112.4 22.4 %collective-permute-start.19 = (f32[64,24,128]{2,1,0:T(8,128)}, f32[64,24,128]{2,1,0:T(8,128)}, u32[]{:S(2)}, u32[]{:S(2)}) collective-permute-start(f32[64,24,128]{2,1,0:T(8,128)} %get-tuple-element.57.x_ref.rest_0_), channel_id=1, source_target_pairs={{0,24},{4,12},{8,0},{12,20},{16,8},{20,28},{24,16},{28,4},{1,25},{... | collective-permute-start | bytes 2359304 | tf_op jit(solution)/shard_map/ppermute | solution.py:34
  112.4 28.5 %collective-permute-start.20 = (f32[64,24,128]{2,1,0:T(8,128)}, f32[64,24,128]{2,1,0:T(8,128)}, u32[]{:S(2)}, u32[]{:S(2)}) collective-permute-start(f32[64,24,128]{2,1,0:T(8,128)} %get-tuple-element.57.x_ref.rest_0_), channel_id=1, source_target_pairs={{0,1},{1,0},{2,3},{3,2},{4,5},{5,4},{6,7},{7,6},{8,9},{9,8},{10,11... | collective-permute-start | bytes 2359304 | tf_op jit(solution)/shard_map/ppermute | solution.py:20
  113.3 27.7 %collective-permute-start.8 = (f32[64,24,128]{2,1,0:T(8,128)S(1)}, f32[64,24,128]{2,1,0:T(8,128)}, u32[]{:S(2)}, u32[]{:S(2)}) collective-permute-start(f32[64,24,128]{2,1,0:T(8,128)S(1)} %get-tuple-element.46.x_ref.rest_0_), channel_id=1, source_target_pairs={{0,1},{1,0},{2,3},{3,2},{4,5},{5,4},{6,7},{7,6},{8,9},{9,8},{10,11... | collective-permute-start | bytes 2359304 | tf_op jit(solution)/shard_map/ppermute | solution.py:20
  122.7 20.5 %collective-permute-start.22 = (f32[64,24,128]{2,1,0:T(8,128)}, f32[64,24,128]{2,1,0:T(8,128)}, u32[]{:S(2)}, u32[]{:S(2)}) collective-permute-start(f32[64,24,128]{2,1,0:T(8,128)} %collective-permute-done.21.rest_2_), channel_id=1, source_target_pairs={{0,1},{1,0},{2,3},{3,2},{4,5},{5,4},{6,7},{7,6},{8,9},{9,8},{10,11... | collective-permute-start | bytes 2359304 | tf_op jit(solution)/shard_map/ppermute | solution.py:20
  131.0 16.1 %collective-permute-start.10 = (f32[64,24,128]{2,1,0:T(8,128)S(1)}, f32[64,24,128]{2,1,0:T(8,128)}, u32[]{:S(2)}, u32[]{:S(2)}) collective-permute-start(f32[64,24,128]{2,1,0:T(8,128)S(1)} %collective-permute-done.9.rest_2_), channel_id=1, source_target_pairs={{0,1},{1,0},{2,3},{3,2},{4,5},{5,4},{6,7},{7,6},{8,9},{9,8},{10,11... | collective-permute-start | bytes 2359304 | tf_op jit(solution)/shard_map/ppermute | solution.py:20
  134.8 20.9 %collective-permute-start.24 = (f32[64,24,128]{2,1,0:T(8,128)}, f32[64,24,128]{2,1,0:T(8,128)S(1)}, u32[]{:S(2)}, u32[]{:S(2)}) collective-permute-start(f32[64,24,128]{2,1,0:T(8,128)} %get-tuple-element.57.x_ref.rest_0_), channel_id=1, source_target_pairs={{0,8},{4,28},{8,16},{12,4},{16,24},{20,12},{24,0},{28,20},{1,9},{5... | collective-permute-start | bytes 2359304 | tf_op jit(solution)/shard_map/ppermute | solution.py:34
  137.4 5.8 %copy-start.25 = (bf16[1024,256]{1,0:T(8,128)(2,1)S(1)}, bf16[1024,256]{1,0:T(8,128)(2,1)}, u32[]{:S(2)}) copy-start(bf16[1024,256]{1,0:T(8,128)(2,1)} %copy-done.24) | copy-start | bytes 1572868
  140.9 2.3 %copy-start.8 = (f32[64,24,128]{2,1,0:T(8,128)S(1)}, f32[64,24,128]{2,1,0:T(8,128)}, u32[]{:S(2)}) copy-start(f32[64,24,128]{2,1,0:T(8,128)} %copy-done.7) | copy-start | bytes 2359300
  140.9 2.3 %copy-start.23 = (bf16[1024,256]{1,0:T(8,128)(2,1)S(1)}, bf16[1024,256]{1,0:T(8,128)(2,1)}, u32[]{:S(2)}) copy-start(bf16[1024,256]{1,0:T(8,128)(2,1)} %copy-done.22) | copy-start | bytes 1572868
  141.0 20.5 %collective-permute-start.23 = (f32[64,24,128]{2,1,0:T(8,128)S(1)}, f32[64,24,128]{2,1,0:T(8,128)S(1)}, u32[]{:S(2)}, u32[]{:S(2)}) collective-permute-start(f32[64,24,128]{2,1,0:T(8,128)S(1)} %get-tuple-element.56), channel_id=1, source_target_pairs={{0,4},{4,0},{8,12},{12,8},{16,20},{20,16},{24,28},{28,24},{1,5},{5... | collective-permute-start | bytes 2359304 | tf_op jit(solution)/shard_map/ppermute | solution.py:25
  141.0 36.5 %collective-permute-start.11 = (f32[64,24,128]{2,1,0:T(8,128)S(1)}, f32[64,24,128]{2,1,0:T(8,128)S(1)}, u32[]{:S(2)}, u32[]{:S(2)}) collective-permute-start(f32[64,24,128]{2,1,0:T(8,128)S(1)} %get-tuple-element.45), channel_id=1, source_target_pairs={{0,4},{4,0},{8,12},{12,8},{16,20},{20,16},{24,28},{28,24},{1,5},{5... | collective-permute-start | bytes 2359304 | tf_op jit(solution)/shard_map/ppermute | solution.py:25
  143.1 25.1 %collective-permute-start.12 = (f32[48,24,128]{2,1,0:T(8,128)S(1)}, f32[48,24,128]{2,1,0:T(8,128)S(1)}, u32[]{:S(2)}, u32[]{:S(2)}) collective-permute-start(f32[48,24,128]{2,1,0:T(8,128)S(1)} %constant_dynamic-slice_fusion.1), channel_id=1, source_target_pairs={{0,8},{4,28},{8,16},{12,4},{16,24},{20,12},{24,0},{28,20},{1,9},{5... | collective-permute-start | bytes 1769480 | tf_op jit(solution)/shard_map/ppermute | solution.py:34
  143.2 4.1 %copy-start.6 = (f32[64,24,128]{2,1,0:T(8,128)S(1)}, f32[64,24,128]{2,1,0:T(8,128)}, u32[]{:S(2)}) copy-start(f32[64,24,128]{2,1,0:T(8,128)} %copy-done.5) | copy-start | bytes 2359300
  147.1 34.6 %collective-permute-start.13 = (f32[16,24,128]{2,1,0:T(8,128)S(1)}, f32[16,24,128]{2,1,0:T(8,128)S(1)}, u32[]{:S(2)}, u32[]{:S(2)}) collective-permute-start(f32[16,24,128]{2,1,0:T(8,128)S(1)} %constant_dynamic-slice_fusion), channel_id=1, source_target_pairs={{0,8},{4,28},{8,16},{12,4},{16,24},{20,12},{24,0},{28,20},{1,9},{5... | collective-permute-start | bytes 589832 | tf_op jit(solution)/shard_map/ppermute | solution.py:34
  (8 other events, 8.2 us)
where the time goes:
time: 185 us; the launch traced here: 184 us
  waiting for transfers between devices  100 us (54%)
  Pallas kernels  52 us (28%)
  starting transfers between devices  20 us (11%)
  local copies, waits for them, and re-layouts  8.77 us (5%)
  other arithmetic  2.31 us (1%)
    ppermute x8, waiting for transfers between devices, far(): return lax.ppermute(value, 'span', pairs)  42.9 us
    ppermute x12, waiting for transfers between devices, exchange(): return lax.ppermute(value, 'wall', [(i, i ^ bit) for i in range(count)])  30.9 us
    ppermute x5, waiting for transfers between devices, partner(): return lax.ppermute(value, 'span', [(i, i ^ 1) for i in range(count)])  26.3 us
    pallas_call x4, Pallas kernels, wall(): pl.pallas_call(functools.partial(wall_kernel, n_blocks), out_shape=jax.Sh...  14.5 us
    pallas_call x4, Pallas kernels, near(): pl.pallas_call(functools.partial(near_kernel, bands), out_shape=(out, out...  13 us
    pallas_call x3, Pallas kernels, last(): pl.pallas_call(functools.partial(last_kernel, bands), out_shape=(out, out...  8.75 us
    ppermute x8, starting transfers between devices, far(): return lax.ppermute(value, 'span', pairs)  8.73 us
    unnamed x62, local copies, waits for them, and re-layouts  8.68 us
  transfers between devices with their start and end apart: 25, of which 10 were waited for; matrix products, arithmetic and copies ran while one was open for 1% of the time, Pallas kernels for 27%

commit v1 on v0

--- a/solution.py
+++ b/solution.py
@@ -47,20 +47,26 @@
     cw = width // chunks
     half = cw // 2
     per = LANES // width
+    lower = lax.broadcasted_iota(jnp.int32, (half, LANES), 1) < HALF
 
     def step(g, _):
-        lanes = pl.ds(pl.multiple_of(g * LANES, LANES), LANES)
-        top = x_ref[:LANES, lanes].T.reshape(per, width, LANES)
-        low = x_ref[LANES:, lanes]
-        pair = jnp.concatenate([low, pltpu.roll(low, LANES - half, 1)], 0)
-        pair = pair.T.reshape(per, width, LANES)
-        here = pl.ds(g * per, per)
-        for k, out_ref in enumerate(out_refs):
-            out_ref[here, :cw, :] = top[:, k * cw : (k + 1) * cw, :]
-            out_ref[here, cw:, :] = pair[:, k * cw : k * cw + half, :]
+        lows = []
+        for u in range(2):
+            lanes = pl.ds(pl.multiple_of((2 * g + u) * LANES, LANES), LANES)
+            top = x_ref[:LANES, lanes].T.reshape(per, width, LANES)
+            for k, out_ref in enumerate(out_refs):
+                out_ref[pl.ds((2 * g + u) * per, per), :cw, :] = top[:, k * cw : (k + 1) * cw, :]
+            lows.append(x_ref[LANES:, lanes])
+        pair = jnp.concatenate(lows, 0).T
+        for z in range(per):
+            for k, out_ref in enumerate(out_refs):
+                row = z * width + k * cw
+                first, second = pair[row : row + half], pair[row + half : row + cw]
+                out_ref[2 * g * per + z, cw:, :] = jnp.where(lower, first, pltpu.roll(second, HALF, 1))
+                out_ref[(2 * g + 1) * per + z, cw:, :] = jnp.where(lower, pltpu.roll(first, HALF, 1), second)
         return 0
 
-    lax.fori_loop(0, x_ref.shape[1] // LANES, step, 0)
+    lax.fori_loop(0, x_ref.shape[1] // (2 * LANES), step, 0, unroll=2)
 
 
 def split(x, chunks, points):
@@ -79,18 +85,20 @@
     )(x)
 
 
-def join(width, sol_parts, res_parts, sol_ref, res_ref, begin, end):
-    chunks = len(sol_parts)
-    cw = width // chunks
+def join_top(width, parts, out_ref, begin, end):
+    cw = width // len(parts)
+    per = LANES // width
+    for g in range(begin, end):
+        rows = [part[g * per + z, :cw, :] for z in range(per) for part in parts]
+        out_ref[:LANES, g * LANES : (g + 1) * LANES] = jnp.concatenate(rows, 0).T
+
+
+def join_low(width, sol_parts, res_parts, sol_ref, res_ref, begin, end):
+    cw = width // len(sol_parts)
     half = cw // 2
     per = LANES // width
     lower = lax.broadcasted_iota(jnp.int32, (half, LANES), 1) < HALF
-
-    def step(g, _):
-        lanes = pl.ds(pl.multiple_of(g * LANES, LANES), LANES)
-        for out_ref, parts in ((sol_ref, sol_parts), (res_ref, res_parts)):
-            rows = [part[g * per + z, :cw, :] for z in range(per) for part in parts]
-            out_ref[:LANES, lanes] = jnp.concatenate(rows, 0).T
+    for g in range(begin, end):
         rows = []
         for z in range(per):
             for sol, res in zip(sol_parts, res_parts):
@@ -99,11 +107,18 @@
                 rows.append(jnp.where(lower, a, pltpu.roll(b, HALF, 1)))
                 rows.append(jnp.where(lower, pltpu.roll(a, HALF, 1), b))
         both = jnp.concatenate(rows, 0).T
+        lanes = slice(g * LANES, (g + 1) * LANES)
         sol_ref[LANES:, lanes] = both[:HALF]
         res_ref[LANES:, lanes] = both[HALF:]
-        return 0
-
-    lax.fori_loop(begin, end, step, 0, unroll=2)
+
+
+def own_sign():
+    return 1 - 2 * lax.rem(lax.axis_index("span"), 2)
+
+
+def read(off_ref):
+    value = off_ref[...]
+    return [value[b, 0] for b in range(value.shape[0])]
 
 
 UNROLL = 4
@@ -132,15 +147,16 @@
     return top, low
 
 
-def near_kernel(bands, off_ref, sign_ref, x_ref, far_ref, w_ref, theirs_ref, partial_ref, sum_ref, ext_ref):
+def near_kernel(bands, off_ref, x_ref, far_ref, w_ref, theirs_ref, partial_ref, sum_ref, ext_ref):
     points, rows, _ = x_ref.shape
     cw = rows * 2 // 3
-    sign = sign_ref[0]
+    sign = own_sign()
+    offsets = read(off_ref)
     own = jnp.where(sign > 0, REACH, REACH + 1)
     fill(ext_ref, [(x_ref, own), (far_ref, own + 2 * sign)], points)
 
     for out_ref, weights, shift in ((partial_ref, theirs_ref, sign), (sum_ref, w_ref, 0)):
-        starts = [(own + shift) * points + off_ref[b] for b in range(bands)]
+        starts = [(own + shift) * points + offsets[b] for b in range(bands)]
 
         def step(i, _):
             for u in range(UNROLL):
@@ -159,20 +175,20 @@
         lax.fori_loop(0, points // UNROLL, step, 0)
 
 
-def near(offsets, sign, x, first, w, theirs):
+def near(offsets, x, first, w, theirs):
     bands = offsets.shape[0]
     points, rows, _ = x.shape
     out = jax.ShapeDtypeStruct(x.shape, x.dtype)
     return pl.pallas_call(
         functools.partial(near_kernel, bands),
         out_shape=(out, out),
-        in_specs=[SMEM, SMEM, VMEM, VMEM, VMEM, VMEM],
+        in_specs=[VMEM] * 5,
         out_specs=(VMEM, VMEM),
         scratch_shapes=[pltpu.VMEM(((2 * REACH + 2) * points, rows, LANES), jnp.float32)],
         compiler_params=params(),
         cost_estimate=pl.CostEstimate(flops=1000000000, bytes_accessed=6 * x.size * 4, transcendentals=0),
         name="near",
-    )(offsets, sign, x, first, w, theirs)
+    )(offsets, x, first, w, theirs)
 
 
 def halves(value):
@@ -241,35 +257,33 @@
     )(f, s, mh, ml, *blocks)
 
 
-def far_terms(bands, lo, n, sign, off_ref, w_ref, far_ref, r_ref):
+def far_terms(lo, n, off_ref, w_ref, far_ref, r_ref):
     points, rows, _ = far_ref.shape
     cw = rows * 2 // 3
 
-    def band(b, _):
-        shift = off_ref[b] + 2 * sign * points
+    sign = own_sign()
+    for b, offset in enumerate(read(off_ref)):
+        shift = offset + 2 * sign * points
         first = jnp.maximum(lo, -shift)
         count = jnp.minimum(lo + n, points - shift) - first
 
-        def point(p):
+        def point(p, b=b, shift=shift):
             top, low = scaled(w_ref, b * points + p, far_ref[p + shift], cw)
             r_ref[p - lo, :cw, :] = r_ref[p - lo, :cw, :] - top
             r_ref[p - lo, cw:, :] = r_ref[p - lo, cw:, :] - low
 
-        def several(i, _):
+        def several(i, _, first=first, point=point):
             for u in range(UNROLL):
                 point(first + i * UNROLL + u)
             return 0
 
-        def one(i, _):
+        def one(i, _, first=first, point=point):
             point(first + i)
             return 0
 
         groups = jnp.maximum(count, 0) // UNROLL
         lax.fori_loop(0, groups, several, 0)
         lax.fori_loop(groups * UNROLL, count, one, 0)
-        return 0
-
-    lax.fori_loop(0, bands, band, 0)
 
 
 def update(x_ref, lo, r_ref, high_ref, low_ref, bh_ref, bl_ref, x_new_ref):
@@ -285,7 +299,7 @@
     x_new_ref[:, cw:, :] = x_ref[here, cw:, :] + low
 
 
-def last_kernel(bands, off_ref, sign_ref, g_ref, t_ref, x_ref, w_ref, bh_ref, bl_ref, far_ref, x_new_ref, r_ref, high_ref, low_ref):
+def last_kernel(off_ref, g_ref, t_ref, x_ref, w_ref, bh_ref, bl_ref, far_ref, x_new_ref, r_ref, high_ref, low_ref):
     points = x_ref.shape[0]
 
     def begin(i, _):
@@ -294,25 +308,24 @@
         return 0
 
     lax.fori_loop(0, points // UNROLL, begin, 0)
-    far_terms(bands, 0, points, sign_ref[0], off_ref, w_ref, far_ref, r_ref)
+    far_terms(0, points, off_ref, w_ref, far_ref, r_ref)
     update(x_ref, 0, r_ref, high_ref, low_ref, bh_ref, bl_ref, x_new_ref)
 
 
-def last(offsets, sign, g, t, x, w, bh, bl, second):
-    bands = offsets.shape[0]
+def last(offsets, g, t, x, w, bh, bl, second):
     points, rows, _ = x.shape
     out = jax.ShapeDtypeStruct(x.shape, x.dtype)
     m_rows = points * rows * 2 // 3
     return pl.pallas_call(
-        functools.partial(last_kernel, bands),
+        last_kernel,
         out_shape=(out, out),
-        in_specs=[SMEM, SMEM] + [VMEM] * 7,
+        in_specs=[VMEM] * 8,
         out_specs=(VMEM, VMEM),
         scratch_shapes=[pltpu.VMEM((m_rows, 2 * LANES), jnp.bfloat16)] * 2,
         compiler_params=params(),
         cost_estimate=pl.CostEstimate(flops=1000000000, bytes_accessed=8 * x.size * 4, transcendentals=0),
         name="last",
-    )(offsets, sign, g, t, x, w, bh, bl, second)
+    )(offsets, g, t, x, w, bh, bl, second)
 
 
 def piece_start(sizes, i, points):
@@ -321,7 +334,7 @@
     return jnp.where(even, points - before - sizes[i], before)
 
 
-def finish_kernel(bands, width, sizes, i, off_ref, g_ref, t_ref, x_ref, w_ref, bh_ref, bl_ref, *rest):
+def finish_kernel(width, sizes, i, off_ref, g_ref, t_ref, x_ref, w_ref, bh_ref, bl_ref, *rest):
     fars = rest[: i + 1]
     n_outs = 2 if i else 0
     *earlier, sol_hbm, res_hbm, far_ref, high_ref, low_ref, x_new_ref, r_ref, sol_ref, res_ref, sems = rest[i + 1 :]
@@ -329,7 +342,6 @@
         earlier = earlier[:-n_outs]
     points = x_ref.shape[0]
     n = sizes[i]
-    sign = 1 - 2 * lax.rem(lax.axis_index("span"), 2)
     lo = piece_start(sizes, i, points)
     for m, ref in enumerate(fars):
         at = piece_start(sizes, m, points)
@@ -346,16 +358,20 @@
         return 0
 
     lax.fori_loop(0, n // UNROLL, begin, 0)
-    far_terms(bands, lo, n, sign, off_ref, w_ref, far_ref, r_ref)
+    far_terms(lo, n, off_ref, w_ref, far_ref, r_ref)
+    views = [ref.at[pl.ds(lo, n)] for ref in earlier]
+    sols, ress = [*views[::2], x_new_ref], [*views[1::2], r_ref]
+    vectors = n * width // LANES
+    join_top(width, ress, res_ref, 0, vectors)
     update(x_ref, lo, r_ref, high_ref, low_ref, bh_ref, bl_ref, x_new_ref)
-    views = [ref.at[pl.ds(lo, n)] for ref in earlier]
     slabs = sems.shape[1]
-    wide = n * width // slabs
+    each = vectors // slabs
     copies = []
     for m in range(slabs):
-        join(width, [*views[::2], x_new_ref], [*views[1::2], r_ref], sol_ref, res_ref, m * wide // LANES, (m + 1) * wide // LANES)
-        here = pl.ds(m * wide, wide)
-        there = pl.ds(pl.multiple_of(lo * width + m * wide, LANES), wide)
+        join_top(width, sols, sol_ref, m * each, (m + 1) * each)
+        join_low(width, sols, ress, sol_ref, res_ref, m * each, (m + 1) * each)
+        here = pl.ds(m * each * LANES, each * LANES)
+        there = pl.ds(pl.multiple_of(lo * width + m * each * LANES, LANES), each * LANES)
         for which, (ref, hbm) in enumerate(((sol_ref, sol_hbm), (res_ref, res_hbm))):
             copy = pltpu.make_async_copy(ref.at[:, here], hbm.at[:, there], sems.at[which, m])
             copy.start()
@@ -368,7 +384,6 @@
 
 
 def finish(offsets, g, t, x, w, bh, bl, fars, earlier, outs, sizes, i, width):
-    bands = offsets.shape[0]
     points, rows, _ = x.shape
     n = sizes[i]
     piece = pltpu.VMEM((n, rows, LANES), jnp.float32)
@@ -378,9 +393,9 @@
     hbm = pl.BlockSpec(memory_space=pltpu.HBM)
     inputs = (offsets, g, t, x, w, bh, bl, *fars, *earlier)
     return pl.pallas_call(
-        functools.partial(finish_kernel, bands, width, sizes, i),
+        functools.partial(finish_kernel, width, sizes, i),
         out_shape=(out, out),
-        in_specs=[SMEM] + [VMEM] * (len(inputs) - 1) + [hbm] * len(outs),
+        in_specs=[VMEM] * len(inputs) + [hbm] * len(outs),
         out_specs=(hbm, hbm),
         input_output_aliases={len(inputs) + k: k for k in range(len(outs))},
         scratch_shapes=[
@@ -469,7 +484,7 @@
     width = breadth // points
     chunks = CHUNKS
     n_wall = lax.axis_size("wall")
-    sign = jnp.where(lax.axis_index("span") % 2 == 0, 1, -1).astype(jnp.int32)[None]
+    offsets = jnp.broadcast_to(offsets[:, None], (bands, LANES))
 
     raw_first = far(start, True)
     state = list(split(start, chunks, points))
@@ -480,7 +495,7 @@
     their_w = partner(own_w[:, : bands * points])
     mh, ml, bh, bl = prep(wall_even, wall_odd, block_inv)
     f = split(forcing, chunks, points)
-    sizes = (points - points // 4, points // 4)
+    sizes = (points * 5 // 8, points * 3 // 8)
     arrived = raw_first
     order = [0]
     bit = n_wall // 2
@@ -514,7 +529,7 @@
         theirs = []
         sums = []
         for k in range(chunks):
-            partial, own_sum = near(offsets, sign, state[k], firsts[k], own_w, their_w)
+            partial, own_sum = near(offsets, state[k], firsts[k], own_w, their_w)
             sums.append(own_sum)
             theirs.append(partner(partial))
         new = []
@@ -528,7 +543,7 @@
                     fars = seconds[k][: i + 1]
                     outs = call(offsets, g, theirs[k], state[k], own_w, bh, bl, fars, earlier, outs)
                 return outs
-            new.append(last(offsets, sign, g, theirs[k], state[k], own_w, bh, bl, seconds[k]))
+            new.append(last(offsets, g, theirs[k], state[k], own_w, bh, bl, seconds[k]))
         state = [pair[0] for pair in new]
 
 

time: 185 us -> 179 us (0.968)
  the two profiles are of different devices: /device:TPU:16 before, /device:TPU:28 now
where the time goes in v1:
time: 179 us; the launch traced here: 178 us
  waiting for transfers between devices  102 us (57%)
  Pallas kernels  44.9 us (25%)
  starting transfers between devices  15.2 us (8%)
  local copies, waits for them, and re-layouts  14 us (8%)
    ppermute x8, waiting for transfers between devices, far(): return lax.ppermute(value, 'span', pairs)  38.9 us
    ppermute x12, waiting for transfers between devices, exchange(): return lax.ppermute(value, 'wall', [(i, i ^ bit) for i in range(count)])  32.6 us
    ppermute x5, waiting for transfers between devices, partner(): return lax.ppermute(value, 'span', [(i, i ^ 1) for i in range(count)])  30.7 us
    pallas_call x4, Pallas kernels, wall(): pl.pallas_call(functools.partial(wall_kernel, n_blocks), out_shape=jax.Sh...  13.9 us
    unnamed x76, local copies, waits for them, and re-layouts  13.8 us
    pallas_call x4, Pallas kernels, near(): pl.pallas_call(functools.partial(near_kernel, bands), out_shape=(out, out...  12.6 us
    pallas_call x3, Pallas kernels, last(): pl.pallas_call(last_kernel, out_shape=(out, out), in_specs=[VMEM] * 8, ou...  8.53 us
    ppermute x8, starting transfers between devices, far(): return lax.ppermute(value, 'span', pairs)  8.36 us
  transfers between devices with their start and end apart: 25, of which 9 were waited for; matrix products, arithmetic and copies ran while one was open for 0% of the time, Pallas kernels for 24%

profile of v1, /device:TPU:28, one launch (start us, length us, event | category | flops | bytes accessed | tf_op | source)
XLA Modules:
  0.0 177.9 jit_solution(15722524626219780986)
XLA Ops:
  1.1 1.4 copy-done
  2.6 1.8 %split.4 = (f32[64,24,128]{2,1,0:T(8,128)S(1)}, f32[64,24,128]{2,1,0:T(8,128)}) custom-call(f32[192,2048]{1,0:T(8,128)S(1)} %copy-done), custom_call_target="tpu_custom_call" | custom-call | bytes 3145728 | tf_op jit(solution)/shard_map/split/pallas_call | solution.py:77
  4.4 0.5 collective-permute-start.3
  5.4 1.3 collective-permute-start.1
  6.7 1.5 collective-permute-start.15
  8.3 16.8 %collective-permute-done.3.rest_2_ = f32[64,24,128]{2,1,0:T(8,128)S(1)} collective-permute-done((f32[64,24,128]{2,1,0:T(8,128)}, f32[64,24,128]{2,1,0:T(8,128)S(1)}, u32[]{:S(2)}, u32[]{:S(2)}) %collective-permute-start.3) | collective-permute-done | bytes 786464 | tf_op jit(solution)/shard_map/ppermute | solution.py:20
  25.0 13.8 %collective-permute-done.x_ref = f32[192,2048]{1,0:T(8,128)S(1)} collective-permute-done((f32[192,2048]{1,0:T(8,128)}, f32[192,2048]{1,0:T(8,128)S(1)}, u32[]{:S(2)}, u32[]{:S(2)}) %collective-permute-start) | collective-permute-done | bytes 1572896 | tf_op jit(solution)/shard_map/ppermute | solution.py:34
  38.8 0.9 split.5
  39.9 3.4 %near.4 = (f32[64,24,128]{2,1,0:T(8,128)S(1)}, f32[64,24,128]{2,1,0:T(8,128)S(1)}) custom-call(s32[8,128]{1,0:T(8,128)S(1)} %broadcast_in_dim.6.off_ref, f32[64,24,128]{2,1,0:T(8,128)} %get-tuple-element.41.x_ref.rest_0_, f32[64,24,128]{2,1,0:T(8,128)S(1)} %get-tuple-element.34.far_ref, f32[2,576,128]{2,1,0:T(8,128)S(1)} %pad_maximum_fusion.w_ref, ...), custom_call_target="tpu_custom_call" | custom-call | flops 1000000000 | bytes 4718592 | tf_op jit(solution)/shard_map/near/pallas_call | solution.py:182
  43.3 0.9 copy-done.28
  44.1 1.8 collective-permute-start.6
  45.9 0.9 copy-done.14
  46.8 0.5 collective-permute-start.16
  47.3 3.0 %near.6 = (f32[64,24,128]{2,1,0:T(8,128)}, f32[64,24,128]{2,1,0:T(8,128)S(1)}) custom-call(s32[8,128]{1,0:T(8,128)S(1)} %broadcast_in_dim.6.off_ref, f32[64,24,128]{2,1,0:T(8,128)S(1)} %get-tuple-element.52.x_ref.rest_0_, f32[64,24,128]{2,1,0:T(8,128)S(1)} %get-tuple-element.49.far_ref, f32[2,576,128]{2,1,0:T(8,128)S(1)} %pad_maximum_fusion.w_ref, ...), custom_call_target="tpu_custom_call" | custom-call | flops 1000000000 | bytes 4718592 | tf_op jit(solution)/shard_map/near/pallas_call | solution.py:182
  50.3 0.9 copy-done.26
  51.2 0.9 copy-done.16
  52.4 12.2 %collective-permute-done.5.t_ref = f32[64,24,128]{2,1,0:T(8,128)S(1)} collective-permute-done((f32[64,24,128]{2,1,0:T(8,128)S(1)}, f32[64,24,128]{2,1,0:T(8,128)S(1)}, u32[]{:S(2)}, u32[]{:S(2)}) %collective-permute-start.5) | collective-permute-done | bytes 786464 | tf_op jit(solution)/shard_map/ppermute | solution.py:25
  64.6 0.9 copy-done.2
  65.5 0.9 split.3
  66.4 1.5 copy-done.18
  67.9 1.1 copy-done.19
  69.0 1.0 prep.1
  70.1 3.3 %wall.4.g_ref = f32[64,24,128]{2,1,0:T(8,128)S(1)} custom-call(f32[64,24,128]{2,1,0:T(8,128)S(1)} %get-tuple-element.32.f_ref, f32[64,24,128]{2,1,0:T(8,128)S(1)} %copy-done.29, bf16[1024,256]{1,0:T(8,128)(2,1)S(1)} %get-tuple-element.36.mh_ref, bf16[1024,256]{1,0:T(8,128)(2,1)S(1)} %get-tuple-element.37.ml_ref, ...), custom_call_target="tpu_custom_call" | custom-call | flops 3000000000 | bytes 6291456 | tf_op jit(solution)/shard_map/wall/pallas_call | solution.py:248
  73.5 2.8 %last.3 = (f32[64,24,128]{2,1,0:T(8,128)S(1)}, f32[64,24,128]{2,1,0:T(8,128)}) custom-call(s32[8,128]{1,0:T(8,128)S(1)} %broadcast_in_dim.6.off_ref, f32[64,24,128]{2,1,0:T(8,128)S(1)} %wall.4.g_ref, f32[64,24,128]{2,1,0:T(8,128)S(1)} %copy-done.3, f32[64,24,128]{2,1,0:T(8,128)} %get-tuple-element.41.x_ref.rest_0_, ...), custom_call_target="tpu_custom_call" | custom-call | flops 1000000000 | bytes 6291456 | tf_op jit(solution)/shard_map/last/pallas_call | solution.py:319
  76.3 2.0 %collective-permute-start.7 = (f32[64,24,128]{2,1,0:T(8,128)S(1)}, f32[64,24,128]{2,1,0:T(8,128)S(1)}, u32[]{:S(2)}, u32[]{:S(2)}) collective-permute-start(f32[64,24,128]{2,1,0:T(8,128)S(1)} %get-tuple-element.46.x_ref.rest_0_), channel_id=1, source_target_pairs={{0,24},{4,12},{8,0},{12,20},{16,8},{20,28},{24,16},{28,4},{1,25},{... | collective-permute-start | bytes 2359304 | tf_op jit(solution)/shard_map/ppermute | solution.py:34
  78.4 3.5 %wall.6.g_ref = f32[64,24,128]{2,1,0:T(8,128)S(1)} custom-call(f32[64,24,128]{2,1,0:T(8,128)S(1)} %get-tuple-element.47.f_ref, f32[64,24,128]{2,1,0:T(8,128)S(1)} %copy-done.27, bf16[1024,256]{1,0:T(8,128)(2,1)S(1)} %get-tuple-element.36.mh_ref, bf16[1024,256]{1,0:T(8,128)(2,1)S(1)} %get-tuple-element.37.ml_ref, ...), custom_call_target="tpu_custom_call" | custom-call | flops 3000000000 | bytes 6291456 | tf_op jit(solution)/shard_map/wall/pallas_call | solution.py:248
  82.0 24.6 %collective-permute-done.18.far_ref = f32[64,24,128]{2,1,0:T(8,128)} collective-permute-done((f32[64,24,128]{2,1,0:T(8,128)S(1)}, f32[64,24,128]{2,1,0:T(8,128)}, u32[]{:S(2)}, u32[]{:S(2)}) %collective-permute-start.18) | collective-permute-done | bytes 786464 | tf_op jit(solution)/shard_map/ppermute | solution.py:34
  106.5 3.4 %last.4 = (f32[64,24,128]{2,1,0:T(8,128)}, f32[64,24,128]{2,1,0:T(8,128)}) custom-call(s32[8,128]{1,0:T(8,128)S(1)} %broadcast_in_dim.6.off_ref, f32[64,24,128]{2,1,0:T(8,128)S(1)} %wall.6.g_ref, f32[64,24,128]{2,1,0:T(8,128)} %collective-permute-done.17.t_ref, f32[64,24,128]{2,1,0:T(8,128)S(1)} %get-tuple-element.52.x_ref.rest_0_, ...), custom_call_target="tpu_custom_call" | custom-call | flops 1000000000 | bytes 6291456 | tf_op jit(solution)/shard_map/last/pallas_call | solution.py:319
  109.9 0.5 collective-permute-start.21
  110.4 1.5 collective-permute-start.9
  112.0 0.9 copy-done.8
  112.8 3.8 %collective-permute-start.24 = (f32[64,24,128]{2,1,0:T(8,128)}, f32[64,24,128]{2,1,0:T(8,128)S(1)}, u32[]{:S(2)}, u32[]{:S(2)}) collective-permute-start(f32[64,24,128]{2,1,0:T(8,128)} %get-tuple-element.57.x_ref.rest_0_), channel_id=1, source_target_pairs={{0,8},{4,28},{8,16},{12,4},{16,24},{20,12},{24,0},{28,20},{1,9},{5... | collective-permute-start | bytes 2359304 | tf_op jit(solution)/shard_map/ppermute | solution.py:34
  116.7 13.8 %collective-permute-done.21.rest_2_ = f32[64,24,128]{2,1,0:T(8,128)} collective-permute-done((f32[64,24,128]{2,1,0:T(8,128)}, f32[64,24,128]{2,1,0:T(8,128)}, u32[]{:S(2)}, u32[]{:S(2)}) %collective-permute-start.21) | collective-permute-done | bytes 786464 | tf_op jit(solution)/shard_map/ppermute | solution.py:20
  131.0 4.1 %near.7 = (f32[64,24,128]{2,1,0:T(8,128)}, f32[64,24,128]{2,1,0:T(8,128)S(1)}) custom-call(s32[8,128]{1,0:T(8,128)S(1)} %broadcast_in_dim.6.off_ref, f32[64,24,128]{2,1,0:T(8,128)} %get-tuple-element.57.x_ref.rest_0_, f32[64,24,128]{2,1,0:T(8,128)S(1)} %collective-permute-done.19.far_ref, f32[2,576,128]{2,1,0:T(8,128)S(1)} %pad_maximum_fusion.w_ref, ...), custom_call_target="tpu_custom_call" | custom-call | flops 1000000000 | bytes 4718592 | tf_op jit(solution)/shard_map/near/pallas_call | solution.py:182
  135.1 0.9 copy-done.24
  136.1 0.9 copy-done.12
  137.0 1.9 %collective-permute-done.9.rest_2_ = f32[64,24,128]{2,1,0:T(8,128)} collective-permute-done((f32[64,24,128]{2,1,0:T(8,128)S(1)}, f32[64,24,128]{2,1,0:T(8,128)}, u32[]{:S(2)}, u32[]{:S(2)}) %collective-permute-start.9) | collective-permute-done | bytes 786464 | tf_op jit(solution)/shard_map/ppermute | solution.py:20
  138.9 1.1 copy-done.9
  140.1 1.0 copy-done.22
  141.1 2.1 %near.5 = (f32[64,24,128]{2,1,0:T(8,128)S(1)}, f32[64,24,128]{2,1,0:T(8,128)S(1)}) custom-call(s32[8,128]{1,0:T(8,128)S(1)} %broadcast_in_dim.6.off_ref, f32[64,24,128]{2,1,0:T(8,128)S(1)} %get-tuple-element.46.x_ref.rest_0_, f32[64,24,128]{2,1,0:T(8,128)S(1)} %copy-done.9, f32[2,576,128]{2,1,0:T(8,128)S(1)} %pad_maximum_fusion.w_ref, ...), custom_call_target="tpu_custom_call" | custom-call | flops 1000000000 | bytes 4718592 | tf_op jit(solution)/shard_map/near/pallas_call | solution.py:182
  143.2 0.6 collective-permute-start.11
  144.6 3.5 %wall.7.g_ref = f32[64,24,128]{2,1,0:T(8,128)S(1)} custom-call(f32[64,24,128]{2,1,0:T(8,128)S(1)} %copy-done.7, f32[64,24,128]{2,1,0:T(8,128)S(1)} %copy-done.25, bf16[1024,256]{1,0:T(8,128)(2,1)S(1)} %copy-done.31, bf16[1024,256]{1,0:T(8,128)(2,1)S(1)} %copy-done.33, f32[64,24,128]{2,1,0:T(8,128)} %get-tuple-element.57.x_ref.rest_0_, ...), custom_call_target="tpu_custom_call" | custom-call | flops 3000000000 | bytes 6291456 | tf_op jit(solution)/shard_map/wall/pallas_call | solution.py:248
  148.1 8.6 %collective-permute-done.23.t_ref = f32[64,24,128]{2,1,0:T(8,128)S(1)} collective-permute-done((f32[64,24,128]{2,1,0:T(8,128)}, f32[64,24,128]{2,1,0:T(8,128)S(1)}, u32[]{:S(2)}, u32[]{:S(2)}) %collective-permute-start.23) | collective-permute-done | bytes 786464 | tf_op jit(solution)/shard_map/ppermute | solution.py:25
  156.7 2.3 %last.5 = (f32[64,24,128]{2,1,0:T(8,128)S(1)}, f32[64,24,128]{2,1,0:T(8,128)S(1)}) custom-call(s32[8,128]{1,0:T(8,128)S(1)} %broadcast_in_dim.6.off_ref, f32[64,24,128]{2,1,0:T(8,128)S(1)} %wall.7.g_ref, f32[64,24,128]{2,1,0:T(8,128)S(1)} %collective-permute-done.23.t_ref, f32[64,24,128]{2,1,0:T(8,128)} %get-tuple-element.57.x_ref.rest_0_, ...), custom_call_target="tpu_custom_call" | custom-call | flops 1000000000 | bytes 6291456 | tf_op jit(solution)/shard_map/last/pallas_call | solution.py:319
  159.0 3.5 %wall.5.g_ref = f32[64,24,128]{2,1,0:T(8,128)S(1)} custom-call(f32[64,24,128]{2,1,0:T(8,128)S(1)} %copy-done.5, f32[64,24,128]{2,1,0:T(8,128)S(1)} %get-tuple-element.44.s_ref, bf16[1024,256]{1,0:T(8,128)(2,1)S(1)} %copy-done.31, bf16[1024,256]{1,0:T(8,128)(2,1)S(1)} %copy-done.33, f32[64,24,128]{2,1,0:T(8,128)S(1)} %get-tuple-element.46.x_ref.rest_0_, ...), custom_call_target="tpu_custom_call" | custom-call | flops 3000000000 | bytes 6291456 | tf_op jit(solution)/shard_map/wall/pallas_call | solution.py:248
  162.6 10.0 %collective-permute-done.11.t_ref = f32[64,24,128]{2,1,0:T(8,128)S(1)} collective-permute-done((f32[64,24,128]{2,1,0:T(8,128)S(1)}, f32[64,24,128]{2,1,0:T(8,128)S(1)}, u32[]{:S(2)}, u32[]{:S(2)}) %collective-permute-start.11) | collective-permute-done | bytes 786464 | tf_op jit(solution)/shard_map/ppermute | solution.py:25
  172.6 2.8 %finish.2 = (f32[192,2048]{1,0:T(8,128)}, f32[192,2048]{1,0:T(8,128)}) custom-call(s32[8,128]{1,0:T(8,128)S(1)} %broadcast_in_dim.6.off_ref, f32[64,24,128]{2,1,0:T(8,128)S(1)} %wall.5.g_ref, f32[64,24,128]{2,1,0:T(8,128)S(1)} %collective-permute-done.11.t_ref, f32[64,24,128]{2,1,0:T(8,128)S(1)} %get-tuple-element.46.x_ref.rest_0_, ...), custom_call_target="tpu_custom_call" | custom-call | flops 1000000000 | bytes 6291456 | tf_op jit(solution)/shard_map/finish/pallas_call | solution.py:395
  175.5 2.3 %finish.3 = (f32[192,2048]{1,0:T(8,128)}, f32[192,2048]{1,0:T(8,128)}) custom-call(s32[8,128]{1,0:T(8,128)S(1)} %broadcast_in_dim.6.off_ref, f32[64,24,128]{2,1,0:T(8,128)S(1)} %wall.5.g_ref, f32[64,24,128]{2,1,0:T(8,128)S(1)} %collective-permute-done.11.t_ref, ...), custom_call_target="tpu_custom_call", output_to_operand_aliasing={{0}: (11, {}), {1}: (12, {})} | custom-call | flops 1000000000 | bytes 6291456 | tf_op jit(solution)/shard_map/finish/pallas_call | solution.py:395
  (105 shorter events, 2.7 us)
Async XLA Ops:
  0.6 38.2 %collective-permute-start = (f32[192,2048]{1,0:T(8,128)}, f32[192,2048]{1,0:T(8,128)S(1)}, u32[]{:S(2)}, u32[]{:S(2)}) collective-permute-start(f32[192,2048]{1,0:T(8,128)} %x_ref.3), channel_id=1, source_target_pairs={{0,24},{4,12},{8,0},{12,20},{16,8},{20,28},{24,16},{28,4},{1,25},{... | collective-permute-start | bytes 4718600 | tf_op jit(solution)/shard_map/ppermute | solution.py:34
  2.6 2.3 %copy-start.36 = (s32[8,64]{1,0:T(8,128)S(1)}, s32[8,64]{1,0:T(8,128)}, u32[]{:S(2)}) copy-start(s32[8,64]{1,0:T(8,128)} %param.16) | copy-start | bytes 6148
  2.6 2.3 %copy-start.34 = (f32[8,192,64]{1,2,0:T(8,128)S(1)}, f32[8,192,64]{1,2,0:T(8,128)}, u32[]{:S(2)}) copy-start(f32[8,192,64]{1,2,0:T(8,128)} %param.14) | copy-start | bytes 1179652
  2.6 2.5 %copy-start.35 = (f32[192,64]{0,1:T(8,128)S(1)}, f32[192,64]{0,1:T(8,128)}, u32[]{:S(2)}) copy-start(f32[192,64]{0,1:T(8,128)} %param.13) | copy-start | bytes 147460
  4.4 20.6 %collective-permute-start.3 = (f32[64,24,128]{2,1,0:T(8,128)}, f32[64,24,128]{2,1,0:T(8,128)S(1)}, u32[]{:S(2)}, u32[]{:S(2)}) collective-permute-start(f32[64,24,128]{2,1,0:T(8,128)} %get-tuple-element.41.x_ref.rest_0_), channel_id=1, source_target_pairs={{0,2},{1,3},{2,0},{3,1},{4,6},{5,7},{6,4},{7,5},{8,10},{9,11},{10,... | collective-permute-start | bytes 2359304 | tf_op jit(solution)/shard_map/ppermute | solution.py:20
  5.3 34.4 %copy-start.37 = (s32[8]{0:T(128)S(1)}, s32[8]{0:T(128)}, u32[]{:S(2)}) copy-start(s32[8]{0:T(128)} %param.15) | copy-start | bytes 100
  5.4 34.4 %collective-permute-start.1 = (f32[2,512,128]{2,1,0:T(8,128)S(1)}, f32[2,512,128]{2,1,0:T(8,128)S(1)}, u32[]{:S(2)}, u32[]{:S(2)}) collective-permute-start(f32[2,512,128]{2,1,0:T(8,128)S(1)} %fusion), channel_id=1, source_target_pairs={{0,4},{4,0},{8,12},{12,8},{16,20},{20,16},{24,28},{28,24},{1,5},{5... | collective-permute-start | bytes 1572872 | tf_op jit(solution)/shard_map/ppermute | solution.py:25
  6.7 39.2 %collective-permute-start.15 = (f32[64,24,128]{2,1,0:T(8,128)S(1)}, f32[64,24,128]{2,1,0:T(8,128)}, u32[]{:S(2)}, u32[]{:S(2)}) collective-permute-start(f32[64,24,128]{2,1,0:T(8,128)S(1)} %get-tuple-element.52.x_ref.rest_0_), channel_id=1, source_target_pairs={{0,2},{1,3},{2,0},{3,1},{4,6},{5,7},{6,4},{7,5},{8,10},{9,11},{10,... | collective-permute-start | bytes 2359304 | tf_op jit(solution)/shard_map/ppermute | solution.py:20
  8.2 37.7 %collective-permute-start.2 = (f32[64,24,128]{2,1,0:T(8,128)}, f32[64,24,128]{2,1,0:T(8,128)S(1)}, u32[]{:S(2)}, u32[]{:S(2)}) collective-permute-start(f32[64,24,128]{2,1,0:T(8,128)} %get-tuple-element.41.x_ref.rest_0_), channel_id=1, source_target_pairs={{0,1},{1,0},{2,3},{3,2},{4,5},{5,4},{6,7},{7,6},{8,9},{9,8},{10,11... | collective-permute-start | bytes 2359304 | tf_op jit(solution)/shard_map/ppermute | solution.py:20
  25.0 18.2 %copy-start.10 = (f32[64,24,128]{2,1,0:T(8,128)}, f32[64,24,128]{2,1,0:T(8,128)S(1)}, u32[]{:S(2)}) copy-start(f32[64,24,128]{2,1,0:T(8,128)S(1)} %collective-permute-done.3.rest_2_) | copy-start | bytes 2359300
  25.0 26.2 %collective-permute-start.4 = (f32[64,24,128]{2,1,0:T(8,128)S(1)}, f32[64,24,128]{2,1,0:T(8,128)S(1)}, u32[]{:S(2)}, u32[]{:S(2)}) collective-permute-start(f32[64,24,128]{2,1,0:T(8,128)S(1)} %collective-permute-done.3.rest_2_), channel_id=1, source_target_pairs={{0,1},{1,0},{2,3},{3,2},{4,5},{5,4},{6,7},{7,6},{8,9},{9,8},{10,11... | collective-permute-start | bytes 2359304 | tf_op jit(solution)/shard_map/ppermute | solution.py:20
  39.8 7.5 %copy-start.20 = (f32[2,512,128]{2,1,0:T(8,128)}, f32[2,512,128]{2,1,0:T(8,128)S(1)}, u32[]{:S(2)}) copy-start(f32[2,512,128]{2,1,0:T(8,128)S(1)} %collective-permute-done.1.theirs_ref) | copy-start | bytes 1572868
  44.1 20.4 %collective-permute-start.5 = (f32[64,24,128]{2,1,0:T(8,128)S(1)}, f32[64,24,128]{2,1,0:T(8,128)S(1)}, u32[]{:S(2)}, u32[]{:S(2)}) collective-permute-start(f32[64,24,128]{2,1,0:T(8,128)S(1)} %get-tuple-element.38), channel_id=1, source_target_pairs={{0,4},{4,0},{8,12},{12,8},{16,20},{20,16},{24,28},{28,24},{1,5},{5... | collective-permute-start | bytes 2359304 | tf_op jit(solution)/shard_map/ppermute | solution.py:25
  44.1 29.3 %collective-permute-start.6 = (f32[64,24,128]{2,1,0:T(8,128)}, f32[64,24,128]{2,1,0:T(8,128)}, u32[]{:S(2)}, u32[]{:S(2)}) collective-permute-start(f32[64,24,128]{2,1,0:T(8,128)} %get-tuple-element.41.x_ref.rest_0_), channel_id=1, source_target_pairs={{0,8},{4,28},{8,16},{12,4},{16,24},{20,12},{24,0},{28,20},{1,9},{5... | collective-permute-start | bytes 2359304 | tf_op jit(solution)/shard_map/ppermute | solution.py:34
  45.9 32.4 %collective-permute-start.14 = (f32[64,24,128]{2,1,0:T(8,128)S(1)}, f32[64,24,128]{2,1,0:T(8,128)}, u32[]{:S(2)}, u32[]{:S(2)}) collective-permute-start(f32[64,24,128]{2,1,0:T(8,128)S(1)} %get-tuple-element.52.x_ref.rest_0_), channel_id=1, source_target_pairs={{0,1},{1,0},{2,3},{3,2},{4,5},{5,4},{6,7},{7,6},{8,9},{9,8},{10,11... | collective-permute-start | bytes 2359304 | tf_op jit(solution)/shard_map/ppermute | solution.py:20
  46.8 31.6 %collective-permute-start.16 = (f32[64,24,128]{2,1,0:T(8,128)}, f32[64,24,128]{2,1,0:T(8,128)}, u32[]{:S(2)}, u32[]{:S(2)}) collective-permute-start(f32[64,24,128]{2,1,0:T(8,128)} %collective-permute-done.15.rest_2_), channel_id=1, source_target_pairs={{0,1},{1,0},{2,3},{3,2},{4,5},{5,4},{6,7},{7,6},{8,9},{9,8},{10,11... | collective-permute-start | bytes 2359304 | tf_op jit(solution)/shard_map/ppermute | solution.py:20
  47.3 18.1 %copy-start.1 = (f32[192,2048]{1,0:T(8,128)S(1)}, f32[192,2048]{1,0:T(8,128)}, u32[]{:S(2)}) copy-start(f32[192,2048]{1,0:T(8,128)} %x_ref.2) | copy-start | bytes 4718596
  47.3 19.1 %copy-start.23 = (f32[192,192]{1,0:T(8,128)S(1)}, f32[192,192]{1,0:T(8,128)}, u32[]{:S(2)}) copy-start(f32[192,192]{1,0:T(8,128)} %inv_ref.1) | copy-start | bytes 442372
  52.1 29.8 %collective-permute-start.17 = (f32[64,24,128]{2,1,0:T(8,128)}, f32[64,24,128]{2,1,0:T(8,128)}, u32[]{:S(2)}, u32[]{:S(2)}) collective-permute-start(f32[64,24,128]{2,1,0:T(8,128)} %get-tuple-element.51), channel_id=1, source_target_pairs={{0,4},{4,0},{8,12},{12,8},{16,20},{20,16},{24,28},{28,24},{1,5},{5... | collective-permute-start | bytes 2359304 | tf_op jit(solution)/shard_map/ppermute | solution.py:25
  65.4 41.1 %collective-permute-start.18 = (f32[64,24,128]{2,1,0:T(8,128)S(1)}, f32[64,24,128]{2,1,0:T(8,128)}, u32[]{:S(2)}, u32[]{:S(2)}) collective-permute-start(f32[64,24,128]{2,1,0:T(8,128)S(1)} %get-tuple-element.52.x_ref.rest_0_), channel_id=1, source_target_pairs={{0,8},{4,28},{8,16},{12,4},{16,24},{20,12},{24,0},{28,20},{1,9},{5... | collective-permute-start | bytes 2359304 | tf_op jit(solution)/shard_map/ppermute | solution.py:34
  65.4 4.6 %copy-start.11 = (f32[64,24,128]{2,1,0:T(8,128)S(1)}, f32[64,24,128]{2,1,0:T(8,128)}, u32[]{:S(2)}) copy-start(f32[64,24,128]{2,1,0:T(8,128)} %copy-done.10) | copy-start | bytes 2359300
  65.4 4.6 %copy-start.15 = (f32[64,24,128]{2,1,0:T(8,128)S(1)}, f32[64,24,128]{2,1,0:T(8,128)}, u32[]{:S(2)}) copy-start(f32[64,24,128]{2,1,0:T(8,128)} %copy-done.14) | copy-start | bytes 2359300
  65.4 4.6 %copy-start.17 = (f32[64,24,128]{2,1,0:T(8,128)S(1)}, f32[64,24,128]{2,1,0:T(8,128)}, u32[]{:S(2)}) copy-start(f32[64,24,128]{2,1,0:T(8,128)} %copy-done.16) | copy-start | bytes 2359300
  66.4 7.1 %copy-start.4 = (f32[64,24,128]{2,1,0:T(8,128)}, f32[64,24,128]{2,1,0:T(8,128)S(1)}, u32[]{:S(2)}) copy-start(f32[64,24,128]{2,1,0:T(8,128)S(1)} %get-tuple-element.32.f_ref) | copy-start | bytes 2359300
  66.4 12.0 %copy-start.6 = (f32[64,24,128]{2,1,0:T(8,128)}, f32[64,24,128]{2,1,0:T(8,128)S(1)}, u32[]{:S(2)}) copy-start(f32[64,24,128]{2,1,0:T(8,128)S(1)} %get-tuple-element.47.f_ref) | copy-start | bytes 2359300
  66.4 1.5 copy-start.18
  70.0 8.4 %copy-start.30 = (bf16[1024,256]{1,0:T(8,128)(2,1)}, bf16[1024,256]{1,0:T(8,128)(2,1)S(1)}, u32[]{:S(2)}) copy-start(bf16[1024,256]{1,0:T(8,128)(2,1)S(1)} %get-tuple-element.36.mh_ref) | copy-start | bytes 1572868
  70.0 8.4 %copy-start.32 = (bf16[1024,256]{1,0:T(8,128)(2,1)}, bf16[1024,256]{1,0:T(8,128)(2,1)S(1)}, u32[]{:S(2)}) copy-start(bf16[1024,256]{1,0:T(8,128)(2,1)S(1)} %get-tuple-element.37.ml_ref) | copy-start | bytes 1572868
  70.1 3.4 %copy-start.3 = (f32[64,24,128]{2,1,0:T(8,128)S(1)}, f32[64,24,128]{2,1,0:T(8,128)}, u32[]{:S(2)}) copy-start(f32[64,24,128]{2,1,0:T(8,128)} %copy-done.2) | copy-start | bytes 2359300
  73.5 4.9 %copy-start.27 = (f32[64,24,128]{2,1,0:T(8,128)S(1)}, f32[64,24,128]{2,1,0:T(8,128)}, u32[]{:S(2)}) copy-start(f32[64,24,128]{2,1,0:T(8,128)} %copy-done.26) | copy-start | bytes 2359300
  76.3 35.6 %collective-permute-start.7 = (f32[64,24,128]{2,1,0:T(8,128)S(1)}, f32[64,24,128]{2,1,0:T(8,128)S(1)}, u32[]{:S(2)}, u32[]{:S(2)}) collective-permute-start(f32[64,24,128]{2,1,0:T(8,128)S(1)} %get-tuple-element.46.x_ref.rest_0_), channel_id=1, source_target_pairs={{0,24},{4,12},{8,0},{12,20},{16,8},{20,28},{24,16},{28,4},{1,25},{... | collective-permute-start | bytes 2359304 | tf_op jit(solution)/shard_map/ppermute | solution.py:34
  81.9 49.1 %copy-start.21 = (f32[2,512,128]{2,1,0:T(8,128)S(1)}, f32[2,512,128]{2,1,0:T(8,128)}, u32[]{:S(2)}) copy-start(f32[2,512,128]{2,1,0:T(8,128)} %copy-done.20) | copy-start | bytes 1572868
  109.9 20.6 %collective-permute-start.21 = (f32[64,24,128]{2,1,0:T(8,128)}, f32[64,24,128]{2,1,0:T(8,128)}, u32[]{:S(2)}, u32[]{:S(2)}) collective-permute-start(f32[64,24,128]{2,1,0:T(8,128)} %get-tuple-element.57.x_ref.rest_0_), channel_id=1, source_target_pairs={{0,2},{1,3},{2,0},{3,1},{4,6},{5,7},{6,4},{7,5},{8,10},{9,11},{10,... | collective-permute-start | bytes 2359304 | tf_op jit(solution)/shard_map/ppermute | solution.py:20
  110.4 20.6 %collective-permute-start.19 = (f32[64,24,128]{2,1,0:T(8,128)}, f32[64,24,128]{2,1,0:T(8,128)S(1)}, u32[]{:S(2)}, u32[]{:S(2)}) collective-permute-start(f32[64,24,128]{2,1,0:T(8,128)} %get-tuple-element.57.x_ref.rest_0_), channel_id=1, source_target_pairs={{0,24},{4,12},{8,0},{12,20},{16,8},{20,28},{24,16},{28,4},{1,25},{... | collective-permute-start | bytes 2359304 | tf_op jit(solution)/shard_map/ppermute | solution.py:34
  110.4 25.6 %collective-permute-start.20 = (f32[64,24,128]{2,1,0:T(8,128)}, f32[64,24,128]{2,1,0:T(8,128)S(1)}, u32[]{:S(2)}, u32[]{:S(2)}) collective-permute-start(f32[64,24,128]{2,1,0:T(8,128)} %get-tuple-element.57.x_ref.rest_0_), channel_id=1, source_target_pairs={{0,1},{1,0},{2,3},{3,2},{4,5},{5,4},{6,7},{7,6},{8,9},{9,8},{10,11... | collective-permute-start | bytes 2359304 | tf_op jit(solution)/shard_map/ppermute | solution.py:20
  110.4 28.5 %collective-permute-start.9 = (f32[64,24,128]{2,1,0:T(8,128)S(1)}, f32[64,24,128]{2,1,0:T(8,128)}, u32[]{:S(2)}, u32[]{:S(2)}) collective-permute-start(f32[64,24,128]{2,1,0:T(8,128)S(1)} %get-tuple-element.46.x_ref.rest_0_), channel_id=1, source_target_pairs={{0,2},{1,3},{2,0},{3,1},{4,6},{5,7},{6,4},{7,5},{8,10},{9,11},{10,... | collective-permute-start | bytes 2359304 | tf_op jit(solution)/shard_map/ppermute | solution.py:20
  112.8 30.4 %collective-permute-start.24 = (f32[64,24,128]{2,1,0:T(8,128)}, f32[64,24,128]{2,1,0:T(8,128)S(1)}, u32[]{:S(2)}, u32[]{:S(2)}) collective-permute-start(f32[64,24,128]{2,1,0:T(8,128)} %get-tuple-element.57.x_ref.rest_0_), channel_id=1, source_target_pairs={{0,8},{4,28},{8,16},{12,4},{16,24},{20,12},{24,0},{28,20},{1,9},{5... | collective-permute-start | bytes 2359304 | tf_op jit(solution)/shard_map/ppermute | solution.py:34
  130.5 13.5 %collective-permute-start.22 = (f32[64,24,128]{2,1,0:T(8,128)}, f32[64,24,128]{2,1,0:T(8,128)}, u32[]{:S(2)}, u32[]{:S(2)}) collective-permute-start(f32[64,24,128]{2,1,0:T(8,128)} %collective-permute-done.21.rest_2_), channel_id=1, source_target_pairs={{0,1},{1,0},{2,3},{3,2},{4,5},{5,4},{6,7},{7,6},{8,9},{9,8},{10,11... | collective-permute-start | bytes 2359304 | tf_op jit(solution)/shard_map/ppermute | solution.py:20
  136.1 20.6 %collective-permute-start.23 = (f32[64,24,128]{2,1,0:T(8,128)}, f32[64,24,128]{2,1,0:T(8,128)S(1)}, u32[]{:S(2)}, u32[]{:S(2)}) collective-permute-start(f32[64,24,128]{2,1,0:T(8,128)} %get-tuple-element.56), channel_id=1, source_target_pairs={{0,4},{4,0},{8,12},{12,8},{16,20},{20,16},{24,28},{28,24},{1,5},{5... | collective-permute-start | bytes 2359304 | tf_op jit(solution)/shard_map/ppermute | solution.py:25
  137.0 22.0 %collective-permute-start.8 = (f32[64,24,128]{2,1,0:T(8,128)S(1)}, f32[64,24,128]{2,1,0:T(8,128)}, u32[]{:S(2)}, u32[]{:S(2)}) collective-permute-start(f32[64,24,128]{2,1,0:T(8,128)S(1)} %get-tuple-element.46.x_ref.rest_0_), channel_id=1, source_target_pairs={{0,1},{1,0},{2,3},{3,2},{4,5},{5,4},{6,7},{7,6},{8,9},{9,8},{10,11... | collective-permute-start | bytes 2359304 | tf_op jit(solution)/shard_map/ppermute | solution.py:20
  138.9 20.1 %collective-permute-start.10 = (f32[64,24,128]{2,1,0:T(8,128)}, f32[64,24,128]{2,1,0:T(8,128)}, u32[]{:S(2)}, u32[]{:S(2)}) collective-permute-start(f32[64,24,128]{2,1,0:T(8,128)} %collective-permute-done.9.rest_2_), channel_id=1, source_target_pairs={{0,1},{1,0},{2,3},{3,2},{4,5},{5,4},{6,7},{7,6},{8,9},{9,8},{10,11... | collective-permute-start | bytes 2359304 | tf_op jit(solution)/shard_map/ppermute | solution.py:20
  141.1 3.1 %copy-start.25 = (f32[64,24,128]{2,1,0:T(8,128)S(1)}, f32[64,24,128]{2,1,0:T(8,128)}, u32[]{:S(2)}) copy-start(f32[64,24,128]{2,1,0:T(8,128)} %copy-done.24) | copy-start | bytes 2359300
  141.1 3.1 %copy-start.31 = (bf16[1024,256]{1,0:T(8,128)(2,1)S(1)}, bf16[1024,256]{1,0:T(8,128)(2,1)}, u32[]{:S(2)}) copy-start(bf16[1024,256]{1,0:T(8,128)(2,1)} %copy-done.30) | copy-start | bytes 1572868
  141.1 3.1 %copy-start.33 = (bf16[1024,256]{1,0:T(8,128)(2,1)S(1)}, bf16[1024,256]{1,0:T(8,128)(2,1)}, u32[]{:S(2)}) copy-start(bf16[1024,256]{1,0:T(8,128)(2,1)} %copy-done.32) | copy-start | bytes 1572868
  143.2 29.4 %collective-permute-start.11 = (f32[64,24,128]{2,1,0:T(8,128)S(1)}, f32[64,24,128]{2,1,0:T(8,128)S(1)}, u32[]{:S(2)}, u32[]{:S(2)}) collective-permute-start(f32[64,24,128]{2,1,0:T(8,128)S(1)} %get-tuple-element.45), channel_id=1, source_target_pairs={{0,4},{4,0},{8,12},{12,8},{16,20},{20,16},{24,28},{28,24},{1,5},{5... | collective-permute-start | bytes 2359304 | tf_op jit(solution)/shard_map/ppermute | solution.py:25
  144.0 18.6 %collective-permute-start.12 = (f32[40,24,128]{2,1,0:T(8,128)S(1)}, f32[40,24,128]{2,1,0:T(8,128)S(1)}, u32[]{:S(2)}, u32[]{:S(2)}) collective-permute-start(f32[40,24,128]{2,1,0:T(8,128)S(1)} %constant_dynamic-slice_fusion.1), channel_id=1, source_target_pairs={{0,8},{4,28},{8,16},{12,4},{16,24},{20,12},{24,0},{28,20},{1,9},{5... | collective-permute-start | bytes 1474568 | tf_op jit(solution)/shard_map/ppermute | solution.py:34
  148.1 10.9 %copy-start.5 = (f32[64,24,128]{2,1,0:T(8,128)S(1)}, f32[64,24,128]{2,1,0:T(8,128)}, u32[]{:S(2)}) copy-start(f32[64,24,128]{2,1,0:T(8,128)} %copy-done.4) | copy-start | bytes 2359300
  156.7 18.7 %collective-permute-start.13 = (f32[24,24,128]{2,1,0:T(8,128)S(1)}, f32[24,24,128]{2,1,0:T(8,128)S(1)}, u32[]{:S(2)}, u32[]{:S(2)}) collective-permute-start(f32[24,24,128]{2,1,0:T(8,128)S(1)} %constant_dynamic-slice_fusion), channel_id=1, source_target_pairs={{0,8},{4,28},{8,16},{12,4},{16,24},{20,12},{24,0},{28,20},{1,9},{5... | collective-permute-start | bytes 884744 | tf_op jit(solution)/shard_map/ppermute | solution.py:34
  (15 other events, 15.5 us)

commit v2 on v1

--- a/solution.py
+++ b/solution.py
@@ -124,21 +124,32 @@
 UNROLL = 4
 
 
-def fill(ext_ref, pieces, points):
+def fill(ext_ref, pieces):
     def step(i, _):
-        for slot in range(ext_ref.shape[0] // points):
-            here = pl.ds(slot * points + i * UNROLL, UNROLL)
-            ext_ref[here] = jnp.zeros((UNROLL, *ext_ref.shape[1:]), jnp.float32)
+        here = pl.ds(i * 2 * UNROLL, 2 * UNROLL)
+        ext_ref[here] = jnp.zeros((2 * UNROLL, *ext_ref.shape[1:]), jnp.float32)
         return 0
 
-    lax.fori_loop(0, points // UNROLL, step, 0)
-
-    def copy(i, _):
-        for ref, slot in pieces:
-            ext_ref[pl.ds(slot * points + i * UNROLL, UNROLL)] = ref[pl.ds(i * UNROLL, UNROLL)]
-        return 0
-
-    lax.fori_loop(0, points // UNROLL, copy, 0)
+    lax.fori_loop(0, ext_ref.shape[0] // (2 * UNROLL), step, 0, unroll=2)
+    place(ext_ref, pieces)
+
+
+def place(ext_ref, pieces):
+    for ref, at in pieces:
+
+        def copy(i, _, ref=ref, at=at):
+            ext_ref[pl.ds(at + i * UNROLL, UNROLL)] = ref[pl.ds(i * UNROLL, UNROLL)]
+            return 0
+
+        lax.fori_loop(0, ref.shape[0] // UNROLL, copy, 0)
+
+
+def in_order(refs, at):
+    out = []
+    for ref in refs:
+        out.append((ref, at))
+        at = at + ref.shape[0]
+    return out
 
 
 def scaled(w_ref, row, value, cw):
@@ -147,13 +158,14 @@
     return top, low
 
 
-def near_kernel(bands, off_ref, x_ref, far_ref, w_ref, theirs_ref, partial_ref, sum_ref, ext_ref):
+def near_kernel(bands, off_ref, x_ref, w_ref, theirs_ref, *rest):
+    *fars, partial_ref, sum_ref, ext_ref = rest
     points, rows, _ = x_ref.shape
     cw = rows * 2 // 3
     sign = own_sign()
     offsets = read(off_ref)
     own = jnp.where(sign > 0, REACH, REACH + 1)
-    fill(ext_ref, [(x_ref, own), (far_ref, own + 2 * sign)], points)
+    fill(ext_ref, [(x_ref, own * points), *in_order(fars, (own + 2 * sign) * points)])
 
     for out_ref, weights, shift in ((partial_ref, theirs_ref, sign), (sum_ref, w_ref, 0)):
         starts = [(own + shift) * points + offsets[b] for b in range(bands)]
@@ -182,13 +194,13 @@
     return pl.pallas_call(
         functools.partial(near_kernel, bands),
         out_shape=(out, out),
-        in_specs=[VMEM] * 5,
+        in_specs=[VMEM] * (4 + len(first)),
         out_specs=(VMEM, VMEM),
         scratch_shapes=[pltpu.VMEM(((2 * REACH + 2) * points, rows, LANES), jnp.float32)],
         compiler_params=params(),
         cost_estimate=pl.CostEstimate(flops=1000000000, bytes_accessed=6 * x.size * 4, transcendentals=0),
         name="near",
-    )(offsets, x, first, w, theirs)
+    )(offsets, x, w, theirs, *first)
 
 
 def halves(value):
@@ -299,8 +311,13 @@
     x_new_ref[:, cw:, :] = x_ref[here, cw:, :] + low
 
 
-def last_kernel(off_ref, g_ref, t_ref, x_ref, w_ref, bh_ref, bl_ref, far_ref, x_new_ref, r_ref, high_ref, low_ref):
+def last_kernel(off_ref, g_ref, t_ref, x_ref, w_ref, bh_ref, bl_ref, *rest):
+    *fars, x_new_ref, r_ref, high_ref, low_ref, far_ref = rest
     points = x_ref.shape[0]
+    if len(fars) > 1:
+        place(far_ref, in_order(fars, 0))
+    else:
+        far_ref = fars[0]
 
     def begin(i, _):
         here = pl.ds(i * UNROLL, UNROLL)
@@ -319,13 +336,14 @@
     return pl.pallas_call(
         last_kernel,
         out_shape=(out, out),
-        in_specs=[VMEM] * 8,
+        in_specs=[VMEM] * (7 + len(second)),
         out_specs=(VMEM, VMEM),
-        scratch_shapes=[pltpu.VMEM((m_rows, 2 * LANES), jnp.bfloat16)] * 2,
+        scratch_shapes=[pltpu.VMEM((m_rows, 2 * LANES), jnp.bfloat16)] * 2
+        + [pltpu.VMEM(x.shape if len(second) > 1 else (1, 8, LANES), jnp.float32)],
         compiler_params=params(),
         cost_estimate=pl.CostEstimate(flops=1000000000, bytes_accessed=8 * x.size * 4, transcendentals=0),
         name="last",
-    )(offsets, g, t, x, w, bh, bl, second)
+    )(offsets, g, t, x, w, bh, bl, *second)
 
 
 def piece_start(sizes, i, points):
@@ -343,14 +361,7 @@
     points = x_ref.shape[0]
     n = sizes[i]
     lo = piece_start(sizes, i, points)
-    for m, ref in enumerate(fars):
-        at = piece_start(sizes, m, points)
-
-        def copy(j, _):
-            far_ref[pl.ds(at + j * UNROLL, UNROLL)] = ref[pl.ds(j * UNROLL, UNROLL)]
-            return 0
-
-        lax.fori_loop(0, sizes[m] // UNROLL, copy, 0)
+    place(far_ref, [(ref, piece_start(sizes, m, points)) for m, ref in enumerate(fars)])
 
     def begin(j, _):
         here = pl.ds(lo + j * UNROLL, UNROLL)
@@ -496,6 +507,7 @@
     mh, ml, bh, bl = prep(wall_even, wall_odd, block_inv)
     f = split(forcing, chunks, points)
     sizes = (points * 5 // 8, points * 3 // 8)
+    main = points - points // 8
     arrived = raw_first
     order = [0]
     bit = n_wall // 2
@@ -504,20 +516,24 @@
         bit //= 2
     for sweep in range(SWEEPS):
         final_sweep = sweep == SWEEPS - 1
+
+        def move(k, first, arrived):
+            value = after(state[k], arrived)
+            if k < chunks - 1:
+                parts = [value]
+            elif final_sweep and not first:
+                parts = [lax.dynamic_slice_in_dim(value, piece_start(sizes, i, points), n, 0) for i, n in enumerate(sizes)]
+            else:
+                parts = [value[:main], value[main:]]
+            return [far(v, first) for v in parts]
+
         if sweep:
-            firsts = [far(after(state[k], arrived), True) for k in range(chunks)]
-            arrived = firsts[-1]
+            firsts = [move(k, True, arrived) for k in range(chunks)]
+            arrived = firsts[-1][0]
         else:
-            firsts = split(raw_first, chunks, points)
-        seconds = []
-        for k in range(chunks):
-            value = after(state[k], arrived)
-            if final_sweep and k == chunks - 1:
-                parts = [lax.dynamic_slice_in_dim(value, piece_start(sizes, i, points), n, 0) for i, n in enumerate(sizes)]
-                seconds.append([far(v, False) for v in parts])
-            else:
-                seconds.append(far(value, False))
-        arrived = seconds[-1]
+            firsts = [[v] for v in split(raw_first, chunks, points)]
+        seconds = [move(k, False, arrived) for k in range(chunks)]
+        arrived = seconds[-1][0]
         walls = []
         for k in range(chunks):
             got = [state[k]]

time: 179 us -> 179 us (level)
  the two profiles are of different devices: /device:TPU:28 before, /device:TPU:8 now
where the time goes in v2:
time: 179 us; the launch traced here: 178 us
  waiting for transfers between devices  77.4 us (43%)
  starting transfers between devices  45.9 us (26%)
  Pallas kernels  39.8 us (22%)
  local copies, waits for them, and re-layouts  13.5 us (8%)
    ppermute x10, waiting for transfers between devices, far(): return lax.ppermute(value, 'span', pairs)  42.2 us
    ppermute x10, starting transfers between devices, far(): return lax.ppermute(value, 'span', pairs)  32 us
    ppermute x5, waiting for transfers between devices, partner(): return lax.ppermute(value, 'span', [(i, i ^ 1) for i in range(count)])  20.4 us
    ppermute x12, waiting for transfers between devices, exchange(): return lax.ppermute(value, 'wall', [(i, i ^ bit) for i in range(count)])  14.9 us
    unnamed x80, local copies, waits for them, and re-layouts  13.3 us
    pallas_call x4, Pallas kernels, wall(): pl.pallas_call(functools.partial(wall_kernel, n_blocks), out_shape=jax.Sh...  12.3 us
    pallas_call x4, Pallas kernels, near(): pl.pallas_call(functools.partial(near_kernel, bands), out_shape=(out, out...  11.4 us
    ppermute x5, starting transfers between devices, partner(): return lax.ppermute(value, 'span', [(i, i ^ 1) for i in range(count)])  8.61 us
  transfers between devices with their start and end apart: 27, of which 9 were waited for; matrix products, arithmetic and copies ran while one was open for 0% of the time, Pallas kernels for 21%

profile of v2, /device:TPU:8, one launch (start us, length us, event | category | flops | bytes accessed | tf_op | source)
XLA Modules:
  0.0 178.2 jit_solution(9204039850279743281)
XLA Ops:
  0.7 1.4 copy-done
  2.1 0.9 split.4
  3.1 2.0 %collective-permute-start.3 = (f32[64,24,128]{2,1,0:T(8,128)S(1)}, f32[64,24,128]{2,1,0:T(8,128)S(1)}, u32[]{:S(2)}, u32[]{:S(2)}) collective-permute-start(f32[64,24,128]{2,1,0:T(8,128)S(1)} %get-tuple-element.41.x_ref.rest_0_), channel_id=1, source_target_pairs={{0,2},{1,3},{2,0},{3,1},{4,6},{5,7},{6,4},{7,5},{8,10},{9,11},{10,... | collective-permute-start | bytes 2359304 | tf_op jit(solution)/shard_map/ppermute | solution.py:20
  5.7 3.0 %collective-permute-start = (f32[2,512,128]{2,1,0:T(8,128)S(1)}, f32[2,512,128]{2,1,0:T(8,128)S(1)}, u32[]{:S(2)}, u32[]{:S(2)}) collective-permute-start(f32[2,512,128]{2,1,0:T(8,128)S(1)} %fusion), channel_id=1, source_target_pairs={{0,4},{4,0},{8,12},{12,8},{16,20},{20,16},{24,28},{28,24},{1,5},{5... | collective-permute-start | bytes 1572872 | tf_op jit(solution)/shard_map/ppermute | solution.py:25
  8.7 14.8 %collective-permute-done.3.rest_2_ = f32[64,24,128]{2,1,0:T(8,128)S(1)} collective-permute-done((f32[64,24,128]{2,1,0:T(8,128)S(1)}, f32[64,24,128]{2,1,0:T(8,128)S(1)}, u32[]{:S(2)}, u32[]{:S(2)}) %collective-permute-start.3) | collective-permute-done | bytes 786464 | tf_op jit(solution)/shard_map/ppermute | solution.py:20
  23.6 13.5 %collective-permute-done.1.x_ref = f32[192,2048]{1,0:T(8,128)S(1)} collective-permute-done((f32[192,2048]{1,0:T(8,128)}, f32[192,2048]{1,0:T(8,128)S(1)}, u32[]{:S(2)}, u32[]{:S(2)}) %collective-permute-start.1) | collective-permute-done | bytes 1572896 | tf_op jit(solution)/shard_map/ppermute | solution.py:34
  37.1 1.6 collective-permute-start.6
  38.8 0.9 split.5
  39.8 3.1 %near.4 = (f32[64,24,128]{2,1,0:T(8,128)}, f32[64,24,128]{2,1,0:T(8,128)S(1)}) custom-call(s32[8,128]{1,0:T(8,128)S(1)} %broadcast_in_dim.6.off_ref, f32[64,24,128]{2,1,0:T(8,128)S(1)} %get-tuple-element.41.x_ref.rest_0_, f32[2,576,128]{2,1,0:T(8,128)S(1)} %pad_maximum_fusion.w_ref, f32[2,512,128]{2,1,0:T(8,128)S(1)} %collective-permute-done.theirs_ref, ...), custom_call_target="tpu_custom_call" | custom-call | flops 1000000000 | bytes 4718592 | tf_op jit(solution)/shard_map/near/pallas_call | solution.py:194
  42.9 2.2 %collective-permute-start.5 = (f32[64,24,128]{2,1,0:T(8,128)}, f32[64,24,128]{2,1,0:T(8,128)S(1)}, u32[]{:S(2)}, u32[]{:S(2)}) collective-permute-start(f32[64,24,128]{2,1,0:T(8,128)} %get-tuple-element.38), channel_id=1, source_target_pairs={{0,4},{4,0},{8,12},{12,8},{16,20},{20,16},{24,28},{28,24},{1,5},{5... | collective-permute-start | bytes 2359304 | tf_op jit(solution)/shard_map/ppermute | solution.py:25
  45.7 1.5 collective-permute-start.7
  47.2 3.1 %near.6 = (f32[64,24,128]{2,1,0:T(8,128)}, f32[64,24,128]{2,1,0:T(8,128)S(1)}) custom-call(s32[8,128]{1,0:T(8,128)S(1)} %broadcast_in_dim.6.off_ref, f32[64,24,128]{2,1,0:T(8,128)S(1)} %get-tuple-element.52.x_ref.rest_0_, f32[2,576,128]{2,1,0:T(8,128)S(1)} %pad_maximum_fusion.w_ref, f32[2,512,128]{2,1,0:T(8,128)S(1)} %collective-permute-done.theirs_ref, ...), custom_call_target="tpu_custom_call" | custom-call | flops 1000000000 | bytes 4718592 | tf_op jit(solution)/shard_map/near/pallas_call | solution.py:194
  51.2 4.8 %collective-permute-done.7.rest_1_ = f32[8,24,128]{2,1,0:T(8,128)S(1)} collective-permute-done((f32[8,24,128]{2,1,0:T(8,128)S(1)}, f32[8,24,128]{2,1,0:T(8,128)S(1)}, u32[]{:S(2)}, u32[]{:S(2)}) %collective-permute-start.7) | collective-permute-done | bytes 98336 | tf_op jit(solution)/shard_map/ppermute | solution.py:34
  55.9 1.3 collective-permute-start.19
  58.0 1.6 collective-permute-start.20
  59.6 1.4 copy-done.1
  61.0 0.9 split.3
  62.0 1.5 copy-done.20
  63.5 1.1 copy-done.21
  64.6 1.0 prep.1
  65.7 1.9 %wall.4.g_ref = f32[64,24,128]{2,1,0:T(8,128)S(1)} custom-call(f32[64,24,128]{2,1,0:T(8,128)S(1)} %get-tuple-element.32.f_ref, f32[64,24,128]{2,1,0:T(8,128)S(1)} %copy-done.31, bf16[1024,256]{1,0:T(8,128)(2,1)S(1)} %get-tuple-element.36.mh_ref, bf16[1024,256]{1,0:T(8,128)(2,1)S(1)} %get-tuple-element.37.ml_ref, ...), custom_call_target="tpu_custom_call" | custom-call | flops 3000000000 | bytes 6291456 | tf_op jit(solution)/shard_map/wall/pallas_call | solution.py:260
  68.6 1.1 copy-done.3
  69.7 2.1 %last.3 = (f32[64,24,128]{2,1,0:T(8,128)S(1)}, f32[64,24,128]{2,1,0:T(8,128)}) custom-call(s32[8,128]{1,0:T(8,128)S(1)} %broadcast_in_dim.6.off_ref, f32[64,24,128]{2,1,0:T(8,128)S(1)} %wall.4.g_ref, f32[64,24,128]{2,1,0:T(8,128)S(1)} %copy-done.3, f32[64,24,128]{2,1,0:T(8,128)S(1)} %get-tuple-element.41.x_ref.rest_0_, ...), custom_call_target="tpu_custom_call" | custom-call | flops 1000000000 | bytes 6291456 | tf_op jit(solution)/shard_map/last/pallas_call | solution.py:336
  71.8 1.0 collective-permute-start.8
  72.8 3.5 %wall.6.g_ref = f32[64,24,128]{2,1,0:T(8,128)S(1)} custom-call(f32[64,24,128]{2,1,0:T(8,128)S(1)} %get-tuple-element.47.f_ref, f32[64,24,128]{2,1,0:T(8,128)S(1)} %copy-done.29, bf16[1024,256]{1,0:T(8,128)(2,1)S(1)} %get-tuple-element.36.mh_ref, bf16[1024,256]{1,0:T(8,128)(2,1)S(1)} %get-tuple-element.37.ml_ref, ...), custom_call_target="tpu_custom_call" | custom-call | flops 3000000000 | bytes 6291456 | tf_op jit(solution)/shard_map/wall/pallas_call | solution.py:260
  76.4 2.4 %collective-permute-done.19.t_ref = f32[64,24,128]{2,1,0:T(8,128)} collective-permute-done((f32[64,24,128]{2,1,0:T(8,128)}, f32[64,24,128]{2,1,0:T(8,128)}, u32[]{:S(2)}, u32[]{:S(2)}) %collective-permute-start.19) | collective-permute-done | bytes 786464 | tf_op jit(solution)/shard_map/ppermute | solution.py:25
  78.8 2.7 %last.4 = (f32[64,24,128]{2,1,0:T(8,128)S(1)}, f32[64,24,128]{2,1,0:T(8,128)}) custom-call(s32[8,128]{1,0:T(8,128)S(1)} %broadcast_in_dim.6.off_ref, f32[64,24,128]{2,1,0:T(8,128)S(1)} %wall.6.g_ref, f32[64,24,128]{2,1,0:T(8,128)} %collective-permute-done.19.t_ref, f32[64,24,128]{2,1,0:T(8,128)S(1)} %get-tuple-element.52.x_ref.rest_0_, ...), custom_call_target="tpu_custom_call" | custom-call | flops 1000000000 | bytes 6291456 | tf_op jit(solution)/shard_map/last/pallas_call | solution.py:336
  81.5 1.5 collective-permute-start.23
  83.0 4.2 %collective-permute-start.21 = (f32[64,24,128]{2,1,0:T(8,128)S(1)}, f32[64,24,128]{2,1,0:T(8,128)S(1)}, u32[]{:S(2)}, u32[]{:S(2)}) collective-permute-start(f32[64,24,128]{2,1,0:T(8,128)S(1)} %get-tuple-element.57.x_ref.rest_0_), channel_id=1, source_target_pairs={{0,24},{4,12},{8,0},{12,20},{16,8},{20,28},{24,16},{28,4},{1,25},{... | collective-permute-start | bytes 2359304 | tf_op jit(solution)/shard_map/ppermute | solution.py:34
  87.7 6.1 %collective-permute-done.8.rest_0_ = f32[56,24,128]{2,1,0:T(8,128)S(1)} collective-permute-done((f32[56,24,128]{2,1,0:T(8,128)S(1)}, f32[56,24,128]{2,1,0:T(8,128)S(1)}, u32[]{:S(2)}, u32[]{:S(2)}) %collective-permute-start.8) | collective-permute-done | bytes 688160 | tf_op jit(solution)/shard_map/ppermute | solution.py:34
  93.8 12.1 %collective-permute-start.26 = (f32[64,24,128]{2,1,0:T(8,128)S(1)}, f32[64,24,128]{2,1,0:T(8,128)S(1)}, u32[]{:S(2)}, u32[]{:S(2)}) collective-permute-start(f32[64,24,128]{2,1,0:T(8,128)S(1)} %get-tuple-element.57.x_ref.rest_0_), channel_id=1, source_target_pairs={{0,8},{4,28},{8,16},{12,4},{16,24},{20,12},{24,0},{28,20},{1,9},{5... | collective-permute-start | bytes 2359304 | tf_op jit(solution)/shard_map/ppermute | solution.py:34
  105.9 12.2 %collective-permute-done.21.rest_0_ = f32[64,24,128]{2,1,0:T(8,128)S(1)} collective-permute-done((f32[64,24,128]{2,1,0:T(8,128)S(1)}, f32[64,24,128]{2,1,0:T(8,128)S(1)}, u32[]{:S(2)}, u32[]{:S(2)}) %collective-permute-start.21) | collective-permute-done | bytes 786464 | tf_op jit(solution)/shard_map/ppermute | solution.py:34
  118.1 8.6 %collective-permute-start.9 = (f32[8,24,128]{2,1,0:T(8,128)S(1)}, f32[8,24,128]{2,1,0:T(8,128)S(1)}, u32[]{:S(2)}, u32[]{:S(2)}) collective-permute-start(f32[8,24,128]{2,1,0:T(8,128)S(1)} %slice.27), channel_id=1, source_target_pairs={{0,24},{4,12},{8,0},{12,20},{16,8},{20,28},{24,16},{28,4},{1,25},{... | collective-permute-start | bytes 294920 | tf_op jit(solution)/shard_map/ppermute | solution.py:34
  126.7 3.1 %near.7 = (f32[64,24,128]{2,1,0:T(8,128)}, f32[64,24,128]{2,1,0:T(8,128)S(1)}) custom-call(s32[8,128]{1,0:T(8,128)S(1)} %broadcast_in_dim.6.off_ref, f32[64,24,128]{2,1,0:T(8,128)S(1)} %get-tuple-element.57.x_ref.rest_0_, f32[2,576,128]{2,1,0:T(8,128)S(1)} %pad_maximum_fusion.w_ref, f32[2,512,128]{2,1,0:T(8,128)S(1)} %copy-done.23, ...), custom_call_target="tpu_custom_call" | custom-call | flops 1000000000 | bytes 4718592 | tf_op jit(solution)/shard_map/near/pallas_call | solution.py:194
  129.8 0.9 copy-done.26
  130.7 5.6 %collective-permute-done.9.rest_1_ = f32[8,24,128]{2,1,0:T(8,128)S(1)} collective-permute-done((f32[8,24,128]{2,1,0:T(8,128)S(1)}, f32[8,24,128]{2,1,0:T(8,128)S(1)}, u32[]{:S(2)}, u32[]{:S(2)}) %collective-permute-start.9) | collective-permute-done | bytes 98336 | tf_op jit(solution)/shard_map/ppermute | solution.py:34
  136.3 0.9 copy-done.14
  137.7 1.1 copy-done.19
  138.8 1.0 copy-done.24
  139.8 2.2 %near.5 = (f32[64,24,128]{2,1,0:T(8,128)S(1)}, f32[64,24,128]{2,1,0:T(8,128)S(1)}) custom-call(s32[8,128]{1,0:T(8,128)S(1)} %broadcast_in_dim.6.off_ref, f32[64,24,128]{2,1,0:T(8,128)S(1)} %get-tuple-element.46.x_ref.rest_0_, f32[2,576,128]{2,1,0:T(8,128)S(1)} %pad_maximum_fusion.w_ref, f32[2,512,128]{2,1,0:T(8,128)S(1)} %copy-done.24, ...), custom_call_target="tpu_custom_call" | custom-call | flops 1000000000 | bytes 4718592 | tf_op jit(solution)/shard_map/near/pallas_call | solution.py:194
  142.1 2.1 %collective-permute-start.13 = (f32[64,24,128]{2,1,0:T(8,128)S(1)}, f32[64,24,128]{2,1,0:T(8,128)S(1)}, u32[]{:S(2)}, u32[]{:S(2)}) collective-permute-start(f32[64,24,128]{2,1,0:T(8,128)S(1)} %get-tuple-element.45), channel_id=1, source_target_pairs={{0,4},{4,0},{8,12},{12,8},{16,20},{20,16},{24,28},{28,24},{1,5},{5... | collective-permute-start | bytes 2359304 | tf_op jit(solution)/shard_map/ppermute | solution.py:25
  145.1 3.3 %wall.7.g_ref = f32[64,24,128]{2,1,0:T(8,128)S(1)} custom-call(f32[64,24,128]{2,1,0:T(8,128)S(1)} %copy-done.9, f32[64,24,128]{2,1,0:T(8,128)S(1)} %copy-done.27, bf16[1024,256]{1,0:T(8,128)(2,1)S(1)} %copy-done.33, bf16[1024,256]{1,0:T(8,128)(2,1)S(1)} %copy-done.35, f32[64,24,128]{2,1,0:T(8,128)S(1)} %get-tuple-element.57.x_ref.rest_0_, ...), custom_call_target="tpu_custom_call" | custom-call | flops 3000000000 | bytes 6291456 | tf_op jit(solution)/shard_map/wall/pallas_call | solution.py:260
  148.4 8.6 %collective-permute-done.25.t_ref = f32[64,24,128]{2,1,0:T(8,128)} collective-permute-done((f32[64,24,128]{2,1,0:T(8,128)}, f32[64,24,128]{2,1,0:T(8,128)}, u32[]{:S(2)}, u32[]{:S(2)}) %collective-permute-start.25) | collective-permute-done | bytes 786464 | tf_op jit(solution)/shard_map/ppermute | solution.py:25
  157.6 2.3 %last.5 = (f32[64,24,128]{2,1,0:T(8,128)S(1)}, f32[64,24,128]{2,1,0:T(8,128)S(1)}) custom-call(s32[8,128]{1,0:T(8,128)S(1)} %broadcast_in_dim.6.off_ref, f32[64,24,128]{2,1,0:T(8,128)S(1)} %wall.7.g_ref, f32[64,24,128]{2,1,0:T(8,128)} %collective-permute-done.25.t_ref, f32[64,24,128]{2,1,0:T(8,128)S(1)} %get-tuple-element.57.x_ref.rest_0_, ...), custom_call_target="tpu_custom_call" | custom-call | flops 1000000000 | bytes 6291456 | tf_op jit(solution)/shard_map/last/pallas_call | solution.py:336
  159.9 3.5 %wall.5.g_ref = f32[64,24,128]{2,1,0:T(8,128)S(1)} custom-call(f32[64,24,128]{2,1,0:T(8,128)S(1)} %copy-done.7, f32[64,24,128]{2,1,0:T(8,128)S(1)} %get-tuple-element.44.s_ref, bf16[1024,256]{1,0:T(8,128)(2,1)S(1)} %copy-done.33, bf16[1024,256]{1,0:T(8,128)(2,1)S(1)} %copy-done.35, f32[64,24,128]{2,1,0:T(8,128)S(1)} %get-tuple-element.46.x_ref.rest_0_, ...), custom_call_target="tpu_custom_call" | custom-call | flops 3000000000 | bytes 6291456 | tf_op jit(solution)/shard_map/wall/pallas_call | solution.py:260
  163.5 9.4 %collective-permute-done.13.t_ref = f32[64,24,128]{2,1,0:T(8,128)S(1)} collective-permute-done((f32[64,24,128]{2,1,0:T(8,128)S(1)}, f32[64,24,128]{2,1,0:T(8,128)S(1)}, u32[]{:S(2)}, u32[]{:S(2)}) %collective-permute-start.13) | collective-permute-done | bytes 786464 | tf_op jit(solution)/shard_map/ppermute | solution.py:25
  172.9 2.8 %finish.2 = (f32[192,2048]{1,0:T(8,128)}, f32[192,2048]{1,0:T(8,128)}) custom-call(s32[8,128]{1,0:T(8,128)S(1)} %broadcast_in_dim.6.off_ref, f32[64,24,128]{2,1,0:T(8,128)S(1)} %wall.5.g_ref, f32[64,24,128]{2,1,0:T(8,128)S(1)} %collective-permute-done.13.t_ref, f32[64,24,128]{2,1,0:T(8,128)S(1)} %get-tuple-element.46.x_ref.rest_0_, ...), custom_call_target="tpu_custom_call" | custom-call | flops 1000000000 | bytes 6291456 | tf_op jit(solution)/shard_map/finish/pallas_call | solution.py:406
  175.7 2.3 %finish.3 = (f32[192,2048]{1,0:T(8,128)}, f32[192,2048]{1,0:T(8,128)}) custom-call(s32[8,128]{1,0:T(8,128)S(1)} %broadcast_in_dim.6.off_ref, f32[64,24,128]{2,1,0:T(8,128)S(1)} %wall.5.g_ref, f32[64,24,128]{2,1,0:T(8,128)S(1)} %collective-permute-done.13.t_ref, ...), custom_call_target="tpu_custom_call", output_to_operand_aliasing={{0}: (11, {}), {1}: (12, {})} | custom-call | flops 1000000000 | bytes 6291456 | tf_op jit(solution)/shard_map/finish/pallas_call | solution.py:406
  (117 shorter events, 6.7 us)
Async XLA Ops:
  0.6 36.4 %collective-permute-start.1 = (f32[192,2048]{1,0:T(8,128)}, f32[192,2048]{1,0:T(8,128)S(1)}, u32[]{:S(2)}, u32[]{:S(2)}) collective-permute-start(f32[192,2048]{1,0:T(8,128)} %x_ref.3), channel_id=1, source_target_pairs={{0,24},{4,12},{8,0},{12,20},{16,8},{20,28},{24,16},{28,4},{1,25},{... | collective-permute-start | bytes 4718600 | tf_op jit(solution)/shard_map/ppermute | solution.py:34
  2.1 3.1 %copy-start.36 = (f32[8,192,64]{1,2,0:T(8,128)S(1)}, f32[8,192,64]{1,2,0:T(8,128)}, u32[]{:S(2)}) copy-start(f32[8,192,64]{1,2,0:T(8,128)} %param.14) | copy-start | bytes 1179652
  2.1 3.3 %copy-start.37 = (f32[192,64]{0,1:T(8,128)S(1)}, f32[192,64]{0,1:T(8,128)}, u32[]{:S(2)}) copy-start(f32[192,64]{0,1:T(8,128)} %param.13) | copy-start | bytes 147460
  3.1 20.5 %collective-permute-start.3 = (f32[64,24,128]{2,1,0:T(8,128)S(1)}, f32[64,24,128]{2,1,0:T(8,128)S(1)}, u32[]{:S(2)}, u32[]{:S(2)}) collective-permute-start(f32[64,24,128]{2,1,0:T(8,128)S(1)} %get-tuple-element.41.x_ref.rest_0_), channel_id=1, source_target_pairs={{0,2},{1,3},{2,0},{3,1},{4,6},{5,7},{6,4},{7,5},{8,10},{9,11},{10,... | collective-permute-start | bytes 2359304 | tf_op jit(solution)/shard_map/ppermute | solution.py:20
  5.1 40.0 %collective-permute-start.2 = (f32[64,24,128]{2,1,0:T(8,128)S(1)}, f32[64,24,128]{2,1,0:T(8,128)S(1)}, u32[]{:S(2)}, u32[]{:S(2)}) collective-permute-start(f32[64,24,128]{2,1,0:T(8,128)S(1)} %get-tuple-element.41.x_ref.rest_0_), channel_id=1, source_target_pairs={{0,1},{1,0},{2,3},{3,2},{4,5},{5,4},{6,7},{7,6},{8,9},{9,8},{10,11... | collective-permute-start | bytes 2359304 | tf_op jit(solution)/shard_map/ppermute | solution.py:20
  5.1 40.0 %collective-permute-start.17 = (f32[64,24,128]{2,1,0:T(8,128)S(1)}, f32[64,24,128]{2,1,0:T(8,128)}, u32[]{:S(2)}, u32[]{:S(2)}) collective-permute-start(f32[64,24,128]{2,1,0:T(8,128)S(1)} %get-tuple-element.52.x_ref.rest_0_), channel_id=1, source_target_pairs={{0,2},{1,3},{2,0},{3,1},{4,6},{5,7},{6,4},{7,5},{8,10},{9,11},{10,... | collective-permute-start | bytes 2359304 | tf_op jit(solution)/shard_map/ppermute | solution.py:20
  5.7 34.0 %collective-permute-start = (f32[2,512,128]{2,1,0:T(8,128)S(1)}, f32[2,512,128]{2,1,0:T(8,128)S(1)}, u32[]{:S(2)}, u32[]{:S(2)}) collective-permute-start(f32[2,512,128]{2,1,0:T(8,128)S(1)} %fusion), channel_id=1, source_target_pairs={{0,4},{4,0},{8,12},{12,8},{16,20},{20,16},{24,28},{28,24},{1,5},{5... | collective-permute-start | bytes 1572872 | tf_op jit(solution)/shard_map/ppermute | solution.py:25
  23.6 16.2 %copy-start.10 = (f32[64,24,128]{2,1,0:T(8,128)}, f32[64,24,128]{2,1,0:T(8,128)S(1)}, u32[]{:S(2)}) copy-start(f32[64,24,128]{2,1,0:T(8,128)S(1)} %collective-permute-done.3.rest_2_) | copy-start | bytes 2359300
  23.6 22.1 %collective-permute-start.4 = (f32[64,24,128]{2,1,0:T(8,128)S(1)}, f32[64,24,128]{2,1,0:T(8,128)S(1)}, u32[]{:S(2)}, u32[]{:S(2)}) collective-permute-start(f32[64,24,128]{2,1,0:T(8,128)S(1)} %collective-permute-done.3.rest_2_), channel_id=1, source_target_pairs={{0,1},{1,0},{2,3},{3,2},{4,5},{5,4},{6,7},{7,6},{8,9},{9,8},{10,11... | collective-permute-start | bytes 2359304 | tf_op jit(solution)/shard_map/ppermute | solution.py:20
  37.1 20.1 %collective-permute-start.6 = (f32[56,24,128]{2,1,0:T(8,128)S(1)}, f32[56,24,128]{2,1,0:T(8,128)S(1)}, u32[]{:S(2)}, u32[]{:S(2)}) collective-permute-start(f32[56,24,128]{2,1,0:T(8,128)S(1)} %slice.24), channel_id=1, source_target_pairs={{0,8},{4,28},{8,16},{12,4},{16,24},{20,12},{24,0},{28,20},{1,9},{5... | collective-permute-start | bytes 2064392 | tf_op jit(solution)/shard_map/ppermute | solution.py:34
  39.7 7.4 %copy-start.22 = (f32[2,512,128]{2,1,0:T(8,128)}, f32[2,512,128]{2,1,0:T(8,128)S(1)}, u32[]{:S(2)}) copy-start(f32[2,512,128]{2,1,0:T(8,128)S(1)} %collective-permute-done.theirs_ref) | copy-start | bytes 1572868
  42.9 7.4 %copy-start.30 = (f32[64,24,128]{2,1,0:T(8,128)}, f32[64,24,128]{2,1,0:T(8,128)S(1)}, u32[]{:S(2)}) copy-start(f32[64,24,128]{2,1,0:T(8,128)S(1)} %get-tuple-element.35.s_ref) | copy-start | bytes 2359300
  42.9 24.8 %collective-permute-start.5 = (f32[64,24,128]{2,1,0:T(8,128)}, f32[64,24,128]{2,1,0:T(8,128)S(1)}, u32[]{:S(2)}, u32[]{:S(2)}) collective-permute-start(f32[64,24,128]{2,1,0:T(8,128)} %get-tuple-element.38), channel_id=1, source_target_pairs={{0,4},{4,0},{8,12},{12,8},{16,20},{20,16},{24,28},{28,24},{1,5},{5... | collective-permute-start | bytes 2359304 | tf_op jit(solution)/shard_map/ppermute | solution.py:25
  45.1 27.7 %collective-permute-start.16 = (f32[64,24,128]{2,1,0:T(8,128)S(1)}, f32[64,24,128]{2,1,0:T(8,128)}, u32[]{:S(2)}, u32[]{:S(2)}) collective-permute-start(f32[64,24,128]{2,1,0:T(8,128)S(1)} %get-tuple-element.52.x_ref.rest_0_), channel_id=1, source_target_pairs={{0,1},{1,0},{2,3},{3,2},{4,5},{5,4},{6,7},{7,6},{8,9},{9,8},{10,11... | collective-permute-start | bytes 2359304 | tf_op jit(solution)/shard_map/ppermute | solution.py:20
  45.1 5.1 %copy-start.12 = (f32[64,24,128]{2,1,0:T(8,128)}, f32[64,24,128]{2,1,0:T(8,128)S(1)}, u32[]{:S(2)}) copy-start(f32[64,24,128]{2,1,0:T(8,128)S(1)} %collective-permute-done.2.rest_1_) | copy-start | bytes 2359300
  45.1 27.6 %collective-permute-start.18 = (f32[64,24,128]{2,1,0:T(8,128)}, f32[64,24,128]{2,1,0:T(8,128)}, u32[]{:S(2)}, u32[]{:S(2)}) collective-permute-start(f32[64,24,128]{2,1,0:T(8,128)} %collective-permute-done.17.rest_2_), channel_id=1, source_target_pairs={{0,1},{1,0},{2,3},{3,2},{4,5},{5,4},{6,7},{7,6},{8,9},{9,8},{10,11... | collective-permute-start | bytes 2359304 | tf_op jit(solution)/shard_map/ppermute | solution.py:20
  45.7 4.6 %copy-start.16 = (f32[64,24,128]{2,1,0:T(8,128)}, f32[64,24,128]{2,1,0:T(8,128)S(1)}, u32[]{:S(2)}) copy-start(f32[64,24,128]{2,1,0:T(8,128)S(1)} %collective-permute-done.4.rest_3_) | copy-start | bytes 2359300
  45.7 10.2 %collective-permute-start.7 = (f32[8,24,128]{2,1,0:T(8,128)S(1)}, f32[8,24,128]{2,1,0:T(8,128)S(1)}, u32[]{:S(2)}, u32[]{:S(2)}) collective-permute-start(f32[8,24,128]{2,1,0:T(8,128)S(1)} %slice.25), channel_id=1, source_target_pairs={{0,8},{4,28},{8,16},{12,4},{16,24},{20,12},{24,0},{28,20},{1,9},{5... | collective-permute-start | bytes 294920 | tf_op jit(solution)/shard_map/ppermute | solution.py:34
  47.2 14.8 %copy-start.25 = (f32[192,192]{1,0:T(8,128)S(1)}, f32[192,192]{1,0:T(8,128)}, u32[]{:S(2)}) copy-start(f32[192,192]{1,0:T(8,128)} %inv_ref.1) | copy-start | bytes 442372
  55.9 22.8 %collective-permute-start.19 = (f32[64,24,128]{2,1,0:T(8,128)}, f32[64,24,128]{2,1,0:T(8,128)}, u32[]{:S(2)}, u32[]{:S(2)}) collective-permute-start(f32[64,24,128]{2,1,0:T(8,128)} %get-tuple-element.51), channel_id=1, source_target_pairs={{0,4},{4,0},{8,12},{12,8},{16,20},{20,16},{24,28},{28,24},{1,5},{5... | collective-permute-start | bytes 2359304 | tf_op jit(solution)/shard_map/ppermute | solution.py:25
  58.0 20.7 %collective-permute-start.20 = (f32[64,24,128]{2,1,0:T(8,128)S(1)}, f32[64,24,128]{2,1,0:T(8,128)}, u32[]{:S(2)}, u32[]{:S(2)}) collective-permute-start(f32[64,24,128]{2,1,0:T(8,128)S(1)} %get-tuple-element.52.x_ref.rest_0_), channel_id=1, source_target_pairs={{0,8},{4,28},{8,16},{12,4},{16,24},{20,12},{24,0},{28,20},{1,9},{5... | collective-permute-start | bytes 2359304 | tf_op jit(solution)/shard_map/ppermute | solution.py:34
  61.0 4.6 %copy-start.11 = (f32[64,24,128]{2,1,0:T(8,128)S(1)}, f32[64,24,128]{2,1,0:T(8,128)}, u32[]{:S(2)}) copy-start(f32[64,24,128]{2,1,0:T(8,128)} %copy-done.10) | copy-start | bytes 2359300
  61.0 4.6 %copy-start.13 = (f32[64,24,128]{2,1,0:T(8,128)S(1)}, f32[64,24,128]{2,1,0:T(8,128)}, u32[]{:S(2)}) copy-start(f32[64,24,128]{2,1,0:T(8,128)} %copy-done.12) | copy-start | bytes 2359300
  61.0 4.6 %copy-start.17 = (f32[64,24,128]{2,1,0:T(8,128)S(1)}, f32[64,24,128]{2,1,0:T(8,128)}, u32[]{:S(2)}) copy-start(f32[64,24,128]{2,1,0:T(8,128)} %copy-done.16) | copy-start | bytes 2359300
  62.0 5.7 %copy-start.6 = (f32[64,24,128]{2,1,0:T(8,128)}, f32[64,24,128]{2,1,0:T(8,128)S(1)}, u32[]{:S(2)}) copy-start(f32[64,24,128]{2,1,0:T(8,128)S(1)} %get-tuple-element.32.f_ref) | copy-start | bytes 2359300
  62.0 10.8 %copy-start.8 = (f32[64,24,128]{2,1,0:T(8,128)}, f32[64,24,128]{2,1,0:T(8,128)S(1)}, u32[]{:S(2)}) copy-start(f32[64,24,128]{2,1,0:T(8,128)S(1)} %get-tuple-element.47.f_ref) | copy-start | bytes 2359300
  65.6 7.2 %copy-start.32 = (bf16[1024,256]{1,0:T(8,128)(2,1)}, bf16[1024,256]{1,0:T(8,128)(2,1)S(1)}, u32[]{:S(2)}) copy-start(bf16[1024,256]{1,0:T(8,128)(2,1)S(1)} %get-tuple-element.36.mh_ref) | copy-start | bytes 1572868
  65.6 7.2 %copy-start.34 = (bf16[1024,256]{1,0:T(8,128)(2,1)}, bf16[1024,256]{1,0:T(8,128)(2,1)S(1)}, u32[]{:S(2)}) copy-start(bf16[1024,256]{1,0:T(8,128)(2,1)S(1)} %get-tuple-element.37.ml_ref) | copy-start | bytes 1572868
  71.8 22.0 %collective-permute-start.8 = (f32[56,24,128]{2,1,0:T(8,128)S(1)}, f32[56,24,128]{2,1,0:T(8,128)S(1)}, u32[]{:S(2)}, u32[]{:S(2)}) collective-permute-start(f32[56,24,128]{2,1,0:T(8,128)S(1)} %slice.26), channel_id=1, source_target_pairs={{0,24},{4,12},{8,0},{12,20},{16,8},{20,28},{24,16},{28,4},{1,25},{... | collective-permute-start | bytes 2064392 | tf_op jit(solution)/shard_map/ppermute | solution.py:34
  76.4 50.3 %copy-start.23 = (f32[2,512,128]{2,1,0:T(8,128)S(1)}, f32[2,512,128]{2,1,0:T(8,128)}, u32[]{:S(2)}) copy-start(f32[2,512,128]{2,1,0:T(8,128)} %copy-done.22) | copy-start | bytes 1572868
  81.5 24.3 %collective-permute-start.23 = (f32[64,24,128]{2,1,0:T(8,128)S(1)}, f32[64,24,128]{2,1,0:T(8,128)}, u32[]{:S(2)}, u32[]{:S(2)}) collective-permute-start(f32[64,24,128]{2,1,0:T(8,128)S(1)} %get-tuple-element.57.x_ref.rest_0_), channel_id=1, source_target_pairs={{0,2},{1,3},{2,0},{3,1},{4,6},{5,7},{6,4},{7,5},{8,10},{9,11},{10,... | collective-permute-start | bytes 2359304 | tf_op jit(solution)/shard_map/ppermute | solution.py:20
  83.0 35.1 %collective-permute-start.21 = (f32[64,24,128]{2,1,0:T(8,128)S(1)}, f32[64,24,128]{2,1,0:T(8,128)S(1)}, u32[]{:S(2)}, u32[]{:S(2)}) collective-permute-start(f32[64,24,128]{2,1,0:T(8,128)S(1)} %get-tuple-element.57.x_ref.rest_0_), channel_id=1, source_target_pairs={{0,24},{4,12},{8,0},{12,20},{16,8},{20,28},{24,16},{28,4},{1,25},{... | collective-permute-start | bytes 2359304 | tf_op jit(solution)/shard_map/ppermute | solution.py:34
  87.2 49.1 %collective-permute-start.22 = (f32[64,24,128]{2,1,0:T(8,128)S(1)}, f32[64,24,128]{2,1,0:T(8,128)S(1)}, u32[]{:S(2)}, u32[]{:S(2)}) collective-permute-start(f32[64,24,128]{2,1,0:T(8,128)S(1)} %get-tuple-element.57.x_ref.rest_0_), channel_id=1, source_target_pairs={{0,1},{1,0},{2,3},{3,2},{4,5},{5,4},{6,7},{7,6},{8,9},{9,8},{10,11... | collective-permute-start | bytes 2359304 | tf_op jit(solution)/shard_map/ppermute | solution.py:20
  87.2 50.1 %collective-permute-start.11 = (f32[64,24,128]{2,1,0:T(8,128)S(1)}, f32[64,24,128]{2,1,0:T(8,128)}, u32[]{:S(2)}, u32[]{:S(2)}) collective-permute-start(f32[64,24,128]{2,1,0:T(8,128)S(1)} %get-tuple-element.46.x_ref.rest_0_), channel_id=1, source_target_pairs={{0,2},{1,3},{2,0},{3,1},{4,6},{5,7},{6,4},{7,5},{8,10},{9,11},{10,... | collective-permute-start | bytes 2359304 | tf_op jit(solution)/shard_map/ppermute | solution.py:20
  93.8 36.0 %copy-start.18 = (f32[56,24,128]{2,1,0:T(8,128)}, f32[56,24,128]{2,1,0:T(8,128)S(1)}, u32[]{:S(2)}) copy-start(f32[56,24,128]{2,1,0:T(8,128)S(1)} %collective-permute-done.8.rest_0_) | copy-start | bytes 2064388
  93.8 48.3 %collective-permute-start.26 = (f32[64,24,128]{2,1,0:T(8,128)S(1)}, f32[64,24,128]{2,1,0:T(8,128)S(1)}, u32[]{:S(2)}, u32[]{:S(2)}) collective-permute-start(f32[64,24,128]{2,1,0:T(8,128)S(1)} %get-tuple-element.57.x_ref.rest_0_), channel_id=1, source_target_pairs={{0,8},{4,28},{8,16},{12,4},{16,24},{20,12},{24,0},{28,20},{1,9},{5... | collective-permute-start | bytes 2359304 | tf_op jit(solution)/shard_map/ppermute | solution.py:34
  105.9 38.4 %collective-permute-start.24 = (f32[64,24,128]{2,1,0:T(8,128)}, f32[64,24,128]{2,1,0:T(8,128)}, u32[]{:S(2)}, u32[]{:S(2)}) collective-permute-start(f32[64,24,128]{2,1,0:T(8,128)} %collective-permute-done.23.rest_2_), channel_id=1, source_target_pairs={{0,1},{1,0},{2,3},{3,2},{4,5},{5,4},{6,7},{7,6},{8,9},{9,8},{10,11... | collective-permute-start | bytes 2359304 | tf_op jit(solution)/shard_map/ppermute | solution.py:20
  118.1 18.2 %collective-permute-start.9 = (f32[8,24,128]{2,1,0:T(8,128)S(1)}, f32[8,24,128]{2,1,0:T(8,128)S(1)}, u32[]{:S(2)}, u32[]{:S(2)}) collective-permute-start(f32[8,24,128]{2,1,0:T(8,128)S(1)} %slice.27), channel_id=1, source_target_pairs={{0,24},{4,12},{8,0},{12,20},{16,8},{20,28},{24,16},{28,4},{1,25},{... | collective-permute-start | bytes 294920 | tf_op jit(solution)/shard_map/ppermute | solution.py:34
  136.3 20.7 %collective-permute-start.25 = (f32[64,24,128]{2,1,0:T(8,128)}, f32[64,24,128]{2,1,0:T(8,128)}, u32[]{:S(2)}, u32[]{:S(2)}) collective-permute-start(f32[64,24,128]{2,1,0:T(8,128)} %get-tuple-element.56), channel_id=1, source_target_pairs={{0,4},{4,0},{8,12},{12,8},{16,20},{20,16},{24,28},{28,24},{1,5},{5... | collective-permute-start | bytes 2359304 | tf_op jit(solution)/shard_map/ppermute | solution.py:25
  137.2 22.7 %collective-permute-start.10 = (f32[64,24,128]{2,1,0:T(8,128)S(1)}, f32[64,24,128]{2,1,0:T(8,128)}, u32[]{:S(2)}, u32[]{:S(2)}) collective-permute-start(f32[64,24,128]{2,1,0:T(8,128)S(1)} %get-tuple-element.46.x_ref.rest_0_), channel_id=1, source_target_pairs={{0,1},{1,0},{2,3},{3,2},{4,5},{5,4},{6,7},{7,6},{8,9},{9,8},{10,11... | collective-permute-start | bytes 2359304 | tf_op jit(solution)/shard_map/ppermute | solution.py:20
  137.3 22.6 %collective-permute-start.12 = (f32[64,24,128]{2,1,0:T(8,128)}, f32[64,24,128]{2,1,0:T(8,128)}, u32[]{:S(2)}, u32[]{:S(2)}) collective-permute-start(f32[64,24,128]{2,1,0:T(8,128)} %collective-permute-done.11.rest_2_), channel_id=1, source_target_pairs={{0,1},{1,0},{2,3},{3,2},{4,5},{5,4},{6,7},{7,6},{8,9},{9,8},{10,11... | collective-permute-start | bytes 2359304 | tf_op jit(solution)/shard_map/ppermute | solution.py:20
  139.8 5.2 %copy-start.27 = (f32[64,24,128]{2,1,0:T(8,128)S(1)}, f32[64,24,128]{2,1,0:T(8,128)}, u32[]{:S(2)}) copy-start(f32[64,24,128]{2,1,0:T(8,128)} %copy-done.26) | copy-start | bytes 2359300
  139.8 5.2 %copy-start.33 = (bf16[1024,256]{1,0:T(8,128)(2,1)S(1)}, bf16[1024,256]{1,0:T(8,128)(2,1)}, u32[]{:S(2)}) copy-start(bf16[1024,256]{1,0:T(8,128)(2,1)} %copy-done.32) | copy-start | bytes 1572868
  139.8 5.2 %copy-start.35 = (bf16[1024,256]{1,0:T(8,128)(2,1)S(1)}, bf16[1024,256]{1,0:T(8,128)(2,1)}, u32[]{:S(2)}) copy-start(bf16[1024,256]{1,0:T(8,128)(2,1)} %copy-done.34) | copy-start | bytes 1572868
  142.1 30.8 %collective-permute-start.13 = (f32[64,24,128]{2,1,0:T(8,128)S(1)}, f32[64,24,128]{2,1,0:T(8,128)S(1)}, u32[]{:S(2)}, u32[]{:S(2)}) collective-permute-start(f32[64,24,128]{2,1,0:T(8,128)S(1)} %get-tuple-element.45), channel_id=1, source_target_pairs={{0,4},{4,0},{8,12},{12,8},{16,20},{20,16},{24,28},{28,24},{1,5},{5... | collective-permute-start | bytes 2359304 | tf_op jit(solution)/shard_map/ppermute | solution.py:25
  144.2 19.2 %collective-permute-start.14 = (f32[40,24,128]{2,1,0:T(8,128)S(1)}, f32[40,24,128]{2,1,0:T(8,128)S(1)}, u32[]{:S(2)}, u32[]{:S(2)}) collective-permute-start(f32[40,24,128]{2,1,0:T(8,128)S(1)} %constant_dynamic-slice_fusion.1), channel_id=1, source_target_pairs={{0,8},{4,28},{8,16},{12,4},{16,24},{20,12},{24,0},{28,20},{1,9},{5... | collective-permute-start | bytes 1474568 | tf_op jit(solution)/shard_map/ppermute | solution.py:34
  148.4 11.5 %copy-start.7 = (f32[64,24,128]{2,1,0:T(8,128)S(1)}, f32[64,24,128]{2,1,0:T(8,128)}, u32[]{:S(2)}) copy-start(f32[64,24,128]{2,1,0:T(8,128)} %copy-done.6) | copy-start | bytes 2359300
  157.0 18.7 %collective-permute-start.15 = (f32[24,24,128]{2,1,0:T(8,128)S(1)}, f32[24,24,128]{2,1,0:T(8,128)S(1)}, u32[]{:S(2)}, u32[]{:S(2)}) collective-permute-start(f32[24,24,128]{2,1,0:T(8,128)S(1)} %constant_dynamic-slice_fusion), channel_id=1, source_target_pairs={{0,8},{4,28},{8,16},{12,4},{16,24},{20,12},{24,0},{28,20},{1,9},{5... | collective-permute-start | bytes 884744 | tf_op jit(solution)/shard_map/ppermute | solution.py:34
  (19 other events, 32.1 us)

commit v3 on v1

--- a/solution.py
+++ b/solution.py
@@ -257,8 +257,8 @@
     )(f, s, mh, ml, *blocks)
 
 
-def far_terms(lo, n, off_ref, w_ref, far_ref, r_ref):
-    points, rows, _ = far_ref.shape
+def far_terms(lo, n, points, base, off_ref, w_ref, far_ref, r_ref):
+    rows = far_ref.shape[1]
     cw = rows * 2 // 3
 
     sign = own_sign()
@@ -268,7 +268,7 @@
         count = jnp.minimum(lo + n, points - shift) - first
 
         def point(p, b=b, shift=shift):
-            top, low = scaled(w_ref, b * points + p, far_ref[p + shift], cw)
+            top, low = scaled(w_ref, b * points + p, far_ref[p + shift - base], cw)
             r_ref[p - lo, :cw, :] = r_ref[p - lo, :cw, :] - top
             r_ref[p - lo, cw:, :] = r_ref[p - lo, cw:, :] - low
 
@@ -308,7 +308,7 @@
         return 0
 
     lax.fori_loop(0, points // UNROLL, begin, 0)
-    far_terms(0, points, off_ref, w_ref, far_ref, r_ref)
+    far_terms(0, points, points, 0, off_ref, w_ref, far_ref, r_ref)
     update(x_ref, 0, r_ref, high_ref, low_ref, bh_ref, bl_ref, x_new_ref)
 
 
@@ -343,22 +343,26 @@
     points = x_ref.shape[0]
     n = sizes[i]
     lo = piece_start(sizes, i, points)
-    for m, ref in enumerate(fars):
-        at = piece_start(sizes, m, points)
-
-        def copy(j, _):
-            far_ref[pl.ds(at + j * UNROLL, UNROLL)] = ref[pl.ds(j * UNROLL, UNROLL)]
-            return 0
-
-        lax.fori_loop(0, sizes[m] // UNROLL, copy, 0)
+    base = 0
+    if i == 0:
+        far_ref, base = fars[0], lo
+    else:
+        for m, ref in enumerate(fars):
+            at = piece_start(sizes, m, points)
+
+            def copy(j, _, ref=ref, at=at):
+                far_ref[pl.ds(at + j * UNROLL, UNROLL)] = ref[pl.ds(j * UNROLL, UNROLL)]
+                return 0
+
+            lax.fori_loop(0, sizes[m] // UNROLL, copy, 0, unroll=2)
 
     def begin(j, _):
         here = pl.ds(lo + j * UNROLL, UNROLL)
         r_ref[pl.ds(j * UNROLL, UNROLL)] = g_ref[here] - t_ref[here]
         return 0
 
-    lax.fori_loop(0, n // UNROLL, begin, 0)
-    far_terms(lo, n, off_ref, w_ref, far_ref, r_ref)
+    lax.fori_loop(0, n // UNROLL, begin, 0, unroll=2)
+    far_terms(lo, n, points, base, off_ref, w_ref, far_ref, r_ref)
     views = [ref.at[pl.ds(lo, n)] for ref in earlier]
     sols, ress = [*views[::2], x_new_ref], [*views[1::2], r_ref]
     vectors = n * width // LANES
@@ -495,7 +499,7 @@
     their_w = partner(own_w[:, : bands * points])
     mh, ml, bh, bl = prep(wall_even, wall_odd, block_inv)
     f = split(forcing, chunks, points)
-    sizes = (points * 5 // 8, points * 3 // 8)
+    sizes = (points * 3 // 8, points * 3 // 8, points // 4)
     arrived = raw_first
     order = [0]
     bit = n_wall // 2

time: 179 us -> 165 us (0.922)
  the two profiles are of different devices: /device:TPU:28 before, /device:TPU:0 now
where the time goes in v3:
time: 165 us; the launch traced here: 164 us
  waiting for transfers between devices  80.3 us (49%)
  Pallas kernels  43 us (26%)
  starting transfers between devices  29 us (18%)
  local copies, waits for them, and re-layouts  10 us (6%)
    ppermute x9, waiting for transfers between devices, far(): return lax.ppermute(value, 'span', pairs)  42.4 us
    ppermute x12, waiting for transfers between devices, exchange(): return lax.ppermute(value, 'wall', [(i, i ^ bit) for i in range(count)])  19.3 us
    ppermute x5, waiting for transfers between devices, partner(): return lax.ppermute(value, 'span', [(i, i ^ 1) for i in range(count)])  18.6 us
    ppermute x5, starting transfers between devices, partner(): return lax.ppermute(value, 'span', [(i, i ^ 1) for i in range(count)])  16.1 us
    pallas_call x4, Pallas kernels, wall(): pl.pallas_call(functools.partial(wall_kernel, n_blocks), out_shape=jax.Sh...  14 us
    pallas_call x4, Pallas kernels, near(): pl.pallas_call(functools.partial(near_kernel, bands), out_shape=(out, out...  11.8 us
    unnamed x56, local copies, waits for them, and re-layouts  9.85 us
    ppermute x9, starting transfers between devices, far(): return lax.ppermute(value, 'span', pairs)  6.7 us
  transfers between devices with their start and end apart: 26, of which 12 were waited for; matrix products, arithmetic and copies ran while one was open for 0% of the time, Pallas kernels for 25%

profile of v3, /device:TPU:0, one launch (start us, length us, event | category | flops | bytes accessed | tf_op | source)
XLA Modules:
  0.0 163.9 jit_solution(3723151630803235333)
XLA Ops:
  0.6 5.1 %collective-permute-start = (f32[192,2048]{1,0:T(8,128)}, f32[192,2048]{1,0:T(8,128)S(1)}, u32[]{:S(2)}, u32[]{:S(2)}) collective-permute-start(f32[192,2048]{1,0:T(8,128)} %x_ref.3), channel_id=1, source_target_pairs={{0,24},{4,12},{8,0},{12,20},{16,8},{20,28},{24,16},{28,4},{1,25},{... | collective-permute-start | bytes 4718600 | tf_op jit(solution)/shard_map/ppermute | solution.py:34
  5.8 1.4 copy-done
  7.2 1.8 %split.4 = (f32[64,24,128]{2,1,0:T(8,128)}, f32[64,24,128]{2,1,0:T(8,128)S(1)}) custom-call(f32[192,2048]{1,0:T(8,128)S(1)} %copy-done), custom_call_target="tpu_custom_call" | custom-call | bytes 3145728 | tf_op jit(solution)/shard_map/split/pallas_call | solution.py:77
  9.0 1.5 collective-permute-start.16
  11.2 0.6 collective-permute-start.3
  11.8 18.0 %collective-permute-done.16.rest_2_ = f32[64,24,128]{2,1,0:T(8,128)} collective-permute-done((f32[64,24,128]{2,1,0:T(8,128)}, f32[64,24,128]{2,1,0:T(8,128)}, u32[]{:S(2)}, u32[]{:S(2)}) %collective-permute-start.16) | collective-permute-done | bytes 786464 | tf_op jit(solution)/shard_map/ppermute | solution.py:20
  29.8 10.0 %collective-permute-done.x_ref = f32[192,2048]{1,0:T(8,128)S(1)} collective-permute-done((f32[192,2048]{1,0:T(8,128)}, f32[192,2048]{1,0:T(8,128)S(1)}, u32[]{:S(2)}, u32[]{:S(2)}) %collective-permute-start) | collective-permute-done | bytes 1572896 | tf_op jit(solution)/shard_map/ppermute | solution.py:34
  39.7 0.9 split.5
  40.7 0.9 copy-done.10
  41.7 4.3 %near.6 = (f32[64,24,128]{2,1,0:T(8,128)}, f32[64,24,128]{2,1,0:T(8,128)S(1)}) custom-call(s32[8,128]{1,0:T(8,128)S(1)} %broadcast_in_dim.6.off_ref, f32[64,24,128]{2,1,0:T(8,128)} %get-tuple-element.54.x_ref.rest_0_, f32[64,24,128]{2,1,0:T(8,128)S(1)} %get-tuple-element.51.far_ref, f32[2,576,128]{2,1,0:T(8,128)S(1)} %pad_maximum_fusion.w_ref, ...), custom_call_target="tpu_custom_call" | custom-call | flops 1000000000 | bytes 4718592 | tf_op jit(solution)/shard_map/near/pallas_call | solution.py:182
  46.0 1.0 copy-done.18
  46.9 2.1 %collective-permute-start.18 = (f32[64,24,128]{2,1,0:T(8,128)}, f32[64,24,128]{2,1,0:T(8,128)}, u32[]{:S(2)}, u32[]{:S(2)}) collective-permute-start(f32[64,24,128]{2,1,0:T(8,128)} %get-tuple-element.53), channel_id=1, source_target_pairs={{0,4},{4,0},{8,12},{12,8},{16,20},{20,16},{24,28},{28,24},{1,5},{5... | collective-permute-start | bytes 2359304 | tf_op jit(solution)/shard_map/ppermute | solution.py:25
  49.1 0.9 copy-done.6
  50.5 0.9 split.3
  51.5 1.5 copy-done.12
  53.0 1.1 copy-done.13
  54.0 1.0 prep.1
  55.1 2.1 %near.4 = (f32[64,24,128]{2,1,0:T(8,128)S(1)}, f32[64,24,128]{2,1,0:T(8,128)S(1)}) custom-call(s32[8,128]{1,0:T(8,128)S(1)} %broadcast_in_dim.6.off_ref, f32[64,24,128]{2,1,0:T(8,128)S(1)} %get-tuple-element.43.x_ref.rest_0_, f32[64,24,128]{2,1,0:T(8,128)S(1)} %copy-done.11, f32[2,576,128]{2,1,0:T(8,128)S(1)} %pad_maximum_fusion.w_ref, ...), custom_call_target="tpu_custom_call" | custom-call | flops 1000000000 | bytes 4718592 | tf_op jit(solution)/shard_map/near/pallas_call | solution.py:182
  57.2 4.1 %collective-permute-start.5 = (f32[64,24,128]{2,1,0:T(8,128)S(1)}, f32[64,24,128]{2,1,0:T(8,128)S(1)}, u32[]{:S(2)}, u32[]{:S(2)}) collective-permute-start(f32[64,24,128]{2,1,0:T(8,128)S(1)} %get-tuple-element.40), channel_id=1, source_target_pairs={{0,4},{4,0},{8,12},{12,8},{16,20},{20,16},{24,28},{28,24},{1,5},{5... | collective-permute-start | bytes 2359304 | tf_op jit(solution)/shard_map/ppermute | solution.py:25
  61.3 6.4 %collective-permute-done.18.t_ref = f32[64,24,128]{2,1,0:T(8,128)} collective-permute-done((f32[64,24,128]{2,1,0:T(8,128)}, f32[64,24,128]{2,1,0:T(8,128)}, u32[]{:S(2)}, u32[]{:S(2)}) %collective-permute-start.18) | collective-permute-done | bytes 786464 | tf_op jit(solution)/shard_map/ppermute | solution.py:25
  68.0 3.5 %wall.6.g_ref = f32[64,24,128]{2,1,0:T(8,128)S(1)} custom-call(f32[64,24,128]{2,1,0:T(8,128)S(1)} %get-tuple-element.49.f_ref, f32[64,24,128]{2,1,0:T(8,128)S(1)} %copy-done.19, bf16[1024,256]{1,0:T(8,128)(2,1)S(1)} %get-tuple-element.38.mh_ref, bf16[1024,256]{1,0:T(8,128)(2,1)S(1)} %get-tuple-element.39.ml_ref, ...), custom_call_target="tpu_custom_call" | custom-call | flops 3000000000 | bytes 6291456 | tf_op jit(solution)/shard_map/wall/pallas_call | solution.py:248
  71.6 3.0 %last.4 = (f32[64,24,128]{2,1,0:T(8,128)S(1)}, f32[64,24,128]{2,1,0:T(8,128)}) custom-call(s32[8,128]{1,0:T(8,128)S(1)} %broadcast_in_dim.6.off_ref, f32[64,24,128]{2,1,0:T(8,128)S(1)} %wall.6.g_ref, f32[64,24,128]{2,1,0:T(8,128)} %collective-permute-done.18.t_ref, f32[64,24,128]{2,1,0:T(8,128)} %get-tuple-element.54.x_ref.rest_0_, ...), custom_call_target="tpu_custom_call" | custom-call | flops 1000000000 | bytes 6291456 | tf_op jit(solution)/shard_map/last/pallas_call | solution.py:319
  74.6 1.5 collective-permute-start.22
  76.1 3.5 %wall.4.g_ref = f32[64,24,128]{2,1,0:T(8,128)S(1)} custom-call(f32[64,24,128]{2,1,0:T(8,128)S(1)} %get-tuple-element.34.f_ref, f32[64,24,128]{2,1,0:T(8,128)S(1)} %get-tuple-element.37.s_ref, bf16[1024,256]{1,0:T(8,128)(2,1)S(1)} %get-tuple-element.38.mh_ref, bf16[1024,256]{1,0:T(8,128)(2,1)S(1)} %get-tuple-element.39.ml_ref, ...), custom_call_target="tpu_custom_call" | custom-call | flops 3000000000 | bytes 6291456 | tf_op jit(solution)/shard_map/wall/pallas_call | solution.py:248
  79.7 3.2 %collective-permute-done.5.t_ref = f32[64,24,128]{2,1,0:T(8,128)S(1)} collective-permute-done((f32[64,24,128]{2,1,0:T(8,128)S(1)}, f32[64,24,128]{2,1,0:T(8,128)S(1)}, u32[]{:S(2)}, u32[]{:S(2)}) %collective-permute-start.5) | collective-permute-done | bytes 786464 | tf_op jit(solution)/shard_map/ppermute | solution.py:25
  82.9 3.4 %collective-permute-done.6.far_ref = f32[64,24,128]{2,1,0:T(8,128)S(1)} collective-permute-done((f32[64,24,128]{2,1,0:T(8,128)S(1)}, f32[64,24,128]{2,1,0:T(8,128)S(1)}, u32[]{:S(2)}, u32[]{:S(2)}) %collective-permute-start.6) | collective-permute-done | bytes 786464 | tf_op jit(solution)/shard_map/ppermute | solution.py:34
  86.2 2.0 %last.3 = (f32[64,24,128]{2,1,0:T(8,128)S(1)}, f32[64,24,128]{2,1,0:T(8,128)}) custom-call(s32[8,128]{1,0:T(8,128)S(1)} %broadcast_in_dim.6.off_ref, f32[64,24,128]{2,1,0:T(8,128)S(1)} %wall.4.g_ref, f32[64,24,128]{2,1,0:T(8,128)S(1)} %collective-permute-done.5.t_ref, f32[64,24,128]{2,1,0:T(8,128)S(1)} %get-tuple-element.43.x_ref.rest_0_, ...), custom_call_target="tpu_custom_call" | custom-call | flops 1000000000 | bytes 6291456 | tf_op jit(solution)/shard_map/last/pallas_call | solution.py:319
  88.2 1.2 collective-permute-start.7
  89.4 1.5 collective-permute-start.9
  90.9 1.3 collective-permute-done.22.rest_2_
  92.2 16.4 %collective-permute-done.7.far_ref = f32[64,24,128]{2,1,0:T(8,128)S(1)} collective-permute-done((f32[64,24,128]{2,1,0:T(8,128)S(1)}, f32[64,24,128]{2,1,0:T(8,128)S(1)}, u32[]{:S(2)}, u32[]{:S(2)}) %collective-permute-start.7) | collective-permute-done | bytes 786464 | tf_op jit(solution)/shard_map/ppermute | solution.py:34
  108.6 0.9 copy-done.8
  110.0 1.1 copy-done.9
  111.2 1.0 copy-done.16
  112.2 2.1 %near.5 = (f32[64,24,128]{2,1,0:T(8,128)S(1)}, f32[64,24,128]{2,1,0:T(8,128)S(1)}) custom-call(s32[8,128]{1,0:T(8,128)S(1)} %broadcast_in_dim.6.off_ref, f32[64,24,128]{2,1,0:T(8,128)S(1)} %get-tuple-element.48.x_ref.rest_0_, f32[64,24,128]{2,1,0:T(8,128)S(1)} %copy-done.9, f32[2,576,128]{2,1,0:T(8,128)S(1)} %pad_maximum_fusion.w_ref, ...), custom_call_target="tpu_custom_call" | custom-call | flops 1000000000 | bytes 4718592 | tf_op jit(solution)/shard_map/near/pallas_call | solution.py:182
  114.3 9.4 %collective-permute-done.20.far_ref = f32[64,24,128]{2,1,0:T(8,128)} collective-permute-done((f32[64,24,128]{2,1,0:T(8,128)S(1)}, f32[64,24,128]{2,1,0:T(8,128)}, u32[]{:S(2)}, u32[]{:S(2)}) %collective-permute-start.20) | collective-permute-done | bytes 786464 | tf_op jit(solution)/shard_map/ppermute | solution.py:34
  123.7 3.3 %near.7 = (f32[64,24,128]{2,1,0:T(8,128)S(1)}, f32[64,24,128]{2,1,0:T(8,128)S(1)}) custom-call(s32[8,128]{1,0:T(8,128)S(1)} %broadcast_in_dim.6.off_ref, f32[64,24,128]{2,1,0:T(8,128)S(1)} %get-tuple-element.59.x_ref.rest_0_, f32[64,24,128]{2,1,0:T(8,128)} %collective-permute-done.20.far_ref, f32[2,576,128]{2,1,0:T(8,128)S(1)} %pad_maximum_fusion.w_ref, ...), custom_call_target="tpu_custom_call" | custom-call | flops 1000000000 | bytes 4718592 | tf_op jit(solution)/shard_map/near/pallas_call | solution.py:182
  127.0 9.6 %collective-permute-start.24 = (f32[64,24,128]{2,1,0:T(8,128)S(1)}, f32[64,24,128]{2,1,0:T(8,128)S(1)}, u32[]{:S(2)}, u32[]{:S(2)}) collective-permute-start(f32[64,24,128]{2,1,0:T(8,128)S(1)} %get-tuple-element.58), channel_id=1, source_target_pairs={{0,4},{4,0},{8,12},{12,8},{16,20},{20,16},{24,28},{28,24},{1,5},{5... | collective-permute-start | bytes 2359304 | tf_op jit(solution)/shard_map/ppermute | solution.py:25
  136.9 3.6 %wall.7.g_ref = f32[64,24,128]{2,1,0:T(8,128)S(1)} custom-call(f32[64,24,128]{2,1,0:T(8,128)S(1)} %copy-done.5, f32[64,24,128]{2,1,0:T(8,128)S(1)} %get-tuple-element.57.s_ref, bf16[1024,256]{1,0:T(8,128)(2,1)S(1)} %copy-done.21, bf16[1024,256]{1,0:T(8,128)(2,1)S(1)} %copy-done.23, f32[64,24,128]{2,1,0:T(8,128)S(1)} %get-tuple-element.59.x_ref.rest_0_, ...), custom_call_target="tpu_custom_call" | custom-call | flops 3000000000 | bytes 6291456 | tf_op jit(solution)/shard_map/wall/pallas_call | solution.py:248
  140.6 3.3 %wall.5.g_ref = f32[64,24,128]{2,1,0:T(8,128)S(1)} custom-call(f32[64,24,128]{2,1,0:T(8,128)S(1)} %copy-done.3, f32[64,24,128]{2,1,0:T(8,128)S(1)} %get-tuple-element.46.s_ref, bf16[1024,256]{1,0:T(8,128)(2,1)S(1)} %copy-done.21, bf16[1024,256]{1,0:T(8,128)(2,1)S(1)} %copy-done.23, f32[64,24,128]{2,1,0:T(8,128)S(1)} %get-tuple-element.48.x_ref.rest_0_, ...), custom_call_target="tpu_custom_call" | custom-call | flops 3000000000 | bytes 6291456 | tf_op jit(solution)/shard_map/wall/pallas_call | solution.py:248
  143.9 2.5 %collective-permute-done.25.far_ref = f32[64,24,128]{2,1,0:T(8,128)S(1)} collective-permute-done((f32[64,24,128]{2,1,0:T(8,128)S(1)}, f32[64,24,128]{2,1,0:T(8,128)S(1)}, u32[]{:S(2)}, u32[]{:S(2)}) %collective-permute-start.25) | collective-permute-done | bytes 786464 | tf_op jit(solution)/shard_map/ppermute | solution.py:34
  146.5 2.5 %collective-permute-done.24.t_ref = f32[64,24,128]{2,1,0:T(8,128)S(1)} collective-permute-done((f32[64,24,128]{2,1,0:T(8,128)S(1)}, f32[64,24,128]{2,1,0:T(8,128)S(1)}, u32[]{:S(2)}, u32[]{:S(2)}) %collective-permute-start.24) | collective-permute-done | bytes 786464 | tf_op jit(solution)/shard_map/ppermute | solution.py:25
  148.9 1.2 last.5
  150.1 0.8 collective-permute-done.12.rest_0_
  150.9 6.5 %collective-permute-done.11.t_ref = f32[64,24,128]{2,1,0:T(8,128)S(1)} collective-permute-done((f32[64,24,128]{2,1,0:T(8,128)S(1)}, f32[64,24,128]{2,1,0:T(8,128)S(1)}, u32[]{:S(2)}, u32[]{:S(2)}) %collective-permute-start.11) | collective-permute-done | bytes 786464 | tf_op jit(solution)/shard_map/ppermute | solution.py:25
  157.4 2.2 %finish.3 = (f32[192,2048]{1,0:T(8,128)}, f32[192,2048]{1,0:T(8,128)}) custom-call(s32[8,128]{1,0:T(8,128)S(1)} %broadcast_in_dim.6.off_ref, f32[64,24,128]{2,1,0:T(8,128)S(1)} %wall.5.g_ref, f32[64,24,128]{2,1,0:T(8,128)S(1)} %collective-permute-done.11.t_ref, f32[64,24,128]{2,1,0:T(8,128)S(1)} %get-tuple-element.48.x_ref.rest_0_, ...), custom_call_target="tpu_custom_call" | custom-call | flops 1000000000 | bytes 6291456 | tf_op jit(solution)/shard_map/finish/pallas_call | solution.py:399
  159.5 2.2 %finish.4 = (f32[192,2048]{1,0:T(8,128)}, f32[192,2048]{1,0:T(8,128)}) custom-call(s32[8,128]{1,0:T(8,128)S(1)} %broadcast_in_dim.6.off_ref, f32[64,24,128]{2,1,0:T(8,128)S(1)} %wall.5.g_ref, f32[64,24,128]{2,1,0:T(8,128)S(1)} %collective-permute-done.11.t_ref, ...), custom_call_target="tpu_custom_call", output_to_operand_aliasing={{0}: (11, {}), {1}: (12, {})} | custom-call | flops 1000000000 | bytes 6291456 | tf_op jit(solution)/shard_map/finish/pallas_call | solution.py:399
  161.8 2.0 %finish.5 = (f32[192,2048]{1,0:T(8,128)}, f32[192,2048]{1,0:T(8,128)}) custom-call(s32[8,128]{1,0:T(8,128)S(1)} %broadcast_in_dim.6.off_ref, f32[64,24,128]{2,1,0:T(8,128)S(1)} %wall.5.g_ref, f32[64,24,128]{2,1,0:T(8,128)S(1)} %collective-permute-done.11.t_ref, ...), custom_call_target="tpu_custom_call", output_to_operand_aliasing={{0}: (12, {}), {1}: (13, {})} | custom-call | flops 1000000000 | bytes 6291456 | tf_op jit(solution)/shard_map/finish/pallas_call | solution.py:399
  (88 shorter events, 2.3 us)
Async XLA Ops:
  0.6 39.1 %collective-permute-start = (f32[192,2048]{1,0:T(8,128)}, f32[192,2048]{1,0:T(8,128)S(1)}, u32[]{:S(2)}, u32[]{:S(2)}) collective-permute-start(f32[192,2048]{1,0:T(8,128)} %x_ref.3), channel_id=1, source_target_pairs={{0,24},{4,12},{8,0},{12,20},{16,8},{20,28},{24,16},{28,4},{1,25},{... | collective-permute-start | bytes 4718600 | tf_op jit(solution)/shard_map/ppermute | solution.py:34
  5.8 1.4 copy-start
  7.2 3.4 %copy-start.26 = (s32[8,64]{1,0:T(8,128)S(1)}, s32[8,64]{1,0:T(8,128)}, u32[]{:S(2)}) copy-start(s32[8,64]{1,0:T(8,128)} %param.16) | copy-start | bytes 6148
  7.2 3.4 %copy-start.24 = (f32[8,192,64]{1,2,0:T(8,128)S(1)}, f32[8,192,64]{1,2,0:T(8,128)}, u32[]{:S(2)}) copy-start(f32[8,192,64]{1,2,0:T(8,128)} %param.14) | copy-start | bytes 1179652
  7.2 3.5 %copy-start.25 = (f32[192,64]{0,1:T(8,128)S(1)}, f32[192,64]{0,1:T(8,128)}, u32[]{:S(2)}) copy-start(f32[192,64]{0,1:T(8,128)} %param.13) | copy-start | bytes 147460
  9.0 20.7 %collective-permute-start.16 = (f32[64,24,128]{2,1,0:T(8,128)}, f32[64,24,128]{2,1,0:T(8,128)}, u32[]{:S(2)}, u32[]{:S(2)}) collective-permute-start(f32[64,24,128]{2,1,0:T(8,128)} %get-tuple-element.54.x_ref.rest_0_), channel_id=1, source_target_pairs={{0,2},{1,3},{2,0},{3,1},{4,6},{5,7},{6,4},{7,5},{8,10},{9,11},{10,... | collective-permute-start | bytes 2359304 | tf_op jit(solution)/shard_map/ppermute | solution.py:20
  11.0 30.6 %copy-start.27 = (s32[8]{0:T(128)S(1)}, s32[8]{0:T(128)}, u32[]{:S(2)}) copy-start(s32[8]{0:T(128)} %param.15) | copy-start | bytes 100
  11.0 30.6 %collective-permute-start.1 = (f32[2,512,128]{2,1,0:T(8,128)S(1)}, f32[2,512,128]{2,1,0:T(8,128)S(1)}, u32[]{:S(2)}, u32[]{:S(2)}) collective-permute-start(f32[2,512,128]{2,1,0:T(8,128)S(1)} %fusion), channel_id=1, source_target_pairs={{0,4},{4,0},{8,12},{12,8},{16,20},{20,16},{24,28},{28,24},{1,5},{5... | collective-permute-start | bytes 1572872 | tf_op jit(solution)/shard_map/ppermute | solution.py:25
  11.1 38.0 %collective-permute-start.15 = (f32[64,24,128]{2,1,0:T(8,128)}, f32[64,24,128]{2,1,0:T(8,128)S(1)}, u32[]{:S(2)}, u32[]{:S(2)}) collective-permute-start(f32[64,24,128]{2,1,0:T(8,128)} %get-tuple-element.54.x_ref.rest_0_), channel_id=1, source_target_pairs={{0,1},{1,0},{2,3},{3,2},{4,5},{5,4},{6,7},{7,6},{8,9},{9,8},{10,11... | collective-permute-start | bytes 2359304 | tf_op jit(solution)/shard_map/ppermute | solution.py:20
  11.2 38.8 %collective-permute-start.3 = (f32[64,24,128]{2,1,0:T(8,128)S(1)}, f32[64,24,128]{2,1,0:T(8,128)}, u32[]{:S(2)}, u32[]{:S(2)}) collective-permute-start(f32[64,24,128]{2,1,0:T(8,128)S(1)} %get-tuple-element.43.x_ref.rest_0_), channel_id=1, source_target_pairs={{0,2},{1,3},{2,0},{3,1},{4,6},{5,7},{6,4},{7,5},{8,10},{9,11},{10,... | collective-permute-start | bytes 2359304 | tf_op jit(solution)/shard_map/ppermute | solution.py:20
  29.8 27.4 %collective-permute-start.17 = (f32[64,24,128]{2,1,0:T(8,128)}, f32[64,24,128]{2,1,0:T(8,128)}, u32[]{:S(2)}, u32[]{:S(2)}) collective-permute-start(f32[64,24,128]{2,1,0:T(8,128)} %collective-permute-done.16.rest_2_), channel_id=1, source_target_pairs={{0,1},{1,0},{2,3},{3,2},{4,5},{5,4},{6,7},{7,6},{8,9},{9,8},{10,11... | collective-permute-start | bytes 2359304 | tf_op jit(solution)/shard_map/ppermute | solution.py:20
  41.6 4.4 %copy-start.14 = (f32[2,512,128]{2,1,0:T(8,128)}, f32[2,512,128]{2,1,0:T(8,128)S(1)}, u32[]{:S(2)}) copy-start(f32[2,512,128]{2,1,0:T(8,128)S(1)} %collective-permute-done.1.theirs_ref) | copy-start | bytes 1572868
  41.7 8.8 %copy-start.1 = (f32[192,2048]{1,0:T(8,128)S(1)}, f32[192,2048]{1,0:T(8,128)}, u32[]{:S(2)}) copy-start(f32[192,2048]{1,0:T(8,128)} %x_ref.2) | copy-start | bytes 4718596
  46.9 4.5 %copy-start.17 = (f32[192,192]{1,0:T(8,128)S(1)}, f32[192,192]{1,0:T(8,128)}, u32[]{:S(2)}) copy-start(f32[192,192]{1,0:T(8,128)} %inv_ref.1) | copy-start | bytes 442372
  46.9 20.8 %collective-permute-start.18 = (f32[64,24,128]{2,1,0:T(8,128)}, f32[64,24,128]{2,1,0:T(8,128)}, u32[]{:S(2)}, u32[]{:S(2)}) collective-permute-start(f32[64,24,128]{2,1,0:T(8,128)} %get-tuple-element.53), channel_id=1, source_target_pairs={{0,4},{4,0},{8,12},{12,8},{16,20},{20,16},{24,28},{28,24},{1,5},{5... | collective-permute-start | bytes 2359304 | tf_op jit(solution)/shard_map/ppermute | solution.py:25
  49.1 22.5 %collective-permute-start.19 = (f32[64,24,128]{2,1,0:T(8,128)}, f32[64,24,128]{2,1,0:T(8,128)}, u32[]{:S(2)}, u32[]{:S(2)}) collective-permute-start(f32[64,24,128]{2,1,0:T(8,128)} %get-tuple-element.54.x_ref.rest_0_), channel_id=1, source_target_pairs={{0,8},{4,28},{8,16},{12,4},{16,24},{20,12},{24,0},{28,20},{1,9},{5... | collective-permute-start | bytes 2359304 | tf_op jit(solution)/shard_map/ppermute | solution.py:34
  50.0 26.1 %collective-permute-start.2 = (f32[64,24,128]{2,1,0:T(8,128)S(1)}, f32[64,24,128]{2,1,0:T(8,128)}, u32[]{:S(2)}, u32[]{:S(2)}) collective-permute-start(f32[64,24,128]{2,1,0:T(8,128)S(1)} %get-tuple-element.43.x_ref.rest_0_), channel_id=1, source_target_pairs={{0,1},{1,0},{2,3},{3,2},{4,5},{5,4},{6,7},{7,6},{8,9},{9,8},{10,11... | collective-permute-start | bytes 2359304 | tf_op jit(solution)/shard_map/ppermute | solution.py:20
  50.0 26.1 %collective-permute-start.4 = (f32[64,24,128]{2,1,0:T(8,128)}, f32[64,24,128]{2,1,0:T(8,128)}, u32[]{:S(2)}, u32[]{:S(2)}) collective-permute-start(f32[64,24,128]{2,1,0:T(8,128)} %collective-permute-done.3.rest_2_), channel_id=1, source_target_pairs={{0,1},{1,0},{2,3},{3,2},{4,5},{5,4},{6,7},{7,6},{8,9},{9,8},{10,11... | collective-permute-start | bytes 2359304 | tf_op jit(solution)/shard_map/ppermute | solution.py:20
  50.5 4.6 %copy-start.11 = (f32[64,24,128]{2,1,0:T(8,128)S(1)}, f32[64,24,128]{2,1,0:T(8,128)}, u32[]{:S(2)}) copy-start(f32[64,24,128]{2,1,0:T(8,128)} %copy-done.10) | copy-start | bytes 2359300
  50.5 4.6 %copy-start.15 = (f32[2,512,128]{2,1,0:T(8,128)S(1)}, f32[2,512,128]{2,1,0:T(8,128)}, u32[]{:S(2)}) copy-start(f32[2,512,128]{2,1,0:T(8,128)} %copy-done.14) | copy-start | bytes 1572868
  51.4 16.6 %copy-start.4 = (f32[64,24,128]{2,1,0:T(8,128)}, f32[64,24,128]{2,1,0:T(8,128)S(1)}, u32[]{:S(2)}) copy-start(f32[64,24,128]{2,1,0:T(8,128)S(1)} %get-tuple-element.49.f_ref) | copy-start | bytes 2359300
  51.4 24.7 %copy-start.2 = (f32[64,24,128]{2,1,0:T(8,128)}, f32[64,24,128]{2,1,0:T(8,128)S(1)}, u32[]{:S(2)}) copy-start(f32[64,24,128]{2,1,0:T(8,128)S(1)} %get-tuple-element.34.f_ref) | copy-start | bytes 2359300
  51.5 1.5 copy-start.12
  55.0 21.1 %copy-start.20 = (bf16[1024,256]{1,0:T(8,128)(2,1)}, bf16[1024,256]{1,0:T(8,128)(2,1)S(1)}, u32[]{:S(2)}) copy-start(bf16[1024,256]{1,0:T(8,128)(2,1)S(1)} %get-tuple-element.38.mh_ref) | copy-start | bytes 1572868
  55.0 21.1 %copy-start.22 = (bf16[1024,256]{1,0:T(8,128)(2,1)}, bf16[1024,256]{1,0:T(8,128)(2,1)S(1)}, u32[]{:S(2)}) copy-start(bf16[1024,256]{1,0:T(8,128)(2,1)S(1)} %get-tuple-element.39.ml_ref) | copy-start | bytes 1572868
  55.1 13.0 %copy-start.7 = (f32[64,24,128]{2,1,0:T(8,128)S(1)}, f32[64,24,128]{2,1,0:T(8,128)}, u32[]{:S(2)}) copy-start(f32[64,24,128]{2,1,0:T(8,128)} %copy-done.6) | copy-start | bytes 2359300
  55.1 13.0 %copy-start.19 = (f32[64,24,128]{2,1,0:T(8,128)S(1)}, f32[64,24,128]{2,1,0:T(8,128)}, u32[]{:S(2)}) copy-start(f32[64,24,128]{2,1,0:T(8,128)} %copy-done.18) | copy-start | bytes 2359300
  57.2 25.7 %collective-permute-start.5 = (f32[64,24,128]{2,1,0:T(8,128)S(1)}, f32[64,24,128]{2,1,0:T(8,128)S(1)}, u32[]{:S(2)}, u32[]{:S(2)}) collective-permute-start(f32[64,24,128]{2,1,0:T(8,128)S(1)} %get-tuple-element.40), channel_id=1, source_target_pairs={{0,4},{4,0},{8,12},{12,8},{16,20},{20,16},{24,28},{28,24},{1,5},{5... | collective-permute-start | bytes 2359304 | tf_op jit(solution)/shard_map/ppermute | solution.py:25
  67.8 18.5 %collective-permute-start.6 = (f32[64,24,128]{2,1,0:T(8,128)S(1)}, f32[64,24,128]{2,1,0:T(8,128)S(1)}, u32[]{:S(2)}, u32[]{:S(2)}) collective-permute-start(f32[64,24,128]{2,1,0:T(8,128)S(1)} %get-tuple-element.43.x_ref.rest_0_), channel_id=1, source_target_pairs={{0,8},{4,28},{8,16},{12,4},{16,24},{20,12},{24,0},{28,20},{1,9},{5... | collective-permute-start | bytes 2359304 | tf_op jit(solution)/shard_map/ppermute | solution.py:34
  74.6 17.6 %collective-permute-start.22 = (f32[64,24,128]{2,1,0:T(8,128)S(1)}, f32[64,24,128]{2,1,0:T(8,128)}, u32[]{:S(2)}, u32[]{:S(2)}) collective-permute-start(f32[64,24,128]{2,1,0:T(8,128)S(1)} %get-tuple-element.59.x_ref.rest_0_), channel_id=1, source_target_pairs={{0,2},{1,3},{2,0},{3,1},{4,6},{5,7},{6,4},{7,5},{8,10},{9,11},{10,... | collective-permute-start | bytes 2359304 | tf_op jit(solution)/shard_map/ppermute | solution.py:20
  88.2 20.4 %collective-permute-start.7 = (f32[64,24,128]{2,1,0:T(8,128)S(1)}, f32[64,24,128]{2,1,0:T(8,128)S(1)}, u32[]{:S(2)}, u32[]{:S(2)}) collective-permute-start(f32[64,24,128]{2,1,0:T(8,128)S(1)} %get-tuple-element.48.x_ref.rest_0_), channel_id=1, source_target_pairs={{0,24},{4,12},{8,0},{12,20},{16,8},{20,28},{24,16},{28,4},{1,25},{... | collective-permute-start | bytes 2359304 | tf_op jit(solution)/shard_map/ppermute | solution.py:34
  89.4 20.1 %collective-permute-start.9 = (f32[64,24,128]{2,1,0:T(8,128)S(1)}, f32[64,24,128]{2,1,0:T(8,128)S(1)}, u32[]{:S(2)}, u32[]{:S(2)}) collective-permute-start(f32[64,24,128]{2,1,0:T(8,128)S(1)} %get-tuple-element.48.x_ref.rest_0_), channel_id=1, source_target_pairs={{0,2},{1,3},{2,0},{3,1},{4,6},{5,7},{6,4},{7,5},{8,10},{9,11},{10,... | collective-permute-start | bytes 2359304 | tf_op jit(solution)/shard_map/ppermute | solution.py:20
  90.9 32.8 %collective-permute-start.20 = (f32[64,24,128]{2,1,0:T(8,128)S(1)}, f32[64,24,128]{2,1,0:T(8,128)}, u32[]{:S(2)}, u32[]{:S(2)}) collective-permute-start(f32[64,24,128]{2,1,0:T(8,128)S(1)} %get-tuple-element.59.x_ref.rest_0_), channel_id=1, source_target_pairs={{0,24},{4,12},{8,0},{12,20},{16,8},{20,28},{24,16},{28,4},{1,25},{... | collective-permute-start | bytes 2359304 | tf_op jit(solution)/shard_map/ppermute | solution.py:34
  90.9 36.1 %collective-permute-start.21 = (f32[64,24,128]{2,1,0:T(8,128)S(1)}, f32[64,24,128]{2,1,0:T(8,128)}, u32[]{:S(2)}, u32[]{:S(2)}) collective-permute-start(f32[64,24,128]{2,1,0:T(8,128)S(1)} %get-tuple-element.59.x_ref.rest_0_), channel_id=1, source_target_pairs={{0,1},{1,0},{2,3},{3,2},{4,5},{5,4},{6,7},{7,6},{8,9},{9,8},{10,11... | collective-permute-start | bytes 2359304 | tf_op jit(solution)/shard_map/ppermute | solution.py:20
  92.2 44.5 %collective-permute-start.23 = (f32[64,24,128]{2,1,0:T(8,128)}, f32[64,24,128]{2,1,0:T(8,128)}, u32[]{:S(2)}, u32[]{:S(2)}) collective-permute-start(f32[64,24,128]{2,1,0:T(8,128)} %collective-permute-done.22.rest_2_), channel_id=1, source_target_pairs={{0,1},{1,0},{2,3},{3,2},{4,5},{5,4},{6,7},{7,6},{8,9},{9,8},{10,11... | collective-permute-start | bytes 2359304 | tf_op jit(solution)/shard_map/ppermute | solution.py:20
  109.5 31.0 %collective-permute-start.8 = (f32[64,24,128]{2,1,0:T(8,128)S(1)}, f32[64,24,128]{2,1,0:T(8,128)}, u32[]{:S(2)}, u32[]{:S(2)}) collective-permute-start(f32[64,24,128]{2,1,0:T(8,128)S(1)} %get-tuple-element.48.x_ref.rest_0_), channel_id=1, source_target_pairs={{0,1},{1,0},{2,3},{3,2},{4,5},{5,4},{6,7},{7,6},{8,9},{9,8},{10,11... | collective-permute-start | bytes 2359304 | tf_op jit(solution)/shard_map/ppermute | solution.py:20
  109.5 31.0 %collective-permute-start.10 = (f32[64,24,128]{2,1,0:T(8,128)S(1)}, f32[64,24,128]{2,1,0:T(8,128)}, u32[]{:S(2)}, u32[]{:S(2)}) collective-permute-start(f32[64,24,128]{2,1,0:T(8,128)S(1)} %collective-permute-done.9.rest_2_), channel_id=1, source_target_pairs={{0,1},{1,0},{2,3},{3,2},{4,5},{5,4},{6,7},{7,6},{8,9},{9,8},{10,11... | collective-permute-start | bytes 2359304 | tf_op jit(solution)/shard_map/ppermute | solution.py:20
  110.0 1.1 copy-start.9
  123.7 22.8 %collective-permute-start.25 = (f32[64,24,128]{2,1,0:T(8,128)S(1)}, f32[64,24,128]{2,1,0:T(8,128)S(1)}, u32[]{:S(2)}, u32[]{:S(2)}) collective-permute-start(f32[64,24,128]{2,1,0:T(8,128)S(1)} %get-tuple-element.59.x_ref.rest_0_), channel_id=1, source_target_pairs={{0,8},{4,28},{8,16},{12,4},{16,24},{20,12},{24,0},{28,20},{1,9},{5... | collective-permute-start | bytes 2359304 | tf_op jit(solution)/shard_map/ppermute | solution.py:34
  123.7 13.1 %copy-start.23 = (bf16[1024,256]{1,0:T(8,128)(2,1)S(1)}, bf16[1024,256]{1,0:T(8,128)(2,1)}, u32[]{:S(2)}) copy-start(bf16[1024,256]{1,0:T(8,128)(2,1)} %copy-done.22) | copy-start | bytes 1572868
  127.0 9.8 %copy-start.5 = (f32[64,24,128]{2,1,0:T(8,128)S(1)}, f32[64,24,128]{2,1,0:T(8,128)}, u32[]{:S(2)}) copy-start(f32[64,24,128]{2,1,0:T(8,128)} %copy-done.4) | copy-start | bytes 2359300
  127.0 9.8 %copy-start.21 = (bf16[1024,256]{1,0:T(8,128)(2,1)S(1)}, bf16[1024,256]{1,0:T(8,128)(2,1)}, u32[]{:S(2)}) copy-start(bf16[1024,256]{1,0:T(8,128)(2,1)} %copy-done.20) | copy-start | bytes 1572868
  127.0 21.9 %collective-permute-start.24 = (f32[64,24,128]{2,1,0:T(8,128)S(1)}, f32[64,24,128]{2,1,0:T(8,128)S(1)}, u32[]{:S(2)}, u32[]{:S(2)}) collective-permute-start(f32[64,24,128]{2,1,0:T(8,128)S(1)} %get-tuple-element.58), channel_id=1, source_target_pairs={{0,4},{4,0},{8,12},{12,8},{16,20},{20,16},{24,28},{28,24},{1,5},{5... | collective-permute-start | bytes 2359304 | tf_op jit(solution)/shard_map/ppermute | solution.py:25
  136.7 20.7 %collective-permute-start.11 = (f32[64,24,128]{2,1,0:T(8,128)S(1)}, f32[64,24,128]{2,1,0:T(8,128)S(1)}, u32[]{:S(2)}, u32[]{:S(2)}) collective-permute-start(f32[64,24,128]{2,1,0:T(8,128)S(1)} %get-tuple-element.47), channel_id=1, source_target_pairs={{0,4},{4,0},{8,12},{12,8},{16,20},{20,16},{24,28},{28,24},{1,5},{5... | collective-permute-start | bytes 2359304 | tf_op jit(solution)/shard_map/ppermute | solution.py:25
  136.9 3.8 %copy-start.3 = (f32[64,24,128]{2,1,0:T(8,128)S(1)}, f32[64,24,128]{2,1,0:T(8,128)}, u32[]{:S(2)}) copy-start(f32[64,24,128]{2,1,0:T(8,128)} %copy-done.2) | copy-start | bytes 2359300
  140.5 10.4 %collective-permute-start.12 = (f32[24,24,128]{2,1,0:T(8,128)S(1)}, f32[24,24,128]{2,1,0:T(8,128)S(1)}, u32[]{:S(2)}, u32[]{:S(2)}) collective-permute-start(f32[24,24,128]{2,1,0:T(8,128)S(1)} %get-tuple-element.67), channel_id=1, source_target_pairs={{0,8},{4,28},{8,16},{12,4},{16,24},{20,12},{24,0},{28,20},{1,9},{5... | collective-permute-start | bytes 884744 | tf_op jit(solution)/shard_map/ppermute | solution.py:34
  140.6 19.0 %collective-permute-start.13 = (f32[24,24,128]{2,1,0:T(8,128)S(1)}, f32[24,24,128]{2,1,0:T(8,128)S(1)}, u32[]{:S(2)}, u32[]{:S(2)}) collective-permute-start(f32[24,24,128]{2,1,0:T(8,128)S(1)} %get-tuple-element.66), channel_id=1, source_target_pairs={{0,8},{4,28},{8,16},{12,4},{16,24},{20,12},{24,0},{28,20},{1,9},{5... | collective-permute-start | bytes 884744 | tf_op jit(solution)/shard_map/ppermute | solution.py:34
  146.5 15.3 %collective-permute-start.14 = (f32[16,24,128]{2,1,0:T(8,128)S(1)}, f32[16,24,128]{2,1,0:T(8,128)S(1)}, u32[]{:S(2)}, u32[]{:S(2)}) collective-permute-start(f32[16,24,128]{2,1,0:T(8,128)S(1)} %constant_dynamic-slice_fusion), channel_id=1, source_target_pairs={{0,8},{4,28},{8,16},{12,4},{16,24},{20,12},{24,0},{28,20},{1,9},{5... | collective-permute-start | bytes 589832 | tf_op jit(solution)/shard_map/ppermute | solution.py:34
  (6 other events, 5.7 us)
